TPU v7x, 32 devices: a whole 2x2x4 slice. The times are simulated.
32 devices in a mesh: strip: 8 (over y, x, core), frame: 4 (over z).
Axes of the slice: x: 2, y: 2, z: 4, core: 2. Of those that a mesh axis runs over, the one named last changes fastest.
Arguments:
- estimate: float32 [1024, 2048], P('strip'), may hold values from -6 to 6
- observed: float32 [8, 1024, 2048], P('frame', 'strip'), may hold values from -6 to 6
- weights: float32 [8, 1024, 2048], P('frame', 'strip'), may hold values from 0.3 to 9, as said below
- column_kernels: float32 [8, 65], P('frame'), may hold values from 0.05 to 1
- row_kernels: float32 [8, 65], P('frame'), may hold values from 0.05 to 1
Outputs:
- solution: float32 [1024, 2048], P('strip')
- residual: float32 [1024, 2048], P('strip')
Inputs may be any that keep to these rules, and one draw needn't show every extreme that they name: Positive weights of each pixel.
All inputs are finite; a program needn't handle non-finite values.
Results may differ from a plain program's by a relative error of at most 0.00013.
Values sent between devices are 32-bit elements; how exact they have to be, the bound alone decides.
No kernel may reach another device: no remote copies, remote signals or barrier semaphores. Data moves between devices by JAX's collectives and lax.ppermute only.
A program may use at most 128 MiB of HBM per device.

v0:
```python
import functools

import jax
import jax.numpy as jnp
from jax import lax
from jax.experimental import pallas as pl
from jax.experimental.pallas import tpu as pltpu
from jax.sharding import PartitionSpec as P


damping = 0.05
f32 = jnp.float32
bf16 = jnp.bfloat16
LANE = 128
VMEM = pl.BlockSpec(memory_space=pltpu.VMEM)
ANY = pl.BlockSpec(memory_space=pl.ANY)
SMEM = pl.BlockSpec(memory_space=pltpu.SMEM)


def split(x):
    hi = x.astype(bf16)
    lo = (x - hi.astype(f32)).astype(bf16)
    return hi, lo


def dot(a, b):
    return jnp.dot(a, b, preferred_element_type=f32)


def choose(flag, a, b):
    return jnp.where(jnp.full(a.shape, flag, jnp.int32) == 1, a, b)


def pack_edge(edge, halo, w):
    rows = edge.shape[0]
    per = LANE // (2 * halo)
    short = rows * 2 * halo // w
    edge = pltpu.roll(edge, halo, 1)
    lane = lax.broadcasted_iota(jnp.int32, (short, LANE), 1)
    out = []
    for t in range(w // LANE):
        tile = None
        for p in range(per):
            k = t * per + p
            part = edge[k * short : (k + 1) * short]
            part = pltpu.roll(part, p * 2 * halo, 1) if p else part
            tile = part if tile is None else jnp.where(lane >= p * 2 * halo, part, tile)
        out.append(tile)
    return jnp.concatenate(out, axis=1)


def unpack_edge(packed, halo):
    _, w = packed.shape
    per = LANE // (2 * halo)
    parts = []
    for k in range(w // (2 * halo)):
        t, p = divmod(k, per)
        part = packed[:, t * LANE : (t + 1) * LANE]
        back = (LANE - halo - p * 2 * halo) % LANE
        parts.append(pltpu.roll(part, back, 1) if back else part)
    return jnp.concatenate(parts, axis=0)


def tiles(width, step=256):
    return [(s, min(step, width - s)) for s in range(0, width, step)]


def toeplitz(base, count):
    wide = base.shape[1]
    return pltpu.roll(jnp.broadcast_to(base, (count, wide)), 0, 1, stride=1, stride_axis=0)


def build_group(taps, g, frames, rows, halo, t_ref, b_ref, bp_ref, ta_ref):
    ext = rows + 2 * halo
    unit = taps / jnp.sum(taps, axis=1, keepdims=True)
    for s in range(frames):
        f = g * frames + s
        col = unit[s : s + 1]
        row = unit[frames + s : frames + s + 1]
        by_rows = toeplitz(row, rows)
        hi, lo = split(by_rows)
        t_ref[f, :rows, :] = hi
        t_ref[f, rows:, :] = lo
        hi, lo = split(by_rows.T[:ext])
        ta_ref[g, :ext, s * rows : (s + 1) * rows] = hi
        ta_ref[g, ext:, s * rows : (s + 1) * rows] = lo
        hi, lo = split(toeplitz(col, LANE).T)
        b_ref[f, :, :LANE] = hi
        b_ref[f, :, LANE:] = lo
        hi, lo = split(toeplitz(pltpu.roll(col, LANE, 1), 2 * LANE)[:, :LANE])
        bp_ref[f, :, :LANE] = hi
        bp_ref[f, :, LANE:] = lo


def matrix_shapes(groups, frames, rows, halo):
    ext = rows + 2 * halo
    return [
        jax.ShapeDtypeStruct(s, bf16)
        for s in (
            (groups * frames, 2 * rows, 2 * LANE),
            (groups * frames, 2 * LANE, 2 * LANE),
            (groups * frames, 2 * LANE, 2 * LANE),
            (groups, 2 * ext, frames * rows),
        )
    ]


def tile_height(frames):
    return -(-2 * frames // 8) * 8


def setup_kernel(frames, rows, halo, starts, *refs):
    tiles_in = refs[: len(starts)]
    mats, taps, sem = refs[len(starts) : -2], refs[-2], refs[-1]
    height = tile_height(frames)

    def copy(g):
        source = tiles_in[g].at[pl.ds(starts[g], height), pl.ds(0, 2 * LANE)]
        return pltpu.make_async_copy(source, taps.at[g], sem.at[g])

    for g in range(len(starts)):
        copy(g).start()
    for g in range(len(starts)):
        copy(g).wait()
        build_group(taps[g], g, frames, rows, halo, *mats)


def setup_matrices(tiles_in, starts, frames, rows, halo):
    groups = len(tiles_in)
    return pl.pallas_call(
        functools.partial(setup_kernel, frames, rows, halo, starts),
        out_shape=matrix_shapes(groups, frames, rows, halo),
        in_specs=[ANY] * groups,
        out_specs=[VMEM] * 4,
        scratch_shapes=[
            pltpu.VMEM((groups, tile_height(frames), 2 * LANE), f32),
            pltpu.SemaphoreType.DMA((groups,)),
        ],
        name="setup_all",
    )(*tiles_in)


def load_image(y_hi, y_lo, image, halo):
    ext, full = image.shape
    shift = LANE - halo
    y = pltpu.roll(image, full - shift, 1)[:, : full - LANE]
    hi, lo = split(y)
    y_hi[:ext, :] = hi
    y_lo[:ext, :] = lo


def group_terms(frames, rows, w, y_hi, y_lo, t, b, bp, ta, weight, data, us, qs, vs_hi, vs_lo, acc, stat, ready=None):
    total = None
    for f in range(frames):
        for c, size in tiles(w + LANE):
            r1 = dot(t(f)[...], y_hi[:, c : c + size])
            r2 = dot(t(f)[:rows, :], y_lo[:, c : c + size])
            hi, lo = split(r1[:rows] + r1[rows:] + r2)
            us[:rows, c : c + size] = hi
            us[rows:, c : c + size] = lo
        if ready is not None:
            ready(f)
        for k in range(w // LANE):
            c = k * LANE
            r = dot(us[:, c : c + 2 * LANE], b(f)[...])
            a = r[:rows, :LANE] + r[:rows, LANE:] + r[rows:, :LANE]
            if data is not None:
                a = a - data(f)[:, c : c + LANE]
            q = weight(f)[:, c : c + LANE] * a
            if stat is not None:
                part = jnp.sum((a * q).reshape(rows // 8, 8, LANE), axis=0)
                total = part if total is None else total + part
            hi, lo = split(q)
            qs[:rows, c + LANE : c + 2 * LANE] = hi
            qs[rows:, c + LANE : c + 2 * LANE] = lo
        for k in range(w // LANE + 1):
            c = k * LANE
            r = dot(qs[:, c : c + 2 * LANE], bp(f)[...])
            hi, lo = split(r[:rows, :LANE] + r[:rows, LANE:] + r[rows:, :LANE])
            vs_hi[f * rows : (f + 1) * rows, c : c + LANE] = hi
            vs_lo[f * rows : (f + 1) * rows, c : c + LANE] = lo
    ext = acc.shape[0]
    for c, size in tiles(w + LANE):
        r1 = dot(ta[...], vs_hi[:, c : c + size])
        r2 = dot(ta[:ext, :], vs_lo[:, c : c + size])
        acc[:, c : c + size] += r1[:ext] + r1[ext:] + r2
    if stat is not None:
        stat[...] += total


def work_scratch(frames, rows, halo, w):
    ext = rows + 2 * halo
    return [
        pltpu.VMEM((2 * LANE, w + LANE), bf16),
        pltpu.VMEM((2 * LANE, w + LANE), bf16),
        pltpu.VMEM((2 * rows, w + LANE), bf16),
        pltpu.VMEM((2 * rows, w + 2 * LANE), bf16),
        pltpu.VMEM((frames * rows, w + LANE), bf16),
        pltpu.VMEM((frames * rows, w + LANE), bf16),
        pltpu.VMEM((ext, w + LANE), f32),
    ]


def clear_edges(y_hi, y_lo, qs, ext, rows, w):
    zero = jnp.zeros((y_hi.shape[0] - ext, y_hi.shape[1]), bf16)
    y_hi[ext:, :] = zero
    y_lo[ext:, :] = zero
    qs[:, :LANE] = jnp.zeros((2 * rows, LANE), bf16)
    qs[:, w + LANE :] = jnp.zeros((2 * rows, LANE), bf16)


def unshift(acc, halo):
    return pltpu.roll(acc, acc.shape[1] - halo, 1)


def first_kernel(
    frames, rows, halo,
    place, est, recv_a, recv_b, t_ref, b_ref, bp_ref, ta_ref, w_hbm, d_hbm,
    send_a, mid, send_b,
    y_hi, y_lo, us, qs, vs_hi, vs_lo, acc, wbuf, dbuf, sem,
):
    ext = rows + 2 * halo
    cols = est.shape[1]
    copies = [
        (
            pltpu.make_async_copy(w_hbm.at[f], wbuf.at[f], sem.at[0, f]),
            pltpu.make_async_copy(d_hbm.at[f], dbuf.at[f], sem.at[1, f]),
        )
        for f in range(frames)
    ]
    for pair in copies:
        for c in pair:
            c.start()
    clear_edges(y_hi, y_lo, qs, ext, rows, cols)
    odd = lax.rem(place[1], 2)
    none = jnp.zeros((ext, LANE), f32)
    for start in range(0, cols, 4 * LANE):
        size = 4 * LANE + LANE
        left = max(start - LANE, 0)
        span = slice(left, min(start + 4 * LANE, cols))
        x = jnp.concatenate(
            [
                choose(odd, recv_a[:, span], recv_b[:, span]),
                est[:, span],
                choose(odd, recv_b[:, span], recv_a[:, span]),
            ],
            axis=0,
        )
        if start == 0:
            x = jnp.concatenate([none, x], axis=1)
        if x.shape[1] < size:
            x = jnp.concatenate([x, jnp.zeros((ext, size - x.shape[1]), f32)], axis=1)
        hi, lo = split(pltpu.roll(x, halo, 1)[:, LANE:])
        y_hi[:ext, start : start + 4 * LANE] = hi
        y_lo[:ext, start : start + 4 * LANE] = lo
        if start + 4 * LANE >= cols:
            tail = jnp.concatenate([x[:, 4 * LANE :], none], axis=1)
            hi, lo = split(pltpu.roll(tail, halo, 1)[:, LANE:])
            y_hi[:ext, cols:] = hi
            y_lo[:ext, cols:] = lo
    acc[...] = jnp.zeros_like(acc)

    def ready(f):
        for c in copies[f]:
            c.wait()

    group_terms(
        frames, rows, cols, y_hi, y_lo,
        lambda f: t_ref.at[f], lambda f: b_ref.at[f], lambda f: bp_ref.at[f], ta_ref.at[0],
        lambda f: wbuf.at[f], lambda f: dbuf.at[f],
        us, qs, vs_hi, vs_lo, acc, None, ready,
    )
    for start in range(0, cols, 4 * LANE):
        size = min(4 * LANE, cols - start)
        z = pltpu.roll(acc[:, start : start + size + LANE], size + LANE - halo, 1)[:, :size]
        span = slice(start, start + size)
        low, high = z[:halo], z[halo + rows :]
        send_a[:, span] = choose(odd, low, high)
        send_b[:, span] = choose(odd, high, low)
        mid[:, span] = z[halo : halo + rows]


def first_terms(place, est, recv_a, recv_b, mats, weights, observed):
    frames, rows, cols = weights.shape
    halo = recv_a.shape[0]
    return pl.pallas_call(
        functools.partial(first_kernel, frames, rows, halo),
        out_shape=[
            jax.ShapeDtypeStruct((halo, cols), f32),
            jax.ShapeDtypeStruct((rows, cols), f32),
            jax.ShapeDtypeStruct((halo, cols), f32),
        ],
        in_specs=[SMEM] + [VMEM] * 7 + [ANY, ANY],
        out_specs=[VMEM] * 3,
        scratch_shapes=work_scratch(frames, rows, halo, cols)
        + [
            pltpu.VMEM((frames, rows, cols), f32),
            pltpu.VMEM((frames, rows, cols), f32),
            pltpu.SemaphoreType.DMA((2, frames)),
        ],
        cost_estimate=pl.CostEstimate(flops=8 * 10**9, bytes_accessed=8 * 2**20, transcendentals=0),
        name="first_terms",
    )(place, est, recv_a, recv_b, *mats, weights, observed)


def prepare_kernel(plan, frames, rows, halo, w, place, cols_in, rows_in, weights, *refs):
    outs, tile, mats, sem = refs[: len(plan)], refs[len(plan)], refs[len(plan) + 1 : -1], refs[-1]
    taps = cols_in.shape[1]
    pending = []
    for i, (distance, lead, count, _) in enumerate(plan):
        start = pl.multiple_of(jnp.bitwise_xor(place[0], distance) * w, LANE)
        for k in range(count):
            copy = pltpu.make_async_copy(
                weights.at[lead + k, :, pl.ds(start, w)],
                outs[i].at[pl.ds(k * rows, rows), :],
                sem.at[i, k],
            )
            copy.start()
            pending.append(copy)
    tile[...] = jnp.zeros_like(tile)
    tile[:frames, :taps] = cols_in[...]
    tile[frames : 2 * frames, :taps] = rows_in[...]
    for i, (_, _, count, with_taps) in enumerate(plan):
        if with_taps:
            outs[i][count * rows :, :] = tile[...]
    build_group(tile[:, : 2 * LANE], 0, frames, rows, halo, *mats)
    for copy in pending:
        copy.wait()


def prepare(plan, place, column_kernels, row_kernels, weights, w, halo):
    frames, rows, _ = weights.shape
    height = tile_height(frames)
    out = pl.pallas_call(
        functools.partial(prepare_kernel, plan, frames, rows, halo, w),
        out_shape=[
            jax.ShapeDtypeStruct((count * rows + (height if taps else 0), w), f32)
            for _, _, count, taps in plan
        ]
        + [jax.ShapeDtypeStruct((height, w), f32)]
        + matrix_shapes(1, frames, rows, halo),
        in_specs=[SMEM, VMEM, VMEM, ANY],
        out_specs=[VMEM] * (len(plan) + 5),
        scratch_shapes=[pltpu.SemaphoreType.DMA((len(plan), frames))],
        name="prepare",
    )(place, column_kernels, row_kernels, weights)
    return out[: len(plan)], out[len(plan)], out[len(plan) + 1 :]


def blocks_kernel(n, halo, w, place, send_a, mid, send_b, recv_a, recv_b, *refs):
    outs, full = refs[:-1], refs[-1]
    rows, cols = mid.shape
    odd = lax.rem(place[1], 2)
    inner = slice(LANE, LANE + cols)
    for end in (0, LANE + cols):
        full[:, end : end + LANE] = jnp.zeros((rows, LANE), f32)
    full[:halo, inner] = mid[:halo, :] + choose(odd, recv_a[...], recv_b[...])
    full[halo : rows - halo, inner] = mid[halo : rows - halo, :]
    full[rows - halo :, inner] = mid[rows - halo :, :] + choose(odd, recv_b[...], recv_a[...])
    lane = lax.broadcasted_iota(jnp.int32, (rows, LANE), 1)
    for i in range(n):
        start = jnp.bitwise_xor(place[0], i) * w
        outs[i][:rows, :] = full[:, pl.ds(pl.multiple_of(start + LANE, LANE), w)]
        before = full[:, pl.ds(pl.multiple_of(start, LANE), LANE)]
        after = full[:, pl.ds(pl.multiple_of(start + LANE + w, LANE), LANE)]
        outs[i][rows:, :] = pack_edge(jnp.where(lane >= LANE - halo, before, after), halo, w)


def column_blocks(n, place, send_a, mid, send_b, recv_a, recv_b, w):
    rows, cols = mid.shape
    halo = send_a.shape[0]
    height = rows + rows * 2 * halo // w
    return pl.pallas_call(
        functools.partial(blocks_kernel, n, halo, w),
        out_shape=[jax.ShapeDtypeStruct((height, w), f32)] * n,
        in_specs=[SMEM] + [VMEM] * 5,
        out_specs=[VMEM] * n,
        scratch_shapes=[pltpu.VMEM((rows, cols + 2 * LANE), f32)],
        name="column_blocks",
    )(place, send_a, mid, send_b, recv_a, recv_b)


def start_kernel(n, rows, halo, w, place, est, *refs):
    parts = refs[:-5]
    k0, wide, send_a, send_b, stat = refs[-5:]
    total = parts[0][...]
    for p in parts[1:]:
        total = total + p[...]
    me = place[0]
    odd = lax.rem(place[1], 2)
    at = lambda start, size: est[:, pl.ds(pl.multiple_of(start, LANE), size)]
    own = -(total[:rows] + damping * at(me * w, w))
    edge = unpack_edge(total[rows:], halo)
    before = at(jnp.maximum(me * w - LANE, 0), LANE)
    after = at(jnp.minimum(me * w + w, (n * w) - LANE), LANE)
    none = jnp.zeros((rows, LANE), f32)
    left = choose((me > 0).astype(jnp.int32), -(edge + damping * before), none)
    right = choose((me < n - 1).astype(jnp.int32), -(edge + damping * after), none)
    k0[...] = own
    wide[:, :LANE] = left
    wide[:, LANE : LANE + w] = own
    wide[:, LANE + w :] = right
    low, high = wide[:halo, :], wide[rows - halo :, :]
    send_a[...] = choose(odd, low, high)
    send_b[...] = choose(odd, high, low)
    square = own * own
    acc = square[:, :LANE]
    for c in range(LANE, w, LANE):
        acc = acc + square[:, c : c + LANE]
    stat[...] = jnp.sum(acc.reshape(rows // 8, 8, LANE), axis=0)


def start_image(n, place, est, parts, halo):
    rows, cols = est.shape
    w = cols // n
    return pl.pallas_call(
        functools.partial(start_kernel, n, rows, halo, w),
        out_shape=[
            jax.ShapeDtypeStruct((rows, w), f32),
            jax.ShapeDtypeStruct((rows, w + 2 * LANE), f32),
            jax.ShapeDtypeStruct((halo, w + 2 * LANE), f32),
            jax.ShapeDtypeStruct((halo, w + 2 * LANE), f32),
            jax.ShapeDtypeStruct((8, LANE), f32),
        ],
        in_specs=[SMEM] + [VMEM] * (1 + len(parts)),
        out_specs=[VMEM] * 5,
        name="start_image",
    )(place, est, *parts)


def apply_kernel(frames, rows, halo, w, groups, origin, cut, count, pieces, place, *refs):
    image, refs = refs[:pieces], refs[pieces:]
    t_hbm, b_hbm, bp_hbm, ta_hbm, own = refs[:5]
    moved = refs[5 : 5 + count]
    send_a, mid, send_b, stat = refs[5 + count : 9 + count]
    refs = refs[9 + count :]
    if pieces > 1:
        whole, refs = refs[0], refs[1:]
    y_hi, y_lo, us, qs, vs_hi, vs_lo, acc, tb, bb, bpb, tab, wbuf, sem, wsem = refs
    odd = lax.rem(place[1], 2)
    ext = rows + 2 * halo

    def copies(g):
        span = pl.ds(g * frames, frames)
        return [
            pltpu.make_async_copy(t_hbm.at[span], tb.at[g], sem.at[0, g]),
            pltpu.make_async_copy(b_hbm.at[span], bb.at[g], sem.at[1, g]),
            pltpu.make_async_copy(bp_hbm.at[span], bpb.at[g], sem.at[2, g]),
            pltpu.make_async_copy(ta_hbm.at[g], tab.at[g], sem.at[3, g]),
        ]

    mine = pl.ds(pl.multiple_of(place[0] * w, LANE), w)
    for g in range(groups):
        for c in copies(g):
            c.start()
        for f in range(frames):
            if g == 0:
                source = own.at[f, :, mine]
            else:
                ref, start = origin[g, f]
                source = moved[ref].at[pl.ds(start, rows), :]
            pltpu.make_async_copy(source, wbuf.at[g, f], wsem.at[g, f]).start()
    clear_edges(y_hi, y_lo, qs, ext, rows, w)
    if pieces > 1:
        wide, recv_a, recv_b = image
        whole[:halo, :] = choose(odd, recv_a[...], recv_b[...])
        whole[halo : halo + rows, :] = wide[...]
        whole[halo + rows :, :] = choose(odd, recv_b[...], recv_a[...])
        load_image(y_hi, y_lo, whole[...], halo)
    else:
        load_image(y_hi, y_lo, image[0][...], halo)
    acc[...] = jnp.zeros_like(acc)
    stat[...] = jnp.zeros_like(stat)

    @pl.loop(0, groups)
    def _(g):
        for c in copies(g):
            c.wait()
        for f in range(frames):
            pltpu.make_async_copy(own.at[f, :, mine], wbuf.at[g, f], wsem.at[g, f]).wait()
        group_terms(
            frames, rows, w, y_hi, y_lo,
            lambda f: tb.at[g, f], lambda f: bb.at[g, f], lambda f: bpb.at[g, f], tab.at[g],
            lambda f: wbuf.at[g, f], None,
            us, qs, vs_hi, vs_lo, acc, stat,
        )

    z = unshift(acc[...], halo)
    send_a[...] = choose(odd, z[:cut], z[ext - cut :])
    send_b[...] = choose(odd, z[ext - cut :], z[:cut])
    mid[...] = z[cut : ext - cut]


def apply_terms(place, image, mats, weights, moved, origin, cut, halo):
    frames, rows, _ = weights.shape
    w = image[0].shape[1] - 2 * LANE
    ext = rows + 2 * halo
    t, b, bp, ta = mats
    groups = ta.shape[0]
    wide = w + LANE
    return pl.pallas_call(
        functools.partial(apply_kernel, frames, rows, halo, w, groups, origin, cut, len(moved), len(image)),
        out_shape=[
            jax.ShapeDtypeStruct((cut, wide), f32),
            jax.ShapeDtypeStruct((ext - 2 * cut, wide), f32),
            jax.ShapeDtypeStruct((cut, wide), f32),
            jax.ShapeDtypeStruct((8, LANE), f32),
        ]
        + [jax.ShapeDtypeStruct((ext, w + 2 * LANE), f32)] * (len(image) > 1),
        in_specs=[SMEM] + [VMEM] * len(image) + [ANY] * (5 + len(moved)),
        out_specs=[VMEM] * (4 + (len(image) > 1)),
        scratch_shapes=work_scratch(frames, rows, halo, w)
        + [
            pltpu.VMEM((groups, frames) + t.shape[1:], bf16),
            pltpu.VMEM((groups, frames) + b.shape[1:], bf16),
            pltpu.VMEM((groups, frames) + bp.shape[1:], bf16),
            pltpu.VMEM((groups,) + ta.shape[1:], bf16),
            pltpu.VMEM((groups, frames, rows, w), f32),
            pltpu.SemaphoreType.DMA((4, groups)),
            pltpu.SemaphoreType.DMA((groups, frames)),
        ],
        cost_estimate=pl.CostEstimate(
            flops=groups * 3 * 10**9, bytes_accessed=groups * 2**20, transcendentals=0
        ),
    )(place, *image, t, b, bp, ta, weights, *moved)


def rows_kernel(strips, halo, w, place, send_a, mid, send_b, recv_a, recv_b, q, col_a, col_b):
    odd = lax.rem(place[1], 2)
    odd_col = lax.rem(place[0], 2)
    edge_rows, wide = send_a.shape
    ext = q.shape[0]
    row = lax.broadcasted_iota(jnp.int32, (edge_rows, wide), 0)
    strip = jnp.full((edge_rows, wide), place[1], jnp.int32)
    low = choose(odd, send_a[...], send_b[...]) + choose(odd, recv_a[...], recv_b[...])
    high = choose(odd, send_b[...], send_a[...]) + choose(odd, recv_b[...], recv_a[...])
    q[:edge_rows, :] = jnp.where((row >= halo) | (strip > 0), low, 0.0)
    q[edge_rows : ext - edge_rows, :] = mid[...]
    q[ext - edge_rows :, :] = jnp.where((row < edge_rows - halo) | (strip < strips - 1), high, 0.0)
    lane = lax.broadcasted_iota(jnp.int32, (ext, LANE), 1)
    edge = q[:, w:]
    to_left = jnp.where(lane < halo, q[:, :LANE], edge)
    to_right = jnp.where(lane >= LANE - halo, q[:, w - LANE : w], edge)
    col_a[...] = choose(odd_col, to_left, to_right)
    col_b[...] = choose(odd_col, to_right, to_left)


def merge_rows(strips, place, send_a, mid, send_b, recv_a, recv_b, halo):
    ext = mid.shape[0] + 2 * send_a.shape[0]
    wide = mid.shape[1]
    return pl.pallas_call(
        functools.partial(rows_kernel, strips, halo, wide - LANE),
        out_shape=[
            jax.ShapeDtypeStruct((ext, wide), f32),
            jax.ShapeDtypeStruct((ext, LANE), f32),
            jax.ShapeDtypeStruct((ext, LANE), f32),
        ],
        in_specs=[SMEM] + [VMEM] * 5,
        out_specs=[VMEM] * 3,
        name="merge_rows",
    )(place, send_a, mid, send_b, recv_a, recv_b)


def cols_kernel(n, rows, halo, place, q, recv_a, recv_b, before, out, block, stat):
    odd = lax.rem(place[0], 2)
    ext, wide = q.shape
    w = wide - LANE
    lane = lax.broadcasted_iota(jnp.int32, (ext, LANE), 1)
    at = jnp.full((ext, LANE), place[0], jnp.int32)
    left = choose(odd, recv_a[...], recv_b[...])
    right = choose(odd, recv_b[...], recv_a[...])
    edge = q[:, w:]
    total = None
    out[:, :LANE] = jnp.where(at > 0, edge + left, 0.0) + damping * before[:, :LANE]
    out[:, LANE + w :] = jnp.where(at < n - 1, edge + right, 0.0) + damping * before[:, LANE + w :]
    for c in range(0, w, LANE):
        x = q[:, c : c + LANE] + damping * before[:, c + LANE : c + 2 * LANE]
        if c == 0:
            x = x + jnp.where(lane < halo, left, 0.0)
        if c == w - LANE:
            x = x + jnp.where(lane >= LANE - halo, right, 0.0)
        out[:, c + LANE : c + 2 * LANE] = x
        own = x[halo : halo + rows]
        block[:, c : c + LANE] = own
        part = jnp.sum((own * own).reshape(rows // 8, 8, LANE), axis=0)
        total = part if total is None else total + part
    stat[...] = total


def merge_cols(n, rows, place, q, recv_a, recv_b, before, halo):
    ext, wide = q.shape
    w = wide - LANE
    return pl.pallas_call(
        functools.partial(cols_kernel, n, rows, halo),
        out_shape=[
            jax.ShapeDtypeStruct((ext, w + 2 * LANE), f32),
            jax.ShapeDtypeStruct((rows, w), f32),
            jax.ShapeDtypeStruct((8, LANE), f32),
        ],
        in_specs=[SMEM] + [VMEM] * 4,
        out_specs=[VMEM] * 3,
        name="merge_cols",
    )(place, q, recv_a, recv_b, before)


def wrap_kernel(rows, halo, w, place, send_a, mid, send_b, recv_a, recv_b, before, out):
    odd = lax.rem(place[1], 2)
    keep = rows - 2 * halo
    pieces = (
        (0, halo, mid[:halo, :] + choose(odd, recv_a[...], recv_b[...])),
        (halo, keep, mid[halo : rows - halo, :]),
        (rows - halo, halo, mid[rows - halo :, :] + choose(odd, recv_b[...], recv_a[...])),
    )
    edges = []
    for start, size, value in pieces:
        span = slice(start, start + size)
        out[span, :] = value[:, :w] + damping * before[span, :]
        edges.append(value[:, w:])
    out[rows:, :] = pack_edge(jnp.concatenate(edges, axis=0), halo, w)


def wrap(place, send_a, mid, send_b, recv_a, recv_b, before, halo):
    rows, w = before.shape
    height = rows + rows * 2 * halo // w
    return pl.pallas_call(
        functools.partial(wrap_kernel, rows, halo, w),
        out_shape=jax.ShapeDtypeStruct((height, w), f32),
        in_specs=[SMEM] + [VMEM] * 6,
        out_specs=VMEM,
        name="wrap",
    )(place, send_a, mid, send_b, recv_a, recv_b, before)


def solution_kernel(n, w, place, est, sums, *refs):
    k0, k1 = refs[:n], refs[n : 2 * n]
    sol, res, coef = refs[2 * n :]
    total = [
        jnp.sum(jnp.sum(sums[i], axis=0, keepdims=True), axis=1, keepdims=True) for i in range(4)
    ]
    k00, k11 = total[0], total[2]
    k01 = total[1] + damping * k00
    k12 = total[3] + damping * k11
    alpha0 = k00 / k01
    norm1 = k00 - 2.0 * alpha0 * k01 + alpha0 * alpha0 * k11
    beta = norm1 / k00
    curve1 = (1.0 + beta) * (1.0 + beta) * k01 - 2.0 * (1.0 + beta) * alpha0 * k11
    curve1 = curve1 + alpha0 * alpha0 * k12
    alpha1 = norm1 / curve1
    c1 = alpha0 + alpha1 * (1.0 + beta)
    c2 = alpha0 * alpha1
    coef[...] = jnp.broadcast_to(c2, coef.shape)
    for i in range(n):
        cols = pl.ds(pl.multiple_of(jnp.bitwise_xor(place[0], i) * w, LANE), w)
        a0, a1 = k0[i][...], k1[i][...]
        sol[:, cols] = est[:, cols] + c1 * a0 - c2 * a1
        res[:, cols] = a0 - c1 * a1


def solution_image(place, est, sums, k0, k1):
    n = len(k0)
    w = k0[0].shape[1]
    return pl.pallas_call(
        functools.partial(solution_kernel, n, w),
        out_shape=[jax.ShapeDtypeStruct(est.shape, f32)] * 2
        + [jax.ShapeDtypeStruct((8, LANE), f32)],
        in_specs=[SMEM] + [VMEM] * (2 + 2 * n),
        out_specs=[VMEM] * 3,
        name="solution_image",
    )(place, est, sums, *k0, *k1)


def residual_kernel(n, rows, halo, w, place, base, coef, *refs):
    k2, (res, full) = refs[:n], refs[n:]
    c2 = coef[0:1, 0:1]
    lane = lax.broadcasted_iota(jnp.int32, (rows, LANE), 1)
    spot = [jnp.bitwise_xor(place[0], i) for i in range(n)]
    full[:, :LANE] = jnp.zeros((rows, LANE), f32)
    full[:, LANE + n * w :] = jnp.zeros((rows, LANE), f32)
    for i in range(n):
        full[:, pl.ds(pl.multiple_of(spot[i] * w + LANE, LANE), w)] = k2[i][:rows, :]
    for i in range(n):
        edge = unpack_edge(k2[i][rows:, :], halo)
        left = pl.ds(pl.multiple_of(spot[i] * w, LANE), LANE)
        right = pl.ds(pl.multiple_of(spot[i] * w + w + LANE, LANE), LANE)
        full[:, left] += jnp.where(lane >= LANE - halo, edge, 0.0)
        full[:, right] += jnp.where(lane < halo, edge, 0.0)
    for c in range(0, n * w, LANE):
        res[:, c : c + LANE] = base[:, c : c + LANE] + c2 * full[:, c + LANE : c + 2 * LANE]


def residual_image(place, base, coef, k2, halo):
    n = len(k2)
    rows, cols = base.shape
    w = cols // n
    return pl.pallas_call(
        functools.partial(residual_kernel, n, rows, halo, w),
        out_shape=jax.ShapeDtypeStruct(base.shape, f32),
        in_specs=[SMEM] + [VMEM] * (2 + n),
        out_specs=VMEM,
        scratch_shapes=[pltpu.VMEM((rows, cols + 2 * LANE), f32)],
        name="residual_image",
    )(place, base, coef, *k2)


def neighbours(send_a, send_b, axis):
    n = lax.axis_size(axis)
    out = []
    for lead, x in ((0, send_a), (1, send_b)):
        pairs = [(i, i + 1) for i in range(lead, n - 1, 2)]
        out.append(lax.ppermute(x, axis, pairs + [(b, a) for a, b in pairs]))
    return out


def swap(x, axis, distance):
    n = lax.axis_size(axis)
    return lax.ppermute(x, axis, [(i, i ^ distance) for i in range(n)])


def steps(estimate, observed, weights, column_kernels, row_kernels):
    n = lax.axis_size("frame")
    me = lax.axis_index("frame")
    strips = lax.axis_size("strip")
    strip = lax.axis_index("strip")
    place = jnp.stack([me, strip]).astype(jnp.int32)
    rows, cols = estimate.shape
    frames = weights.shape[0]
    halo = column_kernels.shape[1] // 2
    w = cols // n
    distances = [1 << k for k in range(n.bit_length() - 1)]

    low, high = estimate[:halo], estimate[rows - halo :]
    odd = strip % 2 == 1
    est_a, est_b = neighbours(
        jnp.where(odd, low, high), jnp.where(odd, high, low), "strip"
    )

    early = frames // 2
    plan = [(d, 0, frames, True) for d in range(1, n - 1)]
    plan += [(n - 1, 0, early, True), (n - 1, early, frames - early, False)]
    packed, tile, own_mats = prepare(plan, place, column_kernels, row_kernels, weights, w, halo)
    moved = []
    for i, (d, _, _, taps) in enumerate(plan):
        moved.append(swap(packed[i], "frame", d))
    origin = {}
    starts = [0]
    for i, (d, lead, count, taps) in enumerate(plan):
        for k in range(count):
            origin[d, lead + k] = (i, k * rows)
        if taps:
            starts.append(count * rows)

    send_a, mid, send_b = first_terms(
        place, estimate, est_a, est_b, own_mats, weights, observed
    )
    mats = setup_matrices([tile] + moved[: n - 1], starts, frames, rows, halo)
    recv_a, recv_b = neighbours(send_a, send_b, "strip")

    part = list(column_blocks(n, place, send_a, mid, send_b, recv_a, recv_b, w))
    mine = [part[0]]
    for i in range(n - 1, 0, -1):
        d = i & -i
        got = swap(part[i], "frame", d)
        if i == d:
            mine.append(got)
        else:
            part[i ^ d] = part[i ^ d] + got
    k0, wide, send_a, send_b, k00_part = start_image(n, place, estimate, mine, halo)
    recv_a, recv_b = neighbours(send_a, send_b, "strip")

    send_a, mid, send_b, stat1, k0x = apply_terms(
        place, (wide, recv_a, recv_b), mats, weights, moved, origin, 2 * halo, halo
    )
    recv_a, recv_b = neighbours(send_a, send_b, "strip")
    q, col_a, col_b = merge_rows(strips, place, send_a, mid, send_b, recv_a, recv_b, halo)
    recv_a, recv_b = neighbours(col_a, col_b, "frame")
    k1x, k1, k11_part = merge_cols(n, rows, place, q, recv_a, recv_b, k0x, halo)

    send_a, mid, send_b, stat2 = apply_terms(
        place, (k1x,), mats, weights, moved, origin, halo, halo
    )
    recv_a, recv_b = neighbours(send_a, send_b, "strip")
    sums = jnp.stack([k00_part, stat1, k11_part, stat2])
    for axis, size in (("strip", strips), ("frame", n)):
        d = 1
        while d < size:
            sums = sums + swap(sums, axis, d)
            d *= 2
    k2 = wrap(place, send_a, mid, send_b, recv_a, recv_b, k1, halo)

    def gathered(x):
        parts = [x] + [None] * (n - 1)
        for i in range(n):
            for d in reversed(distances):
                if i % (2 * d) == 0:
                    parts[i + d] = swap(parts[i], "frame", d)
        return parts

    g0, g1, g2 = gathered(k0), gathered(k1), gathered(k2)
    result, base, coef = solution_image(place, estimate, sums, g0, g1)
    return result, residual_image(place, base, coef, g2, halo)


def solution(mesh):
    return jax.shard_map(
        steps,
        mesh=mesh,
        in_specs=(
            P("strip", None),
            P("frame", "strip", None),
            P("frame", "strip", None),
            P("frame", None),
            P("frame", None),
        ),
        out_specs=(P("strip", None), P("strip", None)),
        check_vma=False,
    )
```

profile of v0, /device:TPU:2, one launch (start us, length us, event | category | flops | bytes accessed | tf_op | source)
XLA Modules:
  0.0 231.2 jit_solution(12731156144213647475)
XLA Ops:
  1.8 1.9 collective-permute-start.1
  4.4 4.0 %prepare.1 = (f32[264,512]{1,0:T(8,128)}, f32[264,512]{1,0:T(8,128)}, f32[136,512]{1,0:T(8,128)}, f32[128,512]{1,0:T(8,128)}, f32[8,512]{1,0:T(8,128)}, /*index=...) custom-call(s32[2]{0:T(128)} %pad_add_fusion.place, ...), custom_call_target="tpu_custom_call" | custom-call | tf_op jit(solution)/shard_map/prepare/pallas_call | solution.py:334
  8.4 1.1 collective-permute-done.1.recv_b
  10.2 8.2 %first_terms.1 = (f32[32,2048]{1,0:T(8,128)}, f32[128,2048]{1,0:T(8,128)}, f32[32,2048]{1,0:T(8,128)}) custom-call(s32[2]{0:T(128)} %pad_add_fusion.place, f32[128,2048]{1,0:T(8,128)} %est.5, f32[32,2048]{1,0:T(8,128)} %copy-done.30, f32[32,2048]{1,0:T(8,128)} %copy-done.31, bf16[2,256,256]{2,1,0:T(8,128)(2,1)} %get-tuple-element.45.t_ref, ...), custom_call_target="tpu_custom_call" | custom-call | flops 8000000000 | bytes 8388608 | tf_op jit(solution)/shard_map/first_terms/pallas_call | solution.py:286
  18.4 3.6 %collective-permute-start.2 = (f32[32,2048]{1,0:T(8,128)}, f32[32,2048]{1,0:T(8,128)S(1)}, u32[]{:S(2)}, u32[]{:S(2)}) collective-permute-start(f32[32,2048]{1,0:T(8,128)} %get-tuple-element.49.send_a), channel_id=1, source_target_pairs={{0,4},{8,12},{16,20},{24,28},{4,0},{12,8},{20,16},{28,24},{1,5},{9... | collective-permute-start | bytes 786440 | tf_op jit(solution)/shard_map/ppermute | solution.py:710
  22.0 1.9 collective-permute-start.3
  24.0 6.7 %collective-permute-done.3.recv_b = f32[32,2048]{1,0:T(8,128)S(1)} collective-permute-done((f32[32,2048]{1,0:T(8,128)}, f32[32,2048]{1,0:T(8,128)S(1)}, u32[]{:S(2)}, u32[]{:S(2)}) %collective-permute-start.3) | collective-permute-done | bytes 262176 | tf_op jit(solution)/shard_map/ppermute | solution.py:710
  31.4 2.8 %column_blocks.1 = (f32[144,512]{1,0:T(8,128)}, f32[144,512]{1,0:T(8,128)}, f32[144,512]{1,0:T(8,128)}, f32[144,512]{1,0:T(8,128)}) custom-call(s32[2]{0:T(128)} %pad_add_fusion.place, f32[32,2048]{1,0:T(8,128)} %get-tuple-element.49.send_a, f32[128,2048]{1,0:T(8,128)} %get-tuple-element.50.mid, f32[32,2048]{1,0:T(8,128)} %get-tuple-element.51.send_b, ...), custom_call_target="tpu_custom_call" | custom-call | tf_op jit(solution)/shard_map/column_blocks/pallas_call | solution.py:373
  36.2 2.0 collective-permute-start.10
  38.2 1.6 collective-permute-start.9
  39.8 15.3 %collective-permute-done.4 = f32[144,512]{1,0:T(8,128)S(1)} collective-permute-done((f32[144,512]{1,0:T(8,128)}, f32[144,512]{1,0:T(8,128)S(1)}, u32[]{:S(2)}, u32[]{:S(2)}) %collective-permute-start.4) | collective-permute-done | bytes 294944 | tf_op jit(solution)/shard_map/ppermute | solution.py:716
  56.1 2.0 collective-permute-start.11
  58.1 3.2 %collective-permute-done.6.refs_2_ = f32[144,512]{1,0:T(8,128)S(1)} collective-permute-done((f32[144,512]{1,0:T(8,128)}, f32[144,512]{1,0:T(8,128)S(1)}, u32[]{:S(2)}, u32[]{:S(2)}) %collective-permute-start.6) | collective-permute-done | bytes 294944 | tf_op jit(solution)/shard_map/ppermute | solution.py:716
  62.1 15.3 %collective-permute-done.5.refs_1_ = f32[144,512]{1,0:T(8,128)S(1)} collective-permute-done((f32[144,512]{1,0:T(8,128)S(1)}, f32[144,512]{1,0:T(8,128)S(1)}, u32[]{:S(2)}, u32[]{:S(2)}) %collective-permute-start.5) | collective-permute-done | bytes 294944 | tf_op jit(solution)/shard_map/ppermute | solution.py:716
  78.1 2.5 %start_image.1 = (f32[128,512]{1,0:T(8,128)}, f32[128,768]{1,0:T(8,128)}, f32[32,768]{1,0:T(8,128)}, f32[32,768]{1,0:T(8,128)}, f32[8,128]{1,0:T(8,128)}) custom-call(s32[2]{0:T(128)} %pad_add_fusion.place, f32[128,2048]{1,0:T(8,128)} %est.5, f32[144,512]{1,0:T(8,128)} %get-tuple-element.52.refs_0_, f32[144,512]{1,0:T(8,128)} %copy-done.7, f32[144,512]{1,0:T(8,128)} %copy-done.6), custom_call_target="tpu_custom_call" | custom-call | tf_op jit(solution)/shard_map/start_image/pallas_call | solution.py:416
  80.7 2.6 %collective-permute-start.7 = (f32[32,768]{1,0:T(8,128)}, f32[32,768]{1,0:T(8,128)S(1)}, u32[]{:S(2)}, u32[]{:S(2)}) collective-permute-start(f32[32,768]{1,0:T(8,128)} %get-tuple-element.58), channel_id=1, source_target_pairs={{0,4},{8,12},{16,20},{24,28},{4,0},{12,8},{20,16},{28,24},{1,5},{9... | collective-permute-start | bytes 294920 | tf_op jit(solution)/shard_map/ppermute | solution.py:710
  83.3 3.1 %collective-permute-done.11.refs_3_.refs_10_.refs_8_ = f32[136,512]{1,0:T(8,128)S(1)} collective-permute-done((f32[136,512]{1,0:T(8,128)S(1)}, f32[136,512]{1,0:T(8,128)S(1)}, u32[]{:S(2)}, u32[]{:S(2)}) %collective-permute-start.11) | collective-permute-done | bytes 278560 | tf_op jit(solution)/shard_map/ppermute | solution.py:716
  86.4 1.9 collective-permute-start.8
  89.3 4.5 %setup_all.1 = (bf16[8,256,256]{2,1,0:T(8,128)(2,1)}, bf16[8,256,256]{2,1,0:T(8,128)(2,1)}, bf16[8,256,256]{2,1,0:T(8,128)(2,1)}, bf16[4,384,256]{2,1,0:T(8,128)(2,1)}) custom-call(f32[8,512]{1,0:T(8,128)} %get-tuple-element.60.refs_0_, f32[264,512]{1,0:T(8,128)} %copy-done.2, f32[264,512]{1,0:T(8,128)} %copy-done.1, f32[136,512]{1,0:T(8,128)} %copy-done.8), custom_call_target="tpu_custom_call" | custom-call | tf_op jit(solution)/shard_map/setup_all/pallas_call | solution.py:130
  94.5 10.7 %shard_map.68 = (f32[64,640]{1,0:T(8,128)}, f32[64,640]{1,0:T(8,128)}, f32[64,640]{1,0:T(8,128)}, f32[8,128]{1,0:T(8,128)}, f32[192,768]{1,0:T(8,128)}) custom-call(s32[2]{0:T(128)} %pad_add_fusion.place, f32[128,768]{1,0:T(8,128)} %get-tuple-element.57.refs_0_, f32[32,768]{1,0:T(8,128)} %copy-done.32, f32[32,768]{1,0:T(8,128)} %copy-done.33, ...), custom_call_target="tpu_custom_call" | custom-call | flops 12000000000 | bytes 4194304 | tf_op jit(solution)/shard_map/pallas_call | solution.py:501
  105.2 5.3 %collective-permute-start.13 = (f32[64,640]{1,0:T(8,128)}, f32[64,640]{1,0:T(8,128)S(1)}, u32[]{:S(2)}, u32[]{:S(2)}) collective-permute-start(f32[64,640]{1,0:T(8,128)} %get-tuple-element.70.send_a), channel_id=1, source_target_pairs={{0,4},{8,12},{16,20},{24,28},{4,0},{12,8},{20,16},{28,24},{1,5},{9... | collective-permute-start | bytes 491528 | tf_op jit(solution)/shard_map/ppermute | solution.py:710
  110.5 1.9 collective-permute-start.14
  112.4 4.9 %collective-permute-done.14.recv_b = f32[64,640]{1,0:T(8,128)S(1)} collective-permute-done((f32[64,640]{1,0:T(8,128)}, f32[64,640]{1,0:T(8,128)S(1)}, u32[]{:S(2)}, u32[]{:S(2)}) %collective-permute-start.14) | collective-permute-done | bytes 163872 | tf_op jit(solution)/shard_map/ppermute | solution.py:710
  117.9 2.2 merge_rows.1
  120.1 5.3 %collective-permute-start.15 = (f32[192,128]{1,0:T(8,128)}, f32[192,128]{1,0:T(8,128)S(1)}, u32[]{:S(2)}, u32[]{:S(2)}) collective-permute-start(f32[192,128]{1,0:T(8,128)} %get-tuple-element.74), channel_id=1, source_target_pairs={{0,1},{2,3},{1,0},{3,2},{4,5},{6,7},{5,4},{7,6},{8,9},{10,11},{9,8... | collective-permute-start | bytes 294920 | tf_op jit(solution)/shard_map/ppermute | solution.py:710
  126.3 2.8 %collective-permute-done.15.recv_a = f32[192,128]{1,0:T(8,128)S(1)} collective-permute-done((f32[192,128]{1,0:T(8,128)}, f32[192,128]{1,0:T(8,128)S(1)}, u32[]{:S(2)}, u32[]{:S(2)}) %collective-permute-start.15) | collective-permute-done | bytes 98336 | tf_op jit(solution)/shard_map/ppermute | solution.py:710
  129.7 2.3 merge_cols.1
  132.1 10.7 %shard_map.69 = (f32[32,640]{1,0:T(8,128)}, f32[128,640]{1,0:T(8,128)}, f32[32,640]{1,0:T(8,128)}, f32[8,128]{1,0:T(8,128)}) custom-call(s32[2]{0:T(128)} %pad_add_fusion.place, f32[192,768]{1,0:T(8,128)} %get-tuple-element.78.refs_0_, bf16[8,256,256]{2,1,0:T(8,128)(2,1)} %get-tuple-element.64.refs_3_.refs_1_, ...), custom_call_target="tpu_custom_call" | custom-call | flops 12000000000 | bytes 4194304 | tf_op jit(solution)/shard_map/pallas_call | solution.py:501
  143.0 1.9 collective-permute-start.29
  145.6 2.4 %collective-permute-start.17 = (f32[4,8,128]{2,1,0:T(8,128)S(1)}, f32[4,8,128]{2,1,0:T(8,128)S(1)}, u32[]{:S(2)}, u32[]{:S(2)}) collective-permute-start(f32[4,8,128]{2,1,0:T(8,128)S(1)} %pad_maximum_fusion), channel_id=1, source_target_pairs={{0,4},{4,0},{8,12},{12,8},{16,20},{20,16},{24,28},{28,24},{1,5},{5... | collective-permute-start | bytes 49160 | tf_op jit(solution)/shard_map/ppermute | solution.py:716
  149.6 2.1 wrap.1.refs_0_
  151.6 5.0 %collective-permute-start.31 = (f32[144,512]{1,0:T(8,128)}, f32[144,512]{1,0:T(8,128)S(1)}, u32[]{:S(2)}, u32[]{:S(2)}) collective-permute-start(f32[144,512]{1,0:T(8,128)} %wrap.1.refs_0_), channel_id=1, source_target_pairs={{0,2},{1,3},{2,0},{3,1},{4,6},{5,7},{6,4},{7,5},{8,10},{9,11},{10,... | collective-permute-start | bytes 884744 | tf_op jit(solution)/shard_map/ppermute | solution.py:716
  157.4 1.7 collective-permute-start.22
  159.1 1.2 collective-permute-start.26
  161.8 3.1 %collective-permute-start.19 = (f32[4,8,128]{2,1,0:T(8,128)S(1)}, f32[4,8,128]{2,1,0:T(8,128)S(1)}, u32[]{:S(2)}, u32[]{:S(2)}) collective-permute-start(f32[4,8,128]{2,1,0:T(8,128)S(1)} %fusion.1), channel_id=1, source_target_pairs={{0,16},{4,20},{8,24},{12,28},{16,0},{20,4},{24,8},{28,12},{1,17},{... | collective-permute-start | bytes 49160 | tf_op jit(solution)/shard_map/ppermute | solution.py:716
  164.8 1.7 collective-permute-done.19
  166.6 2.0 collective-permute-start.20
  168.6 12.5 %collective-permute-done.20 = f32[4,8,128]{2,1,0:T(8,128)S(1)} collective-permute-done((f32[4,8,128]{2,1,0:T(8,128)S(1)}, f32[4,8,128]{2,1,0:T(8,128)S(1)}, u32[]{:S(2)}, u32[]{:S(2)}) %collective-permute-start.20) | collective-permute-done | bytes 16416 | tf_op jit(solution)/shard_map/ppermute | solution.py:716
  181.1 2.5 %collective-permute-start.30 = (f32[144,512]{1,0:T(8,128)}, f32[144,512]{1,0:T(8,128)S(1)}, u32[]{:S(2)}, u32[]{:S(2)}) collective-permute-start(f32[144,512]{1,0:T(8,128)} %wrap.1.refs_0_), channel_id=1, source_target_pairs={{0,1},{1,0},{2,3},{3,2},{4,5},{5,4},{6,7},{7,6},{8,9},{9,8},{10,11... | collective-permute-start | bytes 884744 | tf_op jit(solution)/shard_map/ppermute | solution.py:716
  183.7 3.6 %collective-permute-done.23.refs_2_ = f32[128,512]{1,0:T(8,128)S(1)} collective-permute-done((f32[128,512]{1,0:T(8,128)S(1)}, f32[128,512]{1,0:T(8,128)S(1)}, u32[]{:S(2)}, u32[]{:S(2)}) %collective-permute-start.23) | collective-permute-done | bytes 262176 | tf_op jit(solution)/shard_map/ppermute | solution.py:716
  187.3 1.7 collective-permute-start.24
  189.0 8.9 %collective-permute-done.21 = f32[4,8,128]{2,1,0:T(8,128)S(1)} collective-permute-done((f32[4,8,128]{2,1,0:T(8,128)S(1)}, f32[4,8,128]{2,1,0:T(8,128)S(1)}, u32[]{:S(2)}, u32[]{:S(2)}) %collective-permute-start.21) | collective-permute-done | bytes 16416 | tf_op jit(solution)/shard_map/ppermute | solution.py:716
  197.9 2.2 collective-permute-start.25
  200.7 11.5 %collective-permute-done.24.refs_3_ = f32[128,512]{1,0:T(8,128)S(1)} collective-permute-done((f32[128,512]{1,0:T(8,128)S(1)}, f32[128,512]{1,0:T(8,128)S(1)}, u32[]{:S(2)}, u32[]{:S(2)}) %collective-permute-start.24) | collective-permute-done | bytes 262176 | tf_op jit(solution)/shard_map/ppermute | solution.py:716
  212.2 5.6 %collective-permute-done.25.refs_5_ = f32[128,512]{1,0:T(8,128)S(1)} collective-permute-done((f32[128,512]{1,0:T(8,128)S(1)}, f32[128,512]{1,0:T(8,128)S(1)}, u32[]{:S(2)}, u32[]{:S(2)}) %collective-permute-start.25) | collective-permute-done | bytes 262176 | tf_op jit(solution)/shard_map/ppermute | solution.py:716
  217.8 5.6 %collective-permute-done.27.refs_7_ = f32[128,512]{1,0:T(8,128)S(1)} collective-permute-done((f32[128,512]{1,0:T(8,128)S(1)}, f32[128,512]{1,0:T(8,128)S(1)}, u32[]{:S(2)}, u32[]{:S(2)}) %collective-permute-start.27) | collective-permute-done | bytes 262176 | tf_op jit(solution)/shard_map/ppermute | solution.py:716
  224.1 3.4 %solution_image.1 = (f32[128,2048]{1,0:T(8,128)}, f32[128,2048]{1,0:T(8,128)}, f32[8,128]{1,0:T(8,128)}) custom-call(s32[2]{0:T(128)} %pad_add_fusion.place, f32[128,2048]{1,0:T(8,128)} %est.5, f32[4,8,128]{2,1,0:T(8,128)} %add.28.sums, f32[128,512]{1,0:T(8,128)} %get-tuple-element.80.refs_0_, f32[128,512]{1,0:T(8,128)} %copy-done.13, ...), custom_call_target="tpu_custom_call" | custom-call | tf_op jit(solution)/shard_map/solution_image/pallas_call | solution.py:662
  228.3 2.9 %residual_image.1 = f32[128,2048]{1,0:T(8,128)} custom-call(s32[2]{0:T(128)} %pad_add_fusion.place, f32[128,2048]{1,0:T(8,128)} %get-tuple-element.83.base, f32[8,128]{1,0:T(8,128)} %get-tuple-element.84.coef, f32[144,512]{1,0:T(8,128)} %wrap.1.refs_0_, f32[144,512]{1,0:T(8,128)} %copy-done.4, f32[144,512]{1,0:T(8,128)} %copy-done.3, f32[144,512]{1,0:T(8,128)} %copy-done.5), custom_call_target="tpu_custom_call" | custom-call | tf_op jit(solution)/shard_map/residual_image/pallas_call | solution.py:695
  (107 shorter events, 18.4 us)
Async XLA Ops:
  1.7 6.7 %collective-permute-start = (f32[32,2048]{1,0:T(8,128)S(1)}, f32[32,2048]{1,0:T(8,128)S(1)}, u32[]{:S(2)}, u32[]{:S(2)}) collective-permute-start(f32[32,2048]{1,0:T(8,128)S(1)} %get-tuple-element.89), channel_id=1, source_target_pairs={{0,4},{8,12},{16,20},{24,28},{4,0},{12,8},{20,16},{28,24},{1,5},{9... | collective-permute-start | bytes 786440 | tf_op jit(solution)/shard_map/ppermute | solution.py:710
  1.8 7.7 %collective-permute-start.1 = (f32[32,2048]{1,0:T(8,128)S(1)}, f32[32,2048]{1,0:T(8,128)S(1)}, u32[]{:S(2)}, u32[]{:S(2)}) collective-permute-start(f32[32,2048]{1,0:T(8,128)S(1)} %get-tuple-element.88), channel_id=1, source_target_pairs={{4,8},{12,16},{20,24},{8,4},{16,12},{24,20},{5,9},{13,17},{21,25},... | collective-permute-start | bytes 786440 | tf_op jit(solution)/shard_map/ppermute | solution.py:710
  18.4 17.9 %copy-start.28 = (f32[264,512]{1,0:T(8,128)S(1)}, f32[264,512]{1,0:T(8,128)}, u32[]{:S(2)}) copy-start(f32[264,512]{1,0:T(8,128)} %get-tuple-element.62) | copy-start | bytes 1622020
  18.4 19.8 %copy-start.27 = (f32[264,512]{1,0:T(8,128)S(1)}, f32[264,512]{1,0:T(8,128)}, u32[]{:S(2)}) copy-start(f32[264,512]{1,0:T(8,128)} %get-tuple-element.61) | copy-start | bytes 1622020
  18.4 37.7 %copy-start.29 = (f32[136,512]{1,0:T(8,128)S(1)}, f32[136,512]{1,0:T(8,128)}, u32[]{:S(2)}) copy-start(f32[136,512]{1,0:T(8,128)} %get-tuple-element.63) | copy-start | bytes 835588
  18.4 5.6 %collective-permute-start.2 = (f32[32,2048]{1,0:T(8,128)}, f32[32,2048]{1,0:T(8,128)S(1)}, u32[]{:S(2)}, u32[]{:S(2)}) collective-permute-start(f32[32,2048]{1,0:T(8,128)} %get-tuple-element.49.send_a), channel_id=1, source_target_pairs={{0,4},{8,12},{16,20},{24,28},{4,0},{12,8},{20,16},{28,24},{1,5},{9... | collective-permute-start | bytes 786440 | tf_op jit(solution)/shard_map/ppermute | solution.py:710
  22.0 8.6 %collective-permute-start.3 = (f32[32,2048]{1,0:T(8,128)}, f32[32,2048]{1,0:T(8,128)S(1)}, u32[]{:S(2)}, u32[]{:S(2)}) collective-permute-start(f32[32,2048]{1,0:T(8,128)} %get-tuple-element.51.send_b), channel_id=1, source_target_pairs={{4,8},{12,16},{20,24},{8,4},{16,12},{24,20},{5,9},{13,17},{21,25},... | collective-permute-start | bytes 786440 | tf_op jit(solution)/shard_map/ppermute | solution.py:710
  24.0 6.7 %copy-start.9 = (f32[32,2048]{1,0:T(8,128)}, f32[32,2048]{1,0:T(8,128)S(1)}, u32[]{:S(2)}) copy-start(f32[32,2048]{1,0:T(8,128)S(1)} %collective-permute-done.2.recv_a) | copy-start | bytes 786436
  34.2 20.8 %collective-permute-start.4 = (f32[144,512]{1,0:T(8,128)}, f32[144,512]{1,0:T(8,128)S(1)}, u32[]{:S(2)}, u32[]{:S(2)}) collective-permute-start(f32[144,512]{1,0:T(8,128)} %get-tuple-element.54), channel_id=1, source_target_pairs={{0,1},{1,0},{2,3},{3,2},{4,5},{5,4},{6,7},{7,6},{8,9},{9,8},{10,11... | collective-permute-start | bytes 884744 | tf_op jit(solution)/shard_map/ppermute | solution.py:716
  35.2 26.2 %collective-permute-start.6 = (f32[144,512]{1,0:T(8,128)}, f32[144,512]{1,0:T(8,128)S(1)}, u32[]{:S(2)}, u32[]{:S(2)}) collective-permute-start(f32[144,512]{1,0:T(8,128)} %get-tuple-element.55), channel_id=1, source_target_pairs={{0,1},{1,0},{2,3},{3,2},{4,5},{5,4},{6,7},{7,6},{8,9},{9,8},{10,11... | collective-permute-start | bytes 884744 | tf_op jit(solution)/shard_map/ppermute | solution.py:716
  36.2 52.1 %collective-permute-start.10 = (f32[264,512]{1,0:T(8,128)S(1)}, f32[264,512]{1,0:T(8,128)S(1)}, u32[]{:S(2)}, u32[]{:S(2)}) collective-permute-start(f32[264,512]{1,0:T(8,128)S(1)} %copy-done.28), channel_id=1, source_target_pairs={{0,2},{1,3},{2,0},{3,1},{4,6},{5,7},{6,4},{7,5},{8,10},{9,11},{10,... | collective-permute-start | bytes 1622024 | tf_op jit(solution)/shard_map/ppermute | solution.py:716
  38.2 50.1 %collective-permute-start.9 = (f32[264,512]{1,0:T(8,128)S(1)}, f32[264,512]{1,0:T(8,128)S(1)}, u32[]{:S(2)}, u32[]{:S(2)}) collective-permute-start(f32[264,512]{1,0:T(8,128)S(1)} %copy-done.27), channel_id=1, source_target_pairs={{0,1},{1,0},{2,3},{3,2},{4,5},{5,4},{6,7},{7,6},{8,9},{9,8},{10,11... | collective-permute-start | bytes 1622024 | tf_op jit(solution)/shard_map/ppermute | solution.py:716
  56.1 21.4 %collective-permute-start.5 = (f32[144,512]{1,0:T(8,128)S(1)}, f32[144,512]{1,0:T(8,128)S(1)}, u32[]{:S(2)}, u32[]{:S(2)}) collective-permute-start(f32[144,512]{1,0:T(8,128)S(1)} %add.23), channel_id=1, source_target_pairs={{0,2},{1,3},{2,0},{3,1},{4,6},{5,7},{6,4},{7,5},{8,10},{9,11},{10,... | collective-permute-start | bytes 884744 | tf_op jit(solution)/shard_map/ppermute | solution.py:716
  56.1 30.2 %collective-permute-start.11 = (f32[136,512]{1,0:T(8,128)S(1)}, f32[136,512]{1,0:T(8,128)S(1)}, u32[]{:S(2)}, u32[]{:S(2)}) collective-permute-start(f32[136,512]{1,0:T(8,128)S(1)} %copy-done.29), channel_id=1, source_target_pairs={{0,3},{1,2},{2,1},{3,0},{4,7},{5,6},{6,5},{7,4},{8,11},{9,10},{10,... | collective-permute-start | bytes 835592 | tf_op jit(solution)/shard_map/ppermute | solution.py:716
  61.4 16.1 %copy-start.6 = (f32[144,512]{1,0:T(8,128)}, f32[144,512]{1,0:T(8,128)S(1)}, u32[]{:S(2)}) copy-start(f32[144,512]{1,0:T(8,128)S(1)} %collective-permute-done.6.refs_2_) | copy-start | bytes 884740
  61.4 32.4 %collective-permute-start.12 = (f32[128,512]{1,0:T(8,128)}, f32[128,512]{1,0:T(8,128)}, u32[]{:S(2)}, u32[]{:S(2)}) collective-permute-start(f32[128,512]{1,0:T(8,128)} %get-tuple-element.68), channel_id=1, source_target_pairs={{0,3},{1,2},{2,1},{3,0},{4,7},{5,6},{6,5},{7,4},{8,11},{9,10},{10,... | collective-permute-start | bytes 786440 | tf_op jit(solution)/shard_map/ppermute | solution.py:716
  80.7 13.1 %collective-permute-start.7 = (f32[32,768]{1,0:T(8,128)}, f32[32,768]{1,0:T(8,128)S(1)}, u32[]{:S(2)}, u32[]{:S(2)}) collective-permute-start(f32[32,768]{1,0:T(8,128)} %get-tuple-element.58), channel_id=1, source_target_pairs={{0,4},{8,12},{16,20},{24,28},{4,0},{12,8},{20,16},{28,24},{1,5},{9... | collective-permute-start | bytes 294920 | tf_op jit(solution)/shard_map/ppermute | solution.py:710
  86.4 7.4 %collective-permute-start.8 = (f32[32,768]{1,0:T(8,128)}, f32[32,768]{1,0:T(8,128)S(1)}, u32[]{:S(2)}, u32[]{:S(2)}) collective-permute-start(f32[32,768]{1,0:T(8,128)} %get-tuple-element.59), channel_id=1, source_target_pairs={{4,8},{12,16},{20,24},{8,4},{16,12},{24,20},{5,9},{13,17},{21,25},... | collective-permute-start | bytes 294920 | tf_op jit(solution)/shard_map/ppermute | solution.py:710
  105.2 7.2 %collective-permute-start.13 = (f32[64,640]{1,0:T(8,128)}, f32[64,640]{1,0:T(8,128)S(1)}, u32[]{:S(2)}, u32[]{:S(2)}) collective-permute-start(f32[64,640]{1,0:T(8,128)} %get-tuple-element.70.send_a), channel_id=1, source_target_pairs={{0,4},{8,12},{16,20},{24,28},{4,0},{12,8},{20,16},{28,24},{1,5},{9... | collective-permute-start | bytes 491528 | tf_op jit(solution)/shard_map/ppermute | solution.py:710
  110.5 6.8 %collective-permute-start.14 = (f32[64,640]{1,0:T(8,128)}, f32[64,640]{1,0:T(8,128)S(1)}, u32[]{:S(2)}, u32[]{:S(2)}) collective-permute-start(f32[64,640]{1,0:T(8,128)} %get-tuple-element.72.send_b), channel_id=1, source_target_pairs={{4,8},{12,16},{20,24},{8,4},{16,12},{24,20},{5,9},{13,17},{21,25},... | collective-permute-start | bytes 491528 | tf_op jit(solution)/shard_map/ppermute | solution.py:710
  120.1 8.9 %collective-permute-start.15 = (f32[192,128]{1,0:T(8,128)}, f32[192,128]{1,0:T(8,128)S(1)}, u32[]{:S(2)}, u32[]{:S(2)}) collective-permute-start(f32[192,128]{1,0:T(8,128)} %get-tuple-element.74), channel_id=1, source_target_pairs={{0,1},{2,3},{1,0},{3,2},{4,5},{6,7},{5,4},{7,6},{8,9},{10,11},{9,8... | collective-permute-start | bytes 294920 | tf_op jit(solution)/shard_map/ppermute | solution.py:710
  125.4 3.6 %collective-permute-start.16 = (f32[192,128]{1,0:T(8,128)}, f32[192,128]{1,0:T(8,128)S(1)}, u32[]{:S(2)}, u32[]{:S(2)}) collective-permute-start(f32[192,128]{1,0:T(8,128)} %get-tuple-element.75), channel_id=1, source_target_pairs={{1,2},{2,1},{5,6},{6,5},{9,10},{10,9},{13,14},{14,13},{17,18},{18,... | collective-permute-start | bytes 294920 | tf_op jit(solution)/shard_map/ppermute | solution.py:710
  132.0 12.9 %copy-start.24 = (f32[8,128]{1,0:T(8,128)S(1)}, f32[8,128]{1,0:T(8,128)}, u32[]{:S(2)}) copy-start(f32[8,128]{1,0:T(8,128)} %get-tuple-element.56) | copy-start | bytes 12292
  132.0 12.9 %copy-start.25 = (f32[8,128]{1,0:T(8,128)S(1)}, f32[8,128]{1,0:T(8,128)}, u32[]{:S(2)}) copy-start(f32[8,128]{1,0:T(8,128)} %get-tuple-element.69) | copy-start | bytes 12292
  132.0 12.9 %copy-start.26 = (f32[8,128]{1,0:T(8,128)S(1)}, f32[8,128]{1,0:T(8,128)}, u32[]{:S(2)}) copy-start(f32[8,128]{1,0:T(8,128)} %get-tuple-element.77) | copy-start | bytes 12292
  132.0 25.3 %copy-start.11 = (f32[128,512]{1,0:T(8,128)S(1)}, f32[128,512]{1,0:T(8,128)}, u32[]{:S(2)}) copy-start(f32[128,512]{1,0:T(8,128)} %get-tuple-element.80.refs_0_) | copy-start | bytes 786436
  132.1 27.1 %copy-start = (f32[128,512]{1,0:T(8,128)S(1)}, f32[128,512]{1,0:T(8,128)}, u32[]{:S(2)}) copy-start(f32[128,512]{1,0:T(8,128)} %get-tuple-element.81.refs_4_.before) | copy-start | bytes 786436
  142.8 5.2 %collective-permute-start.28 = (f32[32,640]{1,0:T(8,128)}, f32[32,640]{1,0:T(8,128)S(1)}, u32[]{:S(2)}, u32[]{:S(2)}) collective-permute-start(f32[32,640]{1,0:T(8,128)} %get-tuple-element.85.send_a), channel_id=1, source_target_pairs={{0,4},{8,12},{16,20},{24,28},{4,0},{12,8},{20,16},{28,24},{1,5},{9... | collective-permute-start | bytes 245768 | tf_op jit(solution)/shard_map/ppermute | solution.py:710
  143.0 6.0 %collective-permute-start.29 = (f32[32,640]{1,0:T(8,128)}, f32[32,640]{1,0:T(8,128)S(1)}, u32[]{:S(2)}, u32[]{:S(2)}) collective-permute-start(f32[32,640]{1,0:T(8,128)} %get-tuple-element.87.send_b), channel_id=1, source_target_pairs={{4,8},{12,16},{20,24},{8,4},{16,12},{24,20},{5,9},{13,17},{21,25},... | collective-permute-start | bytes 245768 | tf_op jit(solution)/shard_map/ppermute | solution.py:710
  145.6 11.1 %collective-permute-start.17 = (f32[4,8,128]{2,1,0:T(8,128)S(1)}, f32[4,8,128]{2,1,0:T(8,128)S(1)}, u32[]{:S(2)}, u32[]{:S(2)}) collective-permute-start(f32[4,8,128]{2,1,0:T(8,128)S(1)} %pad_maximum_fusion), channel_id=1, source_target_pairs={{0,4},{4,0},{8,12},{12,8},{16,20},{20,16},{24,28},{28,24},{1,5},{5... | collective-permute-start | bytes 49160 | tf_op jit(solution)/shard_map/ppermute | solution.py:716
  151.6 31.9 %collective-permute-start.31 = (f32[144,512]{1,0:T(8,128)}, f32[144,512]{1,0:T(8,128)S(1)}, u32[]{:S(2)}, u32[]{:S(2)}) collective-permute-start(f32[144,512]{1,0:T(8,128)} %wrap.1.refs_0_), channel_id=1, source_target_pairs={{0,2},{1,3},{2,0},{3,1},{4,6},{5,7},{6,4},{7,5},{8,10},{9,11},{10,... | collective-permute-start | bytes 884744 | tf_op jit(solution)/shard_map/ppermute | solution.py:716
  157.4 3.7 %collective-permute-start.18 = (f32[4,8,128]{2,1,0:T(8,128)S(1)}, f32[4,8,128]{2,1,0:T(8,128)S(1)}, u32[]{:S(2)}, u32[]{:S(2)}) collective-permute-start(f32[4,8,128]{2,1,0:T(8,128)S(1)} %fusion), channel_id=1, source_target_pairs={{0,8},{4,12},{8,0},{12,4},{16,24},{20,28},{24,16},{28,20},{1,9},{5... | collective-permute-start | bytes 49160 | tf_op jit(solution)/shard_map/ppermute | solution.py:716
  157.4 29.9 %collective-permute-start.23 = (f32[128,512]{1,0:T(8,128)S(1)}, f32[128,512]{1,0:T(8,128)S(1)}, u32[]{:S(2)}, u32[]{:S(2)}) collective-permute-start(f32[128,512]{1,0:T(8,128)S(1)} %copy-done.11), channel_id=1, source_target_pairs={{0,2},{1,3},{2,0},{3,1},{4,6},{5,7},{6,4},{7,5},{8,10},{9,11},{10,... | collective-permute-start | bytes 786440 | tf_op jit(solution)/shard_map/ppermute | solution.py:716
  157.4 29.8 %collective-permute-start.22 = (f32[128,512]{1,0:T(8,128)S(1)}, f32[128,512]{1,0:T(8,128)S(1)}, u32[]{:S(2)}, u32[]{:S(2)}) collective-permute-start(f32[128,512]{1,0:T(8,128)S(1)} %copy-done.11), channel_id=1, source_target_pairs={{0,1},{1,0},{2,3},{3,2},{4,5},{5,4},{6,7},{7,6},{8,9},{9,8},{10,11... | collective-permute-start | bytes 786440 | tf_op jit(solution)/shard_map/ppermute | solution.py:716
  159.1 40.9 %collective-permute-start.26 = (f32[128,512]{1,0:T(8,128)S(1)}, f32[128,512]{1,0:T(8,128)S(1)}, u32[]{:S(2)}, u32[]{:S(2)}) collective-permute-start(f32[128,512]{1,0:T(8,128)S(1)} %copy-done), channel_id=1, source_target_pairs={{0,2},{1,3},{2,0},{3,1},{4,6},{5,7},{6,4},{7,5},{8,10},{9,11},{10,... | collective-permute-start | bytes 786440 | tf_op jit(solution)/shard_map/ppermute | solution.py:716
  161.8 4.8 %collective-permute-start.19 = (f32[4,8,128]{2,1,0:T(8,128)S(1)}, f32[4,8,128]{2,1,0:T(8,128)S(1)}, u32[]{:S(2)}, u32[]{:S(2)}) collective-permute-start(f32[4,8,128]{2,1,0:T(8,128)S(1)} %fusion.1), channel_id=1, source_target_pairs={{0,16},{4,20},{8,24},{12,28},{16,0},{20,4},{24,8},{28,12},{1,17},{... | collective-permute-start | bytes 49160 | tf_op jit(solution)/shard_map/ppermute | solution.py:716
  166.6 14.5 %collective-permute-start.20 = (f32[4,8,128]{2,1,0:T(8,128)S(1)}, f32[4,8,128]{2,1,0:T(8,128)S(1)}, u32[]{:S(2)}, u32[]{:S(2)}) collective-permute-start(f32[4,8,128]{2,1,0:T(8,128)S(1)} %add.26), channel_id=1, source_target_pairs={{0,1},{1,0},{2,3},{3,2},{4,5},{5,4},{6,7},{7,6},{8,9},{9,8},{10,11... | collective-permute-start | bytes 49160 | tf_op jit(solution)/shard_map/ppermute | solution.py:716
  181.1 46.4 %collective-permute-start.30 = (f32[144,512]{1,0:T(8,128)}, f32[144,512]{1,0:T(8,128)S(1)}, u32[]{:S(2)}, u32[]{:S(2)}) collective-permute-start(f32[144,512]{1,0:T(8,128)} %wrap.1.refs_0_), channel_id=1, source_target_pairs={{0,1},{1,0},{2,3},{3,2},{4,5},{5,4},{6,7},{7,6},{8,9},{9,8},{10,11... | collective-permute-start | bytes 884744 | tf_op jit(solution)/shard_map/ppermute | solution.py:716
  183.6 44.0 %copy-start.3 = (f32[144,512]{1,0:T(8,128)}, f32[144,512]{1,0:T(8,128)S(1)}, u32[]{:S(2)}) copy-start(f32[144,512]{1,0:T(8,128)S(1)} %collective-permute-done.31.refs_2_) | copy-start | bytes 884740
  183.6 44.0 %collective-permute-start.32 = (f32[144,512]{1,0:T(8,128)S(1)}, f32[144,512]{1,0:T(8,128)S(1)}, u32[]{:S(2)}, u32[]{:S(2)}) collective-permute-start(f32[144,512]{1,0:T(8,128)S(1)} %collective-permute-done.31.refs_2_), channel_id=1, source_target_pairs={{0,1},{1,0},{2,3},{3,2},{4,5},{5,4},{6,7},{7,6},{8,9},{9,8},{10,11... | collective-permute-start | bytes 884744 | tf_op jit(solution)/shard_map/ppermute | solution.py:716
  187.3 36.1 %copy-start.12 = (f32[128,512]{1,0:T(8,128)}, f32[128,512]{1,0:T(8,128)S(1)}, u32[]{:S(2)}) copy-start(f32[128,512]{1,0:T(8,128)S(1)} %collective-permute-done.23.refs_2_) | copy-start | bytes 786436
  187.3 10.6 %collective-permute-start.21 = (f32[4,8,128]{2,1,0:T(8,128)S(1)}, f32[4,8,128]{2,1,0:T(8,128)S(1)}, u32[]{:S(2)}, u32[]{:S(2)}) collective-permute-start(f32[4,8,128]{2,1,0:T(8,128)S(1)} %add.27), channel_id=1, source_target_pairs={{0,2},{1,3},{2,0},{3,1},{4,6},{5,7},{6,4},{7,5},{8,10},{9,11},{10,... | collective-permute-start | bytes 49160 | tf_op jit(solution)/shard_map/ppermute | solution.py:716
  187.3 36.1 %copy-start.13 = (f32[128,512]{1,0:T(8,128)}, f32[128,512]{1,0:T(8,128)S(1)}, u32[]{:S(2)}) copy-start(f32[128,512]{1,0:T(8,128)S(1)} %collective-permute-done.22.refs_1_) | copy-start | bytes 786436
  187.3 24.9 %collective-permute-start.24 = (f32[128,512]{1,0:T(8,128)S(1)}, f32[128,512]{1,0:T(8,128)S(1)}, u32[]{:S(2)}, u32[]{:S(2)}) collective-permute-start(f32[128,512]{1,0:T(8,128)S(1)} %collective-permute-done.23.refs_2_), channel_id=1, source_target_pairs={{0,1},{1,0},{2,3},{3,2},{4,5},{5,4},{6,7},{7,6},{8,9},{9,8},{10,11... | collective-permute-start | bytes 786440 | tf_op jit(solution)/shard_map/ppermute | solution.py:716
  197.9 19.9 %collective-permute-start.25 = (f32[128,512]{1,0:T(8,128)S(1)}, f32[128,512]{1,0:T(8,128)S(1)}, u32[]{:S(2)}, u32[]{:S(2)}) collective-permute-start(f32[128,512]{1,0:T(8,128)S(1)} %copy-done), channel_id=1, source_target_pairs={{0,1},{1,0},{2,3},{3,2},{4,5},{5,4},{6,7},{7,6},{8,9},{9,8},{10,11... | collective-permute-start | bytes 786440 | tf_op jit(solution)/shard_map/ppermute | solution.py:716
  200.0 23.4 %copy-start.14 = (f32[128,512]{1,0:T(8,128)}, f32[128,512]{1,0:T(8,128)S(1)}, u32[]{:S(2)}) copy-start(f32[128,512]{1,0:T(8,128)S(1)} %collective-permute-done.26.refs_6_) | copy-start | bytes 786436
  200.0 23.3 %collective-permute-start.27 = (f32[128,512]{1,0:T(8,128)S(1)}, f32[128,512]{1,0:T(8,128)S(1)}, u32[]{:S(2)}, u32[]{:S(2)}) collective-permute-start(f32[128,512]{1,0:T(8,128)S(1)} %collective-permute-done.26.refs_6_), channel_id=1, source_target_pairs={{0,1},{1,0},{2,3},{3,2},{4,5},{5,4},{6,7},{7,6},{8,9},{9,8},{10,11... | collective-permute-start | bytes 786440 | tf_op jit(solution)/shard_map/ppermute | solution.py:716
  212.2 11.2 %copy-start.15 = (f32[128,512]{1,0:T(8,128)}, f32[128,512]{1,0:T(8,128)S(1)}, u32[]{:S(2)}) copy-start(f32[128,512]{1,0:T(8,128)S(1)} %collective-permute-done.24.refs_3_) | copy-start | bytes 786436
  (19 other events, 24.5 us)
where the time goes:
time: 233 us; the launch traced here: 231 us
  waiting for transfers between devices  103 us (44%)
  starting transfers between devices  57.9 us (25%)
  Pallas kernels  56.3 us (24%)
  local copies, waits for them, and re-layouts  7.19 us (3%)
  other arithmetic  5.4 us (2%)
    ppermute x21, waiting for transfers between devices, swap(): return lax.ppermute(x, axis, [(i, i ^ distance) for i in range(n)])  87 us
    ppermute x21, starting transfers between devices, swap(): return lax.ppermute(x, axis, [(i, i ^ distance) for i in range(n)])  30.4 us
    ppermute x12, starting transfers between devices, neighbours(): out.append(lax.ppermute(x, axis, pairs + [(b, a) for a, b in pairs]))  27.5 us
    pallas_call x2, Pallas kernels, apply_terms(): pl.pallas_call(functools.partial(apply_kernel, frames, rows, halo, w, gro...  21.5 us
    ppermute x12, waiting for transfers between devices, neighbours(): out.append(lax.ppermute(x, axis, pairs + [(b, a) for a, b in pairs]))  16.4 us
    pallas_call x1, Pallas kernels, first_terms(): pl.pallas_call(functools.partial(first_kernel, frames, rows, halo), out_s...  8.18 us
    unnamed x68, local copies, waits for them, and re-layouts  7.19 us
  transfers between devices with their start and end apart: 33, of which 17 were waited for; matrix products, arithmetic and copies ran while one was open for 2% of the time, Pallas kernels for 7%

commit v1 on v0

--- a/solution.py
+++ b/solution.py
@@ -307,11 +307,11 @@
     outs, tile, mats, sem = refs[: len(plan)], refs[len(plan)], refs[len(plan) + 1 : -1], refs[-1]
     taps = cols_in.shape[1]
     pending = []
-    for i, (distance, lead, count, _) in enumerate(plan):
+    for i, (distance, _) in enumerate(plan):
         start = pl.multiple_of(jnp.bitwise_xor(place[0], distance) * w, LANE)
-        for k in range(count):
+        for k in range(frames):
             copy = pltpu.make_async_copy(
-                weights.at[lead + k, :, pl.ds(start, w)],
+                weights.at[k, :, pl.ds(start, w)],
                 outs[i].at[pl.ds(k * rows, rows), :],
                 sem.at[i, k],
             )
@@ -320,9 +320,9 @@
     tile[...] = jnp.zeros_like(tile)
     tile[:frames, :taps] = cols_in[...]
     tile[frames : 2 * frames, :taps] = rows_in[...]
-    for i, (_, _, count, with_taps) in enumerate(plan):
+    for i, (_, with_taps) in enumerate(plan):
         if with_taps:
-            outs[i][count * rows :, :] = tile[...]
+            outs[i][frames * rows :, :] = tile[...]
     build_group(tile[:, : 2 * LANE], 0, frames, rows, halo, *mats)
     for copy in pending:
         copy.wait()
@@ -334,8 +334,8 @@
     out = pl.pallas_call(
         functools.partial(prepare_kernel, plan, frames, rows, halo, w),
         out_shape=[
-            jax.ShapeDtypeStruct((count * rows + (height if taps else 0), w), f32)
-            for _, _, count, taps in plan
+            jax.ShapeDtypeStruct((frames * rows + (height if taps else 0), w), f32)
+            for _, taps in plan
         ]
         + [jax.ShapeDtypeStruct((height, w), f32)]
         + matrix_shapes(1, frames, rows, halo),
@@ -428,7 +428,7 @@
     )(place, est, *parts)
 
 
-def apply_kernel(frames, rows, halo, w, groups, origin, cut, count, pieces, place, *refs):
+def apply_kernel(frames, rows, halo, w, groups, cut, count, pieces, place, *refs):
     image, refs = refs[:pieces], refs[pieces:]
     t_hbm, b_hbm, bp_hbm, ta_hbm, own = refs[:5]
     moved = refs[5 : 5 + count]
@@ -454,12 +454,18 @@
         for c in copies(g):
             c.start()
         for f in range(frames):
+            span = pl.ds(f * rows, rows)
             if g == 0:
-                source = own.at[f, :, mine]
+                pltpu.make_async_copy(own.at[f, :, mine], wbuf.at[g, f], wsem.at[g, f]).start()
+            elif g < groups - 1:
+                pltpu.make_async_copy(moved[g - 1].at[span, :], wbuf.at[g, f], wsem.at[g, f]).start()
             else:
-                ref, start = origin[g, f]
-                source = moved[ref].at[pl.ds(start, rows), :]
-            pltpu.make_async_copy(source, wbuf.at[g, f], wsem.at[g, f]).start()
+                inside = (place[0] >= groups // 4) & (place[0] < groups - groups // 4)
+                for flag, ref in ((inside, moved[-2]), (jnp.logical_not(inside), moved[-1])):
+
+                    @pl.when(flag)
+                    def _(ref=ref, span=span, g=g, f=f):
+                        pltpu.make_async_copy(ref.at[span, :], wbuf.at[g, f], wsem.at[g, f]).start()
     clear_edges(y_hi, y_lo, qs, ext, rows, w)
     if pieces > 1:
         wide, recv_a, recv_b = image
@@ -491,7 +497,7 @@
     mid[...] = z[cut : ext - cut]
 
 
-def apply_terms(place, image, mats, weights, moved, origin, cut, halo):
+def apply_terms(place, image, mats, weights, moved, cut, halo):
     frames, rows, _ = weights.shape
     w = image[0].shape[1] - 2 * LANE
     ext = rows + 2 * halo
@@ -499,7 +505,7 @@
     groups = ta.shape[0]
     wide = w + LANE
     return pl.pallas_call(
-        functools.partial(apply_kernel, frames, rows, halo, w, groups, origin, cut, len(moved), len(image)),
+        functools.partial(apply_kernel, frames, rows, halo, w, groups, cut, len(moved), len(image)),
         out_shape=[
             jax.ShapeDtypeStruct((cut, wide), f32),
             jax.ShapeDtypeStruct((ext - 2 * cut, wide), f32),
@@ -734,25 +740,21 @@
         jnp.where(odd, low, high), jnp.where(odd, high, low), "strip"
     )
 
-    early = frames // 2
-    plan = [(d, 0, frames, True) for d in range(1, n - 1)]
-    plan += [(n - 1, 0, early, True), (n - 1, early, frames - early, False)]
+    plan = [(d, True) for d in range(1, n - 1)] + [(n - 1, False)]
     packed, tile, own_mats = prepare(plan, place, column_kernels, row_kernels, weights, w, halo)
+    far_tile = swap(tile[:, : 2 * LANE], "frame", n - 1)
     moved = []
-    for i, (d, _, _, taps) in enumerate(plan):
-        moved.append(swap(packed[i], "frame", d))
-    origin = {}
-    starts = [0]
-    for i, (d, lead, count, taps) in enumerate(plan):
-        for k in range(count):
-            origin[d, lead + k] = (i, k * rows)
-        if taps:
-            starts.append(count * rows)
+    for i in range(n - 2):
+        moved.append(swap(packed[i], "frame", i + 1))
+    middle = range(n // 4, n - n // 4)
+    for members in (middle, [i for i in range(n) if i not in middle]):
+        moved.append(lax.ppermute(packed[-1], "frame", [(i, n - 1 - i) for i in members]))
+    starts = [0] + [frames * rows] * (n - 2) + [0]
 
     send_a, mid, send_b = first_terms(
         place, estimate, est_a, est_b, own_mats, weights, observed
     )
-    mats = setup_matrices([tile] + moved[: n - 1], starts, frames, rows, halo)
+    mats = setup_matrices([tile] + moved[: n - 2] + [far_tile], starts, frames, rows, halo)
     recv_a, recv_b = neighbours(send_a, send_b, "strip")
 
     part = list(column_blocks(n, place, send_a, mid, send_b, recv_a, recv_b, w))
@@ -768,19 +770,17 @@
     recv_a, recv_b = neighbours(send_a, send_b, "strip")
 
     send_a, mid, send_b, stat1, k0x = apply_terms(
-        place, (wide, recv_a, recv_b), mats, weights, moved, origin, 2 * halo, halo
+        place, (wide, recv_a, recv_b), mats, weights, moved, 2 * halo, halo
     )
     recv_a, recv_b = neighbours(send_a, send_b, "strip")
     q, col_a, col_b = merge_rows(strips, place, send_a, mid, send_b, recv_a, recv_b, halo)
     recv_a, recv_b = neighbours(col_a, col_b, "frame")
     k1x, k1, k11_part = merge_cols(n, rows, place, q, recv_a, recv_b, k0x, halo)
 
-    send_a, mid, send_b, stat2 = apply_terms(
-        place, (k1x,), mats, weights, moved, origin, halo, halo
-    )
+    send_a, mid, send_b, stat2 = apply_terms(place, (k1x,), mats, weights, moved, halo, halo)
     recv_a, recv_b = neighbours(send_a, send_b, "strip")
     sums = jnp.stack([k00_part, stat1, k11_part, stat2])
-    for axis, size in (("strip", strips), ("frame", n)):
+    for axis, size in (("frame", n), ("strip", strips)):
         d = 1
         while d < size:
             sums = sums + swap(sums, axis, d)
@@ -788,6 +788,12 @@
     k2 = wrap(place, send_a, mid, send_b, recv_a, recv_b, k1, halo)
 
     def gathered(x):
+        parts = [x]
+        for d in range(1, n):
+            parts.append(swap(x, "frame", d))
+        return parts
+
+    def gathered_tree(x):
         parts = [x] + [None] * (n - 1)
         for i in range(n):
             for d in reversed(distances):
@@ -795,7 +801,7 @@
                     parts[i + d] = swap(parts[i], "frame", d)
         return parts
 
-    g0, g1, g2 = gathered(k0), gathered(k1), gathered(k2)
+    g0, g1, g2 = gathered(k0), gathered(k1), gathered_tree(k2)
     result, base, coef = solution_image(place, estimate, sums, g0, g1)
     return result, residual_image(place, base, coef, g2, halo)
 

time: 233 us -> 242 us (1.039)
  waiting for transfers between devices: 103 us -> 110 us
    ppermute x12, starting transfers between devices: 27.5 us -> 16.9 us  [neighbours(): out.append(lax.ppermute(x, axis, pairs + [(b, a) for a, b in pairs]))]
    ppermute x21 -> x20, starting transfers between devices: 30.4 us -> 39.8 us  [swap(): return lax.ppermute(x, axis, [(i, i ^ distance) for i in range(n)])]
    ppermute x21 -> x20, waiting for transfers between devices: 87 us -> 94.2 us  [swap(): return lax.ppermute(x, axis, [(i, i ^ distance) for i in range(n)])]
    ppermute x0 -> x2, starting transfers between devices: none -> 3.31 us  [steps(): lax.ppermute(packed[-1], 'frame', [(i, n - 1 - i) for i in members])]
    unnamed x68 -> x70, local copies, waits for them, and re-layouts: 7.19 us -> 7.29 us
  transfers between devices with their start and end apart: 33 -> 34, of which waited for: 17 -> 13; matrix products, arithmetic and copies ran while one was open for 2% -> 2% of each run, Pallas kernels for 7% -> 7%
where the time goes in v1:
time: 242 us; the launch traced here: 240 us
  waiting for transfers between devices  110 us (45%)
  starting transfers between devices  60 us (25%)
  Pallas kernels  56 us (23%)
  local copies, waits for them, and re-layouts  7.29 us (3%)
  other arithmetic  5.37 us (2%)
    ppermute x20, waiting for transfers between devices, swap(): return lax.ppermute(x, axis, [(i, i ^ distance) for i in range(n)])  94.2 us
    ppermute x20, starting transfers between devices, swap(): return lax.ppermute(x, axis, [(i, i ^ distance) for i in range(n)])  39.8 us
    pallas_call x2, Pallas kernels, apply_terms(): pl.pallas_call(functools.partial(apply_kernel, frames, rows, halo, w, gro...  21.2 us
    ppermute x12, starting transfers between devices, neighbours(): out.append(lax.ppermute(x, axis, pairs + [(b, a) for a, b in pairs]))  16.9 us
    ppermute x12, waiting for transfers between devices, neighbours(): out.append(lax.ppermute(x, axis, pairs + [(b, a) for a, b in pairs]))  16.1 us
    pallas_call x1, Pallas kernels, first_terms(): pl.pallas_call(functools.partial(first_kernel, frames, rows, halo), out_s...  8.2 us
    unnamed x70, local copies, waits for them, and re-layouts  7.29 us
  transfers between devices with their start and end apart: 34, of which 13 were waited for; matrix products, arithmetic and copies ran while one was open for 2% of the time, Pallas kernels for 7%

profile of v1, /device:TPU:2, one launch (start us, length us, event | category | flops | bytes accessed | tf_op | source)
XLA Modules:
  0.0 240.1 jit_solution(14830137343860696768)
XLA Ops:
  0.6 1.1 slice_select_fusion
  1.8 1.9 collective-permute-start.1
  4.3 4.0 %prepare.1 = (f32[264,512]{1,0:T(8,128)}, f32[264,512]{1,0:T(8,128)}, f32[256,512]{1,0:T(8,128)}, f32[8,512]{1,0:T(8,128)}, bf16[2,256,256]{2,1,0:T(8,128)(2,1)}...) custom-call(s32[2]{0:T(128)} %pad_add_fusion.place, f32[2,65]{1,0:T(2,128)} %cols_in.1, ...), custom_call_target="tpu_custom_call" | custom-call | tf_op jit(solution)/shard_map/prepare/pallas_call | solution.py:334
  8.4 1.1 collective-permute-done.1.recv_b
  10.2 8.2 %first_terms.1 = (f32[32,2048]{1,0:T(8,128)}, f32[128,2048]{1,0:T(8,128)}, f32[32,2048]{1,0:T(8,128)}) custom-call(s32[2]{0:T(128)} %pad_add_fusion.place, f32[128,2048]{1,0:T(8,128)} %est.5, f32[32,2048]{1,0:T(8,128)} %copy-done.31, f32[32,2048]{1,0:T(8,128)} %copy-done.32, bf16[2,256,256]{2,1,0:T(8,128)(2,1)} %get-tuple-element.44.t_ref, ...), custom_call_target="tpu_custom_call" | custom-call | flops 8000000000 | bytes 8388608 | tf_op jit(solution)/shard_map/first_terms/pallas_call | solution.py:286
  18.4 3.6 %collective-permute-start.2 = (f32[32,2048]{1,0:T(8,128)}, f32[32,2048]{1,0:T(8,128)S(1)}, u32[]{:S(2)}, u32[]{:S(2)}) collective-permute-start(f32[32,2048]{1,0:T(8,128)} %get-tuple-element.48.send_a), channel_id=1, source_target_pairs={{0,4},{8,12},{16,20},{24,28},{4,0},{12,8},{20,16},{28,24},{1,5},{9... | collective-permute-start | bytes 786440 | tf_op jit(solution)/shard_map/ppermute | solution.py:716
  22.1 1.9 collective-permute-start.3
  24.0 6.7 %collective-permute-done.3.recv_b = f32[32,2048]{1,0:T(8,128)S(1)} collective-permute-done((f32[32,2048]{1,0:T(8,128)}, f32[32,2048]{1,0:T(8,128)S(1)}, u32[]{:S(2)}, u32[]{:S(2)}) %collective-permute-start.3) | collective-permute-done | bytes 262176 | tf_op jit(solution)/shard_map/ppermute | solution.py:716
  31.4 2.8 %column_blocks.1 = (f32[144,512]{1,0:T(8,128)}, f32[144,512]{1,0:T(8,128)}, f32[144,512]{1,0:T(8,128)}, f32[144,512]{1,0:T(8,128)}) custom-call(s32[2]{0:T(128)} %pad_add_fusion.place, f32[32,2048]{1,0:T(8,128)} %get-tuple-element.48.send_a, f32[128,2048]{1,0:T(8,128)} %get-tuple-element.49.mid, f32[32,2048]{1,0:T(8,128)} %get-tuple-element.50.send_b, ...), custom_call_target="tpu_custom_call" | custom-call | tf_op jit(solution)/shard_map/column_blocks/pallas_call | solution.py:373
  34.3 1.0 collective-permute-start.4
  35.2 1.1 collective-permute-start.6
  36.3 2.0 collective-permute-start.10
  38.3 1.6 collective-permute-start.9
  40.5 14.6 %collective-permute-done.4 = f32[144,512]{1,0:T(8,128)S(1)} collective-permute-done((f32[144,512]{1,0:T(8,128)}, f32[144,512]{1,0:T(8,128)S(1)}, u32[]{:S(2)}, u32[]{:S(2)}) %collective-permute-start.4) | collective-permute-done | bytes 294944 | tf_op jit(solution)/shard_map/ppermute | solution.py:722
  55.1 2.6 %collective-permute-start.13 = (f32[256,512]{1,0:T(8,128)}, f32[256,512]{1,0:T(8,128)}, u32[]{:S(2)}, u32[]{:S(2)}) collective-permute-start(f32[256,512]{1,0:T(8,128)} %get-tuple-element.66), channel_id=1, source_target_pairs={{0,3},{3,0},{4,7},{7,4},{8,11},{11,8},{12,15},{15,12},{16,19},{19,... | collective-permute-start | bytes 1572872 | tf_op jit(solution)/shard_map/ppermute | solution.py:751
  57.7 1.0 add.23
  58.7 2.7 %collective-permute-done.6.refs_2_ = f32[144,512]{1,0:T(8,128)S(1)} collective-permute-done((f32[144,512]{1,0:T(8,128)}, f32[144,512]{1,0:T(8,128)S(1)}, u32[]{:S(2)}, u32[]{:S(2)}) %collective-permute-start.6) | collective-permute-done | bytes 294944 | tf_op jit(solution)/shard_map/ppermute | solution.py:722
  61.4 37.6 %collective-permute-done.5.refs_1_ = f32[144,512]{1,0:T(8,128)S(1)} collective-permute-done((f32[144,512]{1,0:T(8,128)S(1)}, f32[144,512]{1,0:T(8,128)S(1)}, u32[]{:S(2)}, u32[]{:S(2)}) %collective-permute-start.5) | collective-permute-done | bytes 294944 | tf_op jit(solution)/shard_map/ppermute | solution.py:722
  99.0 2.4 collective-permute-start.11
  101.4 2.5 %start_image.1 = (f32[128,512]{1,0:T(8,128)}, f32[128,768]{1,0:T(8,128)}, f32[32,768]{1,0:T(8,128)}, f32[32,768]{1,0:T(8,128)}, f32[8,128]{1,0:T(8,128)}) custom-call(s32[2]{0:T(128)} %pad_add_fusion.place, f32[128,2048]{1,0:T(8,128)} %est.5, f32[144,512]{1,0:T(8,128)} %get-tuple-element.51.refs_0_, f32[144,512]{1,0:T(8,128)} %copy-done.7, f32[144,512]{1,0:T(8,128)} %copy-done.6), custom_call_target="tpu_custom_call" | custom-call | tf_op jit(solution)/shard_map/start_image/pallas_call | solution.py:416
  104.5 1.9 collective-permute-start.8
  107.2 4.5 %setup_all.1 = (bf16[8,256,256]{2,1,0:T(8,128)(2,1)}, bf16[8,256,256]{2,1,0:T(8,128)(2,1)}, bf16[8,256,256]{2,1,0:T(8,128)(2,1)}, bf16[4,384,256]{2,1,0:T(8,128)(2,1)}) custom-call(f32[8,512]{1,0:T(8,128)} %get-tuple-element.59.refs_0_, f32[264,512]{1,0:T(8,128)} %copy-done.2, f32[264,512]{1,0:T(8,128)} %copy-done.1, f32[8,256]{1,0:T(8,128)} %copy-done.27), custom_call_target="tpu_custom_call" | custom-call | tf_op jit(solution)/shard_map/setup_all/pallas_call | solution.py:130
  112.6 10.6 %shard_map.68 = (f32[64,640]{1,0:T(8,128)}, f32[64,640]{1,0:T(8,128)}, f32[64,640]{1,0:T(8,128)}, f32[8,128]{1,0:T(8,128)}, f32[192,768]{1,0:T(8,128)}) custom-call(s32[2]{0:T(128)} %pad_add_fusion.place, f32[128,768]{1,0:T(8,128)} %get-tuple-element.56.refs_0_, f32[32,768]{1,0:T(8,128)} %copy-done.33, f32[32,768]{1,0:T(8,128)} %copy-done.34, ...), custom_call_target="tpu_custom_call" | custom-call | flops 12000000000 | bytes 4194304 | tf_op jit(solution)/shard_map/pallas_call | solution.py:507
  123.2 1.0 collective-permute-start.14
  124.1 2.7 %collective-permute-start.15 = (f32[64,640]{1,0:T(8,128)}, f32[64,640]{1,0:T(8,128)S(1)}, u32[]{:S(2)}, u32[]{:S(2)}) collective-permute-start(f32[64,640]{1,0:T(8,128)} %get-tuple-element.70.send_b), channel_id=1, source_target_pairs={{4,8},{12,16},{20,24},{8,4},{16,12},{24,20},{5,9},{13,17},{21,25},... | collective-permute-start | bytes 491528 | tf_op jit(solution)/shard_map/ppermute | solution.py:716
  126.9 4.2 %collective-permute-done.15.recv_b = f32[64,640]{1,0:T(8,128)S(1)} collective-permute-done((f32[64,640]{1,0:T(8,128)}, f32[64,640]{1,0:T(8,128)S(1)}, u32[]{:S(2)}, u32[]{:S(2)}) %collective-permute-start.15) | collective-permute-done | bytes 163872 | tf_op jit(solution)/shard_map/ppermute | solution.py:716
  131.7 2.2 merge_rows.1
  134.8 4.1 %collective-permute-done.16.recv_a = f32[192,128]{1,0:T(8,128)S(1)} collective-permute-done((f32[192,128]{1,0:T(8,128)}, f32[192,128]{1,0:T(8,128)S(1)}, u32[]{:S(2)}, u32[]{:S(2)}) %collective-permute-start.16) | collective-permute-done | bytes 98336 | tf_op jit(solution)/shard_map/ppermute | solution.py:716
  139.5 2.3 merge_cols.1
  141.8 10.6 %shard_map.69 = (f32[32,640]{1,0:T(8,128)}, f32[128,640]{1,0:T(8,128)}, f32[32,640]{1,0:T(8,128)}, f32[8,128]{1,0:T(8,128)}) custom-call(s32[2]{0:T(128)} %pad_add_fusion.place, f32[192,768]{1,0:T(8,128)} %get-tuple-element.76.refs_0_, bf16[8,256,256]{2,1,0:T(8,128)(2,1)} %get-tuple-element.62.refs_3_.refs_1_, ...), custom_call_target="tpu_custom_call" | custom-call | flops 12000000000 | bytes 4194304 | tf_op jit(solution)/shard_map/pallas_call | solution.py:507
  152.4 0.9 collective-permute-start.29
  153.3 2.0 collective-permute-start.30
  156.0 3.8 %collective-permute-start.18 = (f32[4,8,128]{2,1,0:T(8,128)S(1)}, f32[4,8,128]{2,1,0:T(8,128)S(1)}, u32[]{:S(2)}, u32[]{:S(2)}) collective-permute-start(f32[4,8,128]{2,1,0:T(8,128)S(1)} %pad_maximum_fusion), channel_id=1, source_target_pairs={{0,1},{1,0},{2,3},{3,2},{4,5},{5,4},{6,7},{7,6},{8,9},{9,8},{10,11... | collective-permute-start | bytes 49160 | tf_op jit(solution)/shard_map/ppermute | solution.py:722
  160.5 2.1 wrap.1.refs_0_
  162.6 4.6 %collective-permute-start.32 = (f32[144,512]{1,0:T(8,128)}, f32[144,512]{1,0:T(8,128)S(1)}, u32[]{:S(2)}, u32[]{:S(2)}) collective-permute-start(f32[144,512]{1,0:T(8,128)} %wrap.1.refs_0_), channel_id=1, source_target_pairs={{0,2},{1,3},{2,0},{3,1},{4,6},{5,7},{6,4},{7,5},{8,10},{9,11},{10,... | collective-permute-start | bytes 884744 | tf_op jit(solution)/shard_map/ppermute | solution.py:722
  167.8 1.7 collective-permute-start.23
  169.5 1.3 collective-permute-start.24
  170.7 1.5 collective-permute-start.25
  172.3 8.9 %collective-permute-done.19 = f32[4,8,128]{2,1,0:T(8,128)S(1)} collective-permute-done((f32[4,8,128]{2,1,0:T(8,128)S(1)}, f32[4,8,128]{2,1,0:T(8,128)S(1)}, u32[]{:S(2)}, u32[]{:S(2)}) %collective-permute-start.19) | collective-permute-done | bytes 16416 | tf_op jit(solution)/shard_map/ppermute | solution.py:722
  181.9 13.5 %collective-permute-start.20 = (f32[4,8,128]{2,1,0:T(8,128)S(1)}, f32[4,8,128]{2,1,0:T(8,128)S(1)}, u32[]{:S(2)}, u32[]{:S(2)}) collective-permute-start(f32[4,8,128]{2,1,0:T(8,128)S(1)} %fusion.1), channel_id=1, source_target_pairs={{0,4},{4,0},{8,12},{12,8},{16,20},{20,16},{24,28},{28,24},{1,5},{5... | collective-permute-start | bytes 49160 | tf_op jit(solution)/shard_map/ppermute | solution.py:722
  196.3 3.7 %collective-permute-done.21 = f32[4,8,128]{2,1,0:T(8,128)S(1)} collective-permute-done((f32[4,8,128]{2,1,0:T(8,128)S(1)}, f32[4,8,128]{2,1,0:T(8,128)S(1)}, u32[]{:S(2)}, u32[]{:S(2)}) %collective-permute-start.21) | collective-permute-done | bytes 16416 | tf_op jit(solution)/shard_map/ppermute | solution.py:722
  200.0 2.0 collective-permute-start.33
  202.0 1.3 collective-permute-start.22
  203.6 2.3 collective-permute-done.22
  205.8 2.0 collective-permute-start.28
  208.5 23.0 %collective-permute-done.26.refs_5_ = f32[128,512]{1,0:T(8,128)S(1)} collective-permute-done((f32[128,512]{1,0:T(8,128)S(1)}, f32[128,512]{1,0:T(8,128)S(1)}, u32[]{:S(2)}, u32[]{:S(2)}) %collective-permute-start.26) | collective-permute-done | bytes 262176 | tf_op jit(solution)/shard_map/ppermute | solution.py:722
  233.0 3.4 %solution_image.1 = (f32[128,2048]{1,0:T(8,128)}, f32[128,2048]{1,0:T(8,128)}, f32[8,128]{1,0:T(8,128)}) custom-call(s32[2]{0:T(128)} %pad_add_fusion.place, f32[128,2048]{1,0:T(8,128)} %est.5, f32[4,8,128]{2,1,0:T(8,128)} %add.28.sums, f32[128,512]{1,0:T(8,128)} %get-tuple-element.78.refs_0_, f32[128,512]{1,0:T(8,128)} %copy-done.11, ...), custom_call_target="tpu_custom_call" | custom-call | tf_op jit(solution)/shard_map/solution_image/pallas_call | solution.py:668
  237.2 2.9 %residual_image.1 = f32[128,2048]{1,0:T(8,128)} custom-call(s32[2]{0:T(128)} %pad_add_fusion.place, f32[128,2048]{1,0:T(8,128)} %get-tuple-element.81.base, f32[8,128]{1,0:T(8,128)} %get-tuple-element.82.coef, f32[144,512]{1,0:T(8,128)} %wrap.1.refs_0_, f32[144,512]{1,0:T(8,128)} %copy-done.4, f32[144,512]{1,0:T(8,128)} %copy-done.3, f32[144,512]{1,0:T(8,128)} %copy-done.5), custom_call_target="tpu_custom_call" | custom-call | tf_op jit(solution)/shard_map/residual_image/pallas_call | solution.py:701
  (112 shorter events, 13.8 us)
Async XLA Ops:
  1.7 6.6 %collective-permute-start = (f32[32,2048]{1,0:T(8,128)S(1)}, f32[32,2048]{1,0:T(8,128)S(1)}, u32[]{:S(2)}, u32[]{:S(2)}) collective-permute-start(f32[32,2048]{1,0:T(8,128)S(1)} %get-tuple-element.87), channel_id=1, source_target_pairs={{0,4},{8,12},{16,20},{24,28},{4,0},{12,8},{20,16},{28,24},{1,5},{9... | collective-permute-start | bytes 786440 | tf_op jit(solution)/shard_map/ppermute | solution.py:716
  1.8 7.7 %collective-permute-start.1 = (f32[32,2048]{1,0:T(8,128)S(1)}, f32[32,2048]{1,0:T(8,128)S(1)}, u32[]{:S(2)}, u32[]{:S(2)}) collective-permute-start(f32[32,2048]{1,0:T(8,128)S(1)} %get-tuple-element.86), channel_id=1, source_target_pairs={{4,8},{12,16},{20,24},{8,4},{16,12},{24,20},{5,9},{13,17},{21,25},... | collective-permute-start | bytes 786440 | tf_op jit(solution)/shard_map/ppermute | solution.py:716
  18.4 17.9 %copy-start.29 = (f32[264,512]{1,0:T(8,128)S(1)}, f32[264,512]{1,0:T(8,128)}, u32[]{:S(2)}) copy-start(f32[264,512]{1,0:T(8,128)} %get-tuple-element.61) | copy-start | bytes 1622020
  18.4 19.9 %copy-start.28 = (f32[264,512]{1,0:T(8,128)S(1)}, f32[264,512]{1,0:T(8,128)}, u32[]{:S(2)}) copy-start(f32[264,512]{1,0:T(8,128)} %get-tuple-element.60) | copy-start | bytes 1622020
  18.4 43.0 %copy-start.23 = (f32[8,512]{1,0:T(8,128)S(1)}, f32[8,512]{1,0:T(8,128)}, u32[]{:S(2)}) copy-start(f32[8,512]{1,0:T(8,128)} %get-tuple-element.59.refs_0_) | copy-start | bytes 49156
  18.4 5.6 %collective-permute-start.2 = (f32[32,2048]{1,0:T(8,128)}, f32[32,2048]{1,0:T(8,128)S(1)}, u32[]{:S(2)}, u32[]{:S(2)}) collective-permute-start(f32[32,2048]{1,0:T(8,128)} %get-tuple-element.48.send_a), channel_id=1, source_target_pairs={{0,4},{8,12},{16,20},{24,28},{4,0},{12,8},{20,16},{28,24},{1,5},{9... | collective-permute-start | bytes 786440 | tf_op jit(solution)/shard_map/ppermute | solution.py:716
  22.1 8.6 %collective-permute-start.3 = (f32[32,2048]{1,0:T(8,128)}, f32[32,2048]{1,0:T(8,128)S(1)}, u32[]{:S(2)}, u32[]{:S(2)}) collective-permute-start(f32[32,2048]{1,0:T(8,128)} %get-tuple-element.50.send_b), channel_id=1, source_target_pairs={{4,8},{12,16},{20,24},{8,4},{16,12},{24,20},{5,9},{13,17},{21,25},... | collective-permute-start | bytes 786440 | tf_op jit(solution)/shard_map/ppermute | solution.py:716
  24.0 6.7 %copy-start.8 = (f32[32,2048]{1,0:T(8,128)}, f32[32,2048]{1,0:T(8,128)S(1)}, u32[]{:S(2)}) copy-start(f32[32,2048]{1,0:T(8,128)S(1)} %collective-permute-done.2.recv_a) | copy-start | bytes 786436
  34.3 20.8 %collective-permute-start.4 = (f32[144,512]{1,0:T(8,128)}, f32[144,512]{1,0:T(8,128)S(1)}, u32[]{:S(2)}, u32[]{:S(2)}) collective-permute-start(f32[144,512]{1,0:T(8,128)} %get-tuple-element.53), channel_id=1, source_target_pairs={{0,1},{1,0},{2,3},{3,2},{4,5},{5,4},{6,7},{7,6},{8,9},{9,8},{10,11... | collective-permute-start | bytes 884744 | tf_op jit(solution)/shard_map/ppermute | solution.py:722
  35.2 26.2 %collective-permute-start.6 = (f32[144,512]{1,0:T(8,128)}, f32[144,512]{1,0:T(8,128)S(1)}, u32[]{:S(2)}, u32[]{:S(2)}) collective-permute-start(f32[144,512]{1,0:T(8,128)} %get-tuple-element.54), channel_id=1, source_target_pairs={{0,1},{1,0},{2,3},{3,2},{4,5},{5,4},{6,7},{7,6},{8,9},{9,8},{10,11... | collective-permute-start | bytes 884744 | tf_op jit(solution)/shard_map/ppermute | solution.py:722
  36.3 68.2 %collective-permute-start.10 = (f32[264,512]{1,0:T(8,128)S(1)}, f32[264,512]{1,0:T(8,128)S(1)}, u32[]{:S(2)}, u32[]{:S(2)}) collective-permute-start(f32[264,512]{1,0:T(8,128)S(1)} %copy-done.29), channel_id=1, source_target_pairs={{0,2},{1,3},{2,0},{3,1},{4,6},{5,7},{6,4},{7,5},{8,10},{9,11},{10,... | collective-permute-start | bytes 1622024 | tf_op jit(solution)/shard_map/ppermute | solution.py:722
  38.3 68.1 %collective-permute-start.9 = (f32[264,512]{1,0:T(8,128)S(1)}, f32[264,512]{1,0:T(8,128)S(1)}, u32[]{:S(2)}, u32[]{:S(2)}) collective-permute-start(f32[264,512]{1,0:T(8,128)S(1)} %copy-done.28), channel_id=1, source_target_pairs={{0,1},{1,0},{2,3},{3,2},{4,5},{5,4},{6,7},{7,6},{8,9},{9,8},{10,11... | collective-permute-start | bytes 1622024 | tf_op jit(solution)/shard_map/ppermute | solution.py:722
  39.8 71.9 %collective-permute-start.12 = (f32[256,512]{1,0:T(8,128)}, f32[256,512]{1,0:T(8,128)S(1)}, u32[]{:S(2)}, u32[]{:S(2)}) collective-permute-start(f32[256,512]{1,0:T(8,128)} %get-tuple-element.66), channel_id=1, source_target_pairs={{1,2},{2,1},{5,6},{6,5},{9,10},{10,9},{13,14},{14,13},{17,18},{18,... | collective-permute-start | bytes 1572872 | tf_op jit(solution)/shard_map/ppermute | solution.py:751
  55.1 56.6 %collective-permute-start.13 = (f32[256,512]{1,0:T(8,128)}, f32[256,512]{1,0:T(8,128)}, u32[]{:S(2)}, u32[]{:S(2)}) collective-permute-start(f32[256,512]{1,0:T(8,128)} %get-tuple-element.66), channel_id=1, source_target_pairs={{0,3},{3,0},{4,7},{7,4},{8,11},{11,8},{12,15},{15,12},{16,19},{19,... | collective-permute-start | bytes 1572872 | tf_op jit(solution)/shard_map/ppermute | solution.py:751
  61.4 40.0 %copy-start.6 = (f32[144,512]{1,0:T(8,128)}, f32[144,512]{1,0:T(8,128)S(1)}, u32[]{:S(2)}) copy-start(f32[144,512]{1,0:T(8,128)S(1)} %collective-permute-done.6.refs_2_) | copy-start | bytes 884740
  61.4 37.6 %collective-permute-start.5 = (f32[144,512]{1,0:T(8,128)S(1)}, f32[144,512]{1,0:T(8,128)S(1)}, u32[]{:S(2)}, u32[]{:S(2)}) collective-permute-start(f32[144,512]{1,0:T(8,128)S(1)} %add.23), channel_id=1, source_target_pairs={{0,2},{1,3},{2,0},{3,1},{4,6},{5,7},{6,4},{7,5},{8,10},{9,11},{10,... | collective-permute-start | bytes 884744 | tf_op jit(solution)/shard_map/ppermute | solution.py:722
  99.0 5.4 %collective-permute-start.11 = (f32[8,256]{1,0:T(8,128)S(1)}, f32[8,256]{1,0:T(8,128)S(1)}, u32[]{:S(2)}, u32[]{:S(2)}) collective-permute-start(f32[8,256]{1,0:T(8,128)S(1)} %slice.11), channel_id=1, source_target_pairs={{0,3},{1,2},{2,1},{3,0},{4,7},{5,6},{6,5},{7,4},{8,11},{9,10},{10,... | collective-permute-start | bytes 24584 | tf_op jit(solution)/shard_map/ppermute | solution.py:722
  104.4 7.3 %collective-permute-start.7 = (f32[32,768]{1,0:T(8,128)}, f32[32,768]{1,0:T(8,128)S(1)}, u32[]{:S(2)}, u32[]{:S(2)}) collective-permute-start(f32[32,768]{1,0:T(8,128)} %get-tuple-element.57), channel_id=1, source_target_pairs={{0,4},{8,12},{16,20},{24,28},{4,0},{12,8},{20,16},{28,24},{1,5},{9... | collective-permute-start | bytes 294920 | tf_op jit(solution)/shard_map/ppermute | solution.py:716
  104.5 7.3 %collective-permute-start.8 = (f32[32,768]{1,0:T(8,128)}, f32[32,768]{1,0:T(8,128)S(1)}, u32[]{:S(2)}, u32[]{:S(2)}) collective-permute-start(f32[32,768]{1,0:T(8,128)} %get-tuple-element.58), channel_id=1, source_target_pairs={{4,8},{12,16},{20,24},{8,4},{16,12},{24,20},{5,9},{13,17},{21,25},... | collective-permute-start | bytes 294920 | tf_op jit(solution)/shard_map/ppermute | solution.py:716
  123.2 3.7 %collective-permute-start.14 = (f32[64,640]{1,0:T(8,128)}, f32[64,640]{1,0:T(8,128)S(1)}, u32[]{:S(2)}, u32[]{:S(2)}) collective-permute-start(f32[64,640]{1,0:T(8,128)} %get-tuple-element.68.send_a), channel_id=1, source_target_pairs={{0,4},{8,12},{16,20},{24,28},{4,0},{12,8},{20,16},{28,24},{1,5},{9... | collective-permute-start | bytes 491528 | tf_op jit(solution)/shard_map/ppermute | solution.py:716
  124.1 6.9 %collective-permute-start.15 = (f32[64,640]{1,0:T(8,128)}, f32[64,640]{1,0:T(8,128)S(1)}, u32[]{:S(2)}, u32[]{:S(2)}) collective-permute-start(f32[64,640]{1,0:T(8,128)} %get-tuple-element.70.send_b), channel_id=1, source_target_pairs={{4,8},{12,16},{20,24},{8,4},{16,12},{24,20},{5,9},{13,17},{21,25},... | collective-permute-start | bytes 491528 | tf_op jit(solution)/shard_map/ppermute | solution.py:716
  134.0 4.9 %collective-permute-start.16 = (f32[192,128]{1,0:T(8,128)}, f32[192,128]{1,0:T(8,128)S(1)}, u32[]{:S(2)}, u32[]{:S(2)}) collective-permute-start(f32[192,128]{1,0:T(8,128)} %get-tuple-element.72), channel_id=1, source_target_pairs={{0,1},{2,3},{1,0},{3,2},{4,5},{6,7},{5,4},{7,6},{8,9},{10,11},{9,8... | collective-permute-start | bytes 294920 | tf_op jit(solution)/shard_map/ppermute | solution.py:716
  134.0 4.9 %collective-permute-start.17 = (f32[192,128]{1,0:T(8,128)}, f32[192,128]{1,0:T(8,128)S(1)}, u32[]{:S(2)}, u32[]{:S(2)}) collective-permute-start(f32[192,128]{1,0:T(8,128)} %get-tuple-element.73), channel_id=1, source_target_pairs={{1,2},{2,1},{5,6},{6,5},{9,10},{10,9},{13,14},{14,13},{17,18},{18,... | collective-permute-start | bytes 294920 | tf_op jit(solution)/shard_map/ppermute | solution.py:716
  141.8 13.5 %copy-start.24 = (f32[8,128]{1,0:T(8,128)S(1)}, f32[8,128]{1,0:T(8,128)}, u32[]{:S(2)}) copy-start(f32[8,128]{1,0:T(8,128)} %get-tuple-element.55) | copy-start | bytes 12292
  141.8 13.5 %copy-start.25 = (f32[8,128]{1,0:T(8,128)S(1)}, f32[8,128]{1,0:T(8,128)}, u32[]{:S(2)}) copy-start(f32[8,128]{1,0:T(8,128)} %get-tuple-element.67) | copy-start | bytes 12292
  141.8 13.5 %copy-start.26 = (f32[8,128]{1,0:T(8,128)S(1)}, f32[8,128]{1,0:T(8,128)}, u32[]{:S(2)}) copy-start(f32[8,128]{1,0:T(8,128)} %get-tuple-element.75) | copy-start | bytes 12292
  141.8 26.0 %copy-start.10 = (f32[128,512]{1,0:T(8,128)S(1)}, f32[128,512]{1,0:T(8,128)}, u32[]{:S(2)}) copy-start(f32[128,512]{1,0:T(8,128)} %get-tuple-element.78.refs_0_) | copy-start | bytes 786436
  141.8 61.6 %copy-start = (f32[128,512]{1,0:T(8,128)S(1)}, f32[128,512]{1,0:T(8,128)}, u32[]{:S(2)}) copy-start(f32[128,512]{1,0:T(8,128)} %get-tuple-element.79.refs_4_.before) | copy-start | bytes 786436
  152.4 7.4 %collective-permute-start.29 = (f32[32,640]{1,0:T(8,128)}, f32[32,640]{1,0:T(8,128)S(1)}, u32[]{:S(2)}, u32[]{:S(2)}) collective-permute-start(f32[32,640]{1,0:T(8,128)} %get-tuple-element.83.send_a), channel_id=1, source_target_pairs={{0,4},{8,12},{16,20},{24,28},{4,0},{12,8},{20,16},{28,24},{1,5},{9... | collective-permute-start | bytes 245768 | tf_op jit(solution)/shard_map/ppermute | solution.py:716
  153.3 6.5 %collective-permute-start.30 = (f32[32,640]{1,0:T(8,128)}, f32[32,640]{1,0:T(8,128)S(1)}, u32[]{:S(2)}, u32[]{:S(2)}) collective-permute-start(f32[32,640]{1,0:T(8,128)} %get-tuple-element.85.send_b), channel_id=1, source_target_pairs={{4,8},{12,16},{20,24},{8,4},{16,12},{24,20},{5,9},{13,17},{21,25},... | collective-permute-start | bytes 245768 | tf_op jit(solution)/shard_map/ppermute | solution.py:716
  156.0 11.1 %collective-permute-start.18 = (f32[4,8,128]{2,1,0:T(8,128)S(1)}, f32[4,8,128]{2,1,0:T(8,128)S(1)}, u32[]{:S(2)}, u32[]{:S(2)}) collective-permute-start(f32[4,8,128]{2,1,0:T(8,128)S(1)} %pad_maximum_fusion), channel_id=1, source_target_pairs={{0,1},{1,0},{2,3},{3,2},{4,5},{5,4},{6,7},{7,6},{8,9},{9,8},{10,11... | collective-permute-start | bytes 49160 | tf_op jit(solution)/shard_map/ppermute | solution.py:722
  162.6 37.4 %collective-permute-start.32 = (f32[144,512]{1,0:T(8,128)}, f32[144,512]{1,0:T(8,128)S(1)}, u32[]{:S(2)}, u32[]{:S(2)}) collective-permute-start(f32[144,512]{1,0:T(8,128)} %wrap.1.refs_0_), channel_id=1, source_target_pairs={{0,2},{1,3},{2,0},{3,1},{4,6},{5,7},{6,4},{7,5},{8,10},{9,11},{10,... | collective-permute-start | bytes 884744 | tf_op jit(solution)/shard_map/ppermute | solution.py:722
  167.8 13.4 %collective-permute-start.19 = (f32[4,8,128]{2,1,0:T(8,128)S(1)}, f32[4,8,128]{2,1,0:T(8,128)S(1)}, u32[]{:S(2)}, u32[]{:S(2)}) collective-permute-start(f32[4,8,128]{2,1,0:T(8,128)S(1)} %fusion), channel_id=1, source_target_pairs={{0,2},{1,3},{2,0},{3,1},{4,6},{5,7},{6,4},{7,5},{8,10},{9,11},{10,... | collective-permute-start | bytes 49160 | tf_op jit(solution)/shard_map/ppermute | solution.py:722
  167.8 34.2 %collective-permute-start.23 = (f32[128,512]{1,0:T(8,128)S(1)}, f32[128,512]{1,0:T(8,128)S(1)}, u32[]{:S(2)}, u32[]{:S(2)}) collective-permute-start(f32[128,512]{1,0:T(8,128)S(1)} %copy-done.10), channel_id=1, source_target_pairs={{0,1},{1,0},{2,3},{3,2},{4,5},{5,4},{6,7},{7,6},{8,9},{9,8},{10,11... | collective-permute-start | bytes 786440 | tf_op jit(solution)/shard_map/ppermute | solution.py:722
  169.5 33.9 %collective-permute-start.24 = (f32[128,512]{1,0:T(8,128)S(1)}, f32[128,512]{1,0:T(8,128)S(1)}, u32[]{:S(2)}, u32[]{:S(2)}) collective-permute-start(f32[128,512]{1,0:T(8,128)S(1)} %copy-done.10), channel_id=1, source_target_pairs={{0,2},{1,3},{2,0},{3,1},{4,6},{5,7},{6,4},{7,5},{8,10},{9,11},{10,... | collective-permute-start | bytes 786440 | tf_op jit(solution)/shard_map/ppermute | solution.py:722
  170.7 32.8 %collective-permute-start.25 = (f32[128,512]{1,0:T(8,128)S(1)}, f32[128,512]{1,0:T(8,128)S(1)}, u32[]{:S(2)}, u32[]{:S(2)}) collective-permute-start(f32[128,512]{1,0:T(8,128)S(1)} %copy-done.10), channel_id=1, source_target_pairs={{0,3},{1,2},{2,1},{3,0},{4,7},{5,6},{6,5},{7,4},{8,11},{9,10},{10,... | collective-permute-start | bytes 786440 | tf_op jit(solution)/shard_map/ppermute | solution.py:722
  181.9 14.4 %collective-permute-start.20 = (f32[4,8,128]{2,1,0:T(8,128)S(1)}, f32[4,8,128]{2,1,0:T(8,128)S(1)}, u32[]{:S(2)}, u32[]{:S(2)}) collective-permute-start(f32[4,8,128]{2,1,0:T(8,128)S(1)} %fusion.1), channel_id=1, source_target_pairs={{0,4},{4,0},{8,12},{12,8},{16,20},{20,16},{24,28},{28,24},{1,5},{5... | collective-permute-start | bytes 49160 | tf_op jit(solution)/shard_map/ppermute | solution.py:722
  196.3 3.7 %collective-permute-start.21 = (f32[4,8,128]{2,1,0:T(8,128)S(1)}, f32[4,8,128]{2,1,0:T(8,128)S(1)}, u32[]{:S(2)}, u32[]{:S(2)}) collective-permute-start(f32[4,8,128]{2,1,0:T(8,128)S(1)} %add.26), channel_id=1, source_target_pairs={{0,8},{4,12},{8,0},{12,4},{16,24},{20,28},{24,16},{28,20},{1,9},{5... | collective-permute-start | bytes 49160 | tf_op jit(solution)/shard_map/ppermute | solution.py:722
  200.0 36.4 %collective-permute-start.31 = (f32[144,512]{1,0:T(8,128)}, f32[144,512]{1,0:T(8,128)S(1)}, u32[]{:S(2)}, u32[]{:S(2)}) collective-permute-start(f32[144,512]{1,0:T(8,128)} %wrap.1.refs_0_), channel_id=1, source_target_pairs={{0,1},{1,0},{2,3},{3,2},{4,5},{5,4},{6,7},{7,6},{8,9},{9,8},{10,11... | collective-permute-start | bytes 884744 | tf_op jit(solution)/shard_map/ppermute | solution.py:722
  200.0 36.4 %copy-start.3 = (f32[144,512]{1,0:T(8,128)}, f32[144,512]{1,0:T(8,128)S(1)}, u32[]{:S(2)}) copy-start(f32[144,512]{1,0:T(8,128)S(1)} %collective-permute-done.32.refs_2_) | copy-start | bytes 884740
  200.0 36.4 %collective-permute-start.33 = (f32[144,512]{1,0:T(8,128)S(1)}, f32[144,512]{1,0:T(8,128)S(1)}, u32[]{:S(2)}, u32[]{:S(2)}) collective-permute-start(f32[144,512]{1,0:T(8,128)S(1)} %collective-permute-done.32.refs_2_), channel_id=1, source_target_pairs={{0,1},{1,0},{2,3},{3,2},{4,5},{5,4},{6,7},{7,6},{8,9},{9,8},{10,11... | collective-permute-start | bytes 884744 | tf_op jit(solution)/shard_map/ppermute | solution.py:722
  202.0 29.5 %copy-start.11 = (f32[128,512]{1,0:T(8,128)}, f32[128,512]{1,0:T(8,128)S(1)}, u32[]{:S(2)}) copy-start(f32[128,512]{1,0:T(8,128)S(1)} %collective-permute-done.23.refs_1_) | copy-start | bytes 786436
  202.0 3.8 %collective-permute-start.22 = (f32[4,8,128]{2,1,0:T(8,128)S(1)}, f32[4,8,128]{2,1,0:T(8,128)S(1)}, u32[]{:S(2)}, u32[]{:S(2)}) collective-permute-start(f32[4,8,128]{2,1,0:T(8,128)S(1)} %add.27), channel_id=1, source_target_pairs={{0,16},{4,20},{8,24},{12,28},{16,0},{20,4},{24,8},{28,12},{1,17},{... | collective-permute-start | bytes 49160 | tf_op jit(solution)/shard_map/ppermute | solution.py:722
  203.4 28.1 %copy-start.12 = (f32[128,512]{1,0:T(8,128)}, f32[128,512]{1,0:T(8,128)S(1)}, u32[]{:S(2)}) copy-start(f32[128,512]{1,0:T(8,128)S(1)} %collective-permute-done.24.refs_2_) | copy-start | bytes 786436
  203.4 28.1 %collective-permute-start.26 = (f32[128,512]{1,0:T(8,128)S(1)}, f32[128,512]{1,0:T(8,128)S(1)}, u32[]{:S(2)}, u32[]{:S(2)}) collective-permute-start(f32[128,512]{1,0:T(8,128)S(1)} %copy-done), channel_id=1, source_target_pairs={{0,1},{1,0},{2,3},{3,2},{4,5},{5,4},{6,7},{7,6},{8,9},{9,8},{10,11... | collective-permute-start | bytes 786440 | tf_op jit(solution)/shard_map/ppermute | solution.py:722
  203.5 28.0 %copy-start.13 = (f32[128,512]{1,0:T(8,128)}, f32[128,512]{1,0:T(8,128)S(1)}, u32[]{:S(2)}) copy-start(f32[128,512]{1,0:T(8,128)S(1)} %collective-permute-done.25.refs_3_) | copy-start | bytes 786436
  203.5 28.0 %collective-permute-start.27 = (f32[128,512]{1,0:T(8,128)S(1)}, f32[128,512]{1,0:T(8,128)S(1)}, u32[]{:S(2)}, u32[]{:S(2)}) collective-permute-start(f32[128,512]{1,0:T(8,128)S(1)} %copy-done), channel_id=1, source_target_pairs={{0,2},{1,3},{2,0},{3,1},{4,6},{5,7},{6,4},{7,5},{8,10},{9,11},{10,... | collective-permute-start | bytes 786440 | tf_op jit(solution)/shard_map/ppermute | solution.py:722
  205.8 25.6 %collective-permute-start.28 = (f32[128,512]{1,0:T(8,128)S(1)}, f32[128,512]{1,0:T(8,128)S(1)}, u32[]{:S(2)}, u32[]{:S(2)}) collective-permute-start(f32[128,512]{1,0:T(8,128)S(1)} %copy-done), channel_id=1, source_target_pairs={{0,3},{1,2},{2,1},{3,0},{4,7},{5,6},{6,5},{7,4},{8,11},{9,10},{10,... | collective-permute-start | bytes 786440 | tf_op jit(solution)/shard_map/ppermute | solution.py:722
  (21 other events, 23.2 us)

commit v2 on v1

--- a/solution.py
+++ b/solution.py
@@ -15,6 +15,10 @@
 VMEM = pl.BlockSpec(memory_space=pltpu.VMEM)
 ANY = pl.BlockSpec(memory_space=pl.ANY)
 SMEM = pl.BlockSpec(memory_space=pltpu.SMEM)
+
+
+def room(mib):
+    return pltpu.CompilerParams(vmem_limit_bytes=mib * 2**20)
 
 
 def split(x):
@@ -136,6 +140,7 @@
             pltpu.VMEM((groups, tile_height(frames), 2 * LANE), f32),
             pltpu.SemaphoreType.DMA((groups,)),
         ],
+        compiler_params=room(24),
         name="setup_all",
     )(*tiles_in)
 
@@ -299,6 +304,7 @@
             pltpu.SemaphoreType.DMA((2, frames)),
         ],
         cost_estimate=pl.CostEstimate(flops=8 * 10**9, bytes_accessed=8 * 2**20, transcendentals=0),
+        compiler_params=room(36),
         name="first_terms",
     )(place, est, recv_a, recv_b, *mats, weights, observed)
 
@@ -342,6 +348,7 @@
         in_specs=[SMEM, VMEM, VMEM, ANY],
         out_specs=[VMEM] * (len(plan) + 5),
         scratch_shapes=[pltpu.SemaphoreType.DMA((len(plan), frames))],
+        compiler_params=room(24),
         name="prepare",
     )(place, column_kernels, row_kernels, weights)
     return out[: len(plan)], out[len(plan)], out[len(plan) + 1 :]
@@ -376,6 +383,7 @@
         in_specs=[SMEM] + [VMEM] * 5,
         out_specs=[VMEM] * n,
         scratch_shapes=[pltpu.VMEM((rows, cols + 2 * LANE), f32)],
+        compiler_params=room(16),
         name="column_blocks",
     )(place, send_a, mid, send_b, recv_a, recv_b)
 
@@ -424,6 +432,7 @@
         ],
         in_specs=[SMEM] + [VMEM] * (1 + len(parts)),
         out_specs=[VMEM] * 5,
+        compiler_params=room(12),
         name="start_image",
     )(place, est, *parts)
 
@@ -528,6 +537,7 @@
         cost_estimate=pl.CostEstimate(
             flops=groups * 3 * 10**9, bytes_accessed=groups * 2**20, transcendentals=0
         ),
+        compiler_params=room(28),
     )(place, *image, t, b, bp, ta, weights, *moved)
 
 
@@ -563,6 +573,7 @@
         ],
         in_specs=[SMEM] + [VMEM] * 5,
         out_specs=[VMEM] * 3,
+        compiler_params=room(8),
         name="merge_rows",
     )(place, send_a, mid, send_b, recv_a, recv_b)
 
@@ -605,6 +616,7 @@
         ],
         in_specs=[SMEM] + [VMEM] * 4,
         out_specs=[VMEM] * 3,
+        compiler_params=room(10),
         name="merge_cols",
     )(place, q, recv_a, recv_b, before)
 
@@ -633,6 +645,7 @@
         out_shape=jax.ShapeDtypeStruct((height, w), f32),
         in_specs=[SMEM] + [VMEM] * 6,
         out_specs=VMEM,
+        compiler_params=room(8),
         name="wrap",
     )(place, send_a, mid, send_b, recv_a, recv_b, before)
 
@@ -671,6 +684,7 @@
         + [jax.ShapeDtypeStruct((8, LANE), f32)],
         in_specs=[SMEM] + [VMEM] * (2 + 2 * n),
         out_specs=[VMEM] * 3,
+        compiler_params=room(20),
         name="solution_image",
     )(place, est, sums, *k0, *k1)
 
@@ -704,6 +718,7 @@
         in_specs=[SMEM] + [VMEM] * (2 + n),
         out_specs=VMEM,
         scratch_shapes=[pltpu.VMEM((rows, cols + 2 * LANE), f32)],
+        compiler_params=room(16),
         name="residual_image",
     )(place, base, coef, *k2)
 

time: 242 us -> 220 us (0.909)
  Pallas kernels: 56 us -> 35.5 us
  waiting for transfers between devices: 110 us -> 116 us
  other arithmetic: 5.37 us -> 1.3 us
  local copies, waits for them, and re-layouts: 7.29 us -> 4.55 us
    ppermute x12, waiting for transfers between devices: 16.1 us -> 19.7 us  [neighbours(): out.append(lax.ppermute(x, axis, pairs + [(b, a) for a, b in pairs]))]
    pallas_call x1, Pallas kernels: 4 us -> 1.24 us  [prepare(): pl.pallas_call(functools.partial(prepare_kernel, plan, frames, rows, halo...]
    unnamed x70 -> x12, local copies, waits for them, and re-layouts: 7.29 us -> 4.55 us
    pallas_call x1, Pallas kernels: 8.2 us -> 5.73 us  [first_terms(): pl.pallas_call(functools.partial(first_kernel, frames, rows, halo), out_s...]
  transfers between devices with their start and end apart: 34 -> 34, of which waited for: 13 -> 15; matrix products, arithmetic and copies ran while one was open for 2% -> 0% of each run, Pallas kernels for 7% -> 3%
where the time goes in v2:
time: 220 us; the launch traced here: 218 us
  waiting for transfers between devices  116 us (53%)
  starting transfers between devices  60 us (27%)
  Pallas kernels  35.5 us (16%)
  local copies, waits for them, and re-layouts  4.55 us (2%)
    ppermute x20, waiting for transfers between devices, swap(): return lax.ppermute(x, axis, [(i, i ^ distance) for i in range(n)])  96.6 us
    ppermute x20, starting transfers between devices, swap(): return lax.ppermute(x, axis, [(i, i ^ distance) for i in range(n)])  41.2 us
    ppermute x12, waiting for transfers between devices, neighbours(): out.append(lax.ppermute(x, axis, pairs + [(b, a) for a, b in pairs]))  19.7 us
    pallas_call x2, Pallas kernels, apply_terms(): pl.pallas_call(functools.partial(apply_kernel, frames, rows, halo, w, gro...  18.9 us
    ppermute x12, starting transfers between devices, neighbours(): out.append(lax.ppermute(x, axis, pairs + [(b, a) for a, b in pairs]))  15.6 us
    pallas_call x1, Pallas kernels, first_terms(): pl.pallas_call(functools.partial(first_kernel, frames, rows, halo), out_s...  5.73 us
    unnamed x12, local copies, waits for them, and re-layouts  4.55 us
  transfers between devices with their start and end apart: 34, of which 15 were waited for; matrix products, arithmetic and copies ran while one was open for 0% of the time, Pallas kernels for 3%

profile of v2, /device:TPU:2, one launch (start us, length us, event | category | flops | bytes accessed | tf_op | source)
XLA Modules:
  0.0 218.5 jit_solution(13532964446532062260)
XLA Ops:
  0.7 1.2 slice_select_fusion
  1.9 1.9 collective-permute-start.1
  3.9 1.6 copy-done.1
  6.9 1.2 prepare.1
  8.1 1.5 collective-permute-done.1.recv_b
  9.6 1.6 copy-done.5
  11.2 5.7 %first_terms.1 = (f32[32,2048]{1,0:T(8,128)S(1)}, f32[128,2048]{1,0:T(8,128)S(1)}, f32[32,2048]{1,0:T(8,128)S(1)}) custom-call(s32[2]{0:T(128)S(1)} %pad_add_fusion.place, f32[128,2048]{1,0:T(8,128)S(1)} %copy-done, f32[32,2048]{1,0:T(8,128)S(1)} %collective-permute-done.recv_a, f32[32,2048]{1,0:T(8,128)S(1)} %collective-permute-done.1.recv_b, ...), custom_call_target="tpu_custom_call" | custom-call | flops 8000000000 | bytes 8388608 | tf_op jit(solution)/shard_map/first_terms/pallas_call | solution.py:291
  16.9 3.6 %collective-permute-start.2 = (f32[32,2048]{1,0:T(8,128)S(1)}, f32[32,2048]{1,0:T(8,128)S(1)}, u32[]{:S(2)}, u32[]{:S(2)}) collective-permute-start(f32[32,2048]{1,0:T(8,128)S(1)} %get-tuple-element.48.send_a), channel_id=1, source_target_pairs={{0,4},{8,12},{16,20},{24,28},{4,0},{12,8},{20,16},{28,24},{1,5},{9... | collective-permute-start | bytes 786440 | tf_op jit(solution)/shard_map/ppermute | solution.py:731
  20.6 1.9 collective-permute-start.3
  22.5 6.5 %collective-permute-done.3.recv_b = f32[32,2048]{1,0:T(8,128)S(1)} collective-permute-done((f32[32,2048]{1,0:T(8,128)S(1)}, f32[32,2048]{1,0:T(8,128)S(1)}, u32[]{:S(2)}, u32[]{:S(2)}) %collective-permute-start.3) | collective-permute-done | bytes 262176 | tf_op jit(solution)/shard_map/ppermute | solution.py:731
  29.0 0.9 column_blocks.1
  29.9 1.0 collective-permute-start.4
  31.0 1.1 collective-permute-start.6
  32.0 2.0 collective-permute-start.10
  34.0 1.6 collective-permute-start.9
  36.3 14.3 %collective-permute-done.4 = f32[144,512]{1,0:T(8,128)S(1)} collective-permute-done((f32[144,512]{1,0:T(8,128)S(1)}, f32[144,512]{1,0:T(8,128)S(1)}, u32[]{:S(2)}, u32[]{:S(2)}) %collective-permute-start.4) | collective-permute-done | bytes 294944 | tf_op jit(solution)/shard_map/ppermute | solution.py:737
  50.6 2.5 %collective-permute-start.13 = (f32[256,512]{1,0:T(8,128)S(1)}, f32[256,512]{1,0:T(8,128)S(1)}, u32[]{:S(2)}, u32[]{:S(2)}) collective-permute-start(f32[256,512]{1,0:T(8,128)S(1)} %get-tuple-element.66), channel_id=1, source_target_pairs={{0,3},{3,0},{4,7},{7,4},{8,11},{11,8},{12,15},{15,12},{16,19},{19,... | collective-permute-start | bytes 1572872 | tf_op jit(solution)/shard_map/ppermute | solution.py:766
  53.1 3.8 %collective-permute-done.6.refs_2_ = f32[144,512]{1,0:T(8,128)S(1)} collective-permute-done((f32[144,512]{1,0:T(8,128)S(1)}, f32[144,512]{1,0:T(8,128)S(1)}, u32[]{:S(2)}, u32[]{:S(2)}) %collective-permute-start.6) | collective-permute-done | bytes 294944 | tf_op jit(solution)/shard_map/ppermute | solution.py:737
  56.9 37.9 %collective-permute-done.5.refs_1_ = f32[144,512]{1,0:T(8,128)S(1)} collective-permute-done((f32[144,512]{1,0:T(8,128)S(1)}, f32[144,512]{1,0:T(8,128)S(1)}, u32[]{:S(2)}, u32[]{:S(2)}) %collective-permute-start.5) | collective-permute-done | bytes 294944 | tf_op jit(solution)/shard_map/ppermute | solution.py:737
  94.8 2.4 %collective-permute-start.11 = (f32[8,256]{1,0:T(8,128)S(1)}, f32[8,256]{1,0:T(8,128)S(1)}, u32[]{:S(2)}, u32[]{:S(2)}) collective-permute-start(f32[8,256]{1,0:T(8,128)S(1)} %slice.11), channel_id=1, source_target_pairs={{0,3},{1,2},{2,1},{3,0},{4,7},{5,6},{6,5},{7,4},{8,11},{9,10},{10,... | collective-permute-start | bytes 24584 | tf_op jit(solution)/shard_map/ppermute | solution.py:737
  97.2 0.7 start_image.1
  97.9 2.4 %collective-permute-done.11.refs_3_ = f32[8,256]{1,0:T(8,128)S(1)} collective-permute-done((f32[8,256]{1,0:T(8,128)S(1)}, f32[8,256]{1,0:T(8,128)S(1)}, u32[]{:S(2)}, u32[]{:S(2)}) %collective-permute-start.11) | collective-permute-done | bytes 8224 | tf_op jit(solution)/shard_map/ppermute | solution.py:737
  100.3 1.9 collective-permute-start.8
  102.2 2.1 setup_all.1
  104.3 1.9 collective-permute-done.8.refs_2_
  106.2 9.4 %shard_map.68 = (f32[64,640]{1,0:T(8,128)S(1)}, f32[64,640]{1,0:T(8,128)S(1)}, f32[64,640]{1,0:T(8,128)S(1)}, f32[8,128]{1,0:T(8,128)S(1)}, f32[192,768]{1,0:T(8,128)S(1)}) custom-call(s32[2]{0:T(128)S(1)} %pad_add_fusion.place, f32[128,768]{1,0:T(8,128)S(1)} %get-tuple-element.56.refs_0_, f32[32,768]{1,0:T(8,128)S(1)} %collective-permute-done.7.refs_1_, ...), custom_call_target="tpu_custom_call" | custom-call | flops 12000000000 | bytes 4194304 | tf_op jit(solution)/shard_map/pallas_call | solution.py:516
  115.5 1.5 collective-permute-start.14
  117.0 1.9 collective-permute-start.15
  119.0 4.7 %collective-permute-done.15.recv_b = f32[64,640]{1,0:T(8,128)S(1)} collective-permute-done((f32[64,640]{1,0:T(8,128)S(1)}, f32[64,640]{1,0:T(8,128)S(1)}, u32[]{:S(2)}, u32[]{:S(2)}) %collective-permute-start.15) | collective-permute-done | bytes 163872 | tf_op jit(solution)/shard_map/ppermute | solution.py:731
  125.1 4.9 %collective-permute-done.16.recv_a = f32[192,128]{1,0:T(8,128)S(1)} collective-permute-done((f32[192,128]{1,0:T(8,128)S(1)}, f32[192,128]{1,0:T(8,128)S(1)}, u32[]{:S(2)}, u32[]{:S(2)}) %collective-permute-start.16) | collective-permute-done | bytes 98336 | tf_op jit(solution)/shard_map/ppermute | solution.py:731
  130.7 9.5 %shard_map.69 = (f32[32,640]{1,0:T(8,128)S(1)}, f32[128,640]{1,0:T(8,128)S(1)}, f32[32,640]{1,0:T(8,128)S(1)}, f32[8,128]{1,0:T(8,128)S(1)}) custom-call(s32[2]{0:T(128)S(1)} %pad_add_fusion.place, f32[192,768]{1,0:T(8,128)S(1)} %get-tuple-element.76.refs_0_, bf16[8,256,256]{2,1,0:T(8,128)(2,1)S(1)} %get-tuple-element.62.refs_3_.refs_1_, ...), custom_call_target="tpu_custom_call" | custom-call | flops 12000000000 | bytes 4194304 | tf_op jit(solution)/shard_map/pallas_call | solution.py:516
  140.4 1.9 collective-permute-start.30
  142.3 3.6 %collective-permute-start.18 = (f32[4,8,128]{2,1,0:T(8,128)S(1)}, f32[4,8,128]{2,1,0:T(8,128)S(1)}, u32[]{:S(2)}, u32[]{:S(2)}) collective-permute-start(f32[4,8,128]{2,1,0:T(8,128)S(1)} %pad_maximum_fusion), channel_id=1, source_target_pairs={{0,1},{1,0},{2,3},{3,2},{4,5},{5,4},{6,7},{7,6},{8,9},{9,8},{10,11... | collective-permute-start | bytes 49160 | tf_op jit(solution)/shard_map/ppermute | solution.py:737
  146.8 4.7 %collective-permute-start.32 = (f32[144,512]{1,0:T(8,128)S(1)}, f32[144,512]{1,0:T(8,128)S(1)}, u32[]{:S(2)}, u32[]{:S(2)}) collective-permute-start(f32[144,512]{1,0:T(8,128)S(1)} %wrap.1.refs_0_), channel_id=1, source_target_pairs={{0,2},{1,3},{2,0},{3,1},{4,6},{5,7},{6,4},{7,5},{8,10},{9,11},{10,... | collective-permute-start | bytes 884744 | tf_op jit(solution)/shard_map/ppermute | solution.py:737
  151.6 1.8 collective-permute-start.23
  153.4 1.1 collective-permute-start.24
  154.5 1.5 collective-permute-start.25
  156.0 9.6 %collective-permute-done.19 = f32[4,8,128]{2,1,0:T(8,128)S(1)} collective-permute-done((f32[4,8,128]{2,1,0:T(8,128)S(1)}, f32[4,8,128]{2,1,0:T(8,128)S(1)}, u32[]{:S(2)}, u32[]{:S(2)}) %collective-permute-start.19) | collective-permute-done | bytes 16416 | tf_op jit(solution)/shard_map/ppermute | solution.py:737
  165.7 12.8 %collective-permute-start.20 = (f32[4,8,128]{2,1,0:T(8,128)S(1)}, f32[4,8,128]{2,1,0:T(8,128)S(1)}, u32[]{:S(2)}, u32[]{:S(2)}) collective-permute-start(f32[4,8,128]{2,1,0:T(8,128)S(1)} %fusion.1), channel_id=1, source_target_pairs={{0,4},{4,0},{8,12},{12,8},{16,20},{20,16},{24,28},{28,24},{1,5},{5... | collective-permute-start | bytes 49160 | tf_op jit(solution)/shard_map/ppermute | solution.py:737
  178.5 0.8 collective-permute-done.20
  179.3 3.7 %collective-permute-done.21 = f32[4,8,128]{2,1,0:T(8,128)S(1)} collective-permute-done((f32[4,8,128]{2,1,0:T(8,128)S(1)}, f32[4,8,128]{2,1,0:T(8,128)S(1)}, u32[]{:S(2)}, u32[]{:S(2)}) %collective-permute-start.21) | collective-permute-done | bytes 16416 | tf_op jit(solution)/shard_map/ppermute | solution.py:737
  183.0 2.0 collective-permute-start.33
  185.1 1.4 collective-permute-start.22
  186.5 1.9 collective-permute-start.27
  188.9 2.2 %collective-permute-start.28 = (f32[128,512]{1,0:T(8,128)S(1)}, f32[128,512]{1,0:T(8,128)S(1)}, u32[]{:S(2)}, u32[]{:S(2)}) collective-permute-start(f32[128,512]{1,0:T(8,128)S(1)} %get-tuple-element.79.refs_4_.before), channel_id=1, source_target_pairs={{0,3},{1,2},{2,1},{3,0},{4,7},{5,6},{6,5},{7,4},{8,11},{9,10},{10,... | collective-permute-start | bytes 786440 | tf_op jit(solution)/shard_map/ppermute | solution.py:737
  191.1 23.5 %collective-permute-done.26.refs_5_ = f32[128,512]{1,0:T(8,128)S(1)} collective-permute-done((f32[128,512]{1,0:T(8,128)S(1)}, f32[128,512]{1,0:T(8,128)S(1)}, u32[]{:S(2)}, u32[]{:S(2)}) %collective-permute-start.26) | collective-permute-done | bytes 262176 | tf_op jit(solution)/shard_map/ppermute | solution.py:737
  214.6 2.0 solution_image.1
  216.7 1.8 residual_image.1
  (54 shorter events, 6.0 us)
Async XLA Ops:
  0.6 9.0 %copy-start = (f32[128,2048]{1,0:T(8,128)S(1)}, f32[128,2048]{1,0:T(8,128)}, u32[]{:S(2)}) copy-start(f32[128,2048]{1,0:T(8,128)} %est.5) | copy-start | bytes 3145732
  1.8 6.3 %collective-permute-start = (f32[32,2048]{1,0:T(8,128)S(1)}, f32[32,2048]{1,0:T(8,128)S(1)}, u32[]{:S(2)}, u32[]{:S(2)}) collective-permute-start(f32[32,2048]{1,0:T(8,128)S(1)} %get-tuple-element.87), channel_id=1, source_target_pairs={{0,4},{8,12},{16,20},{24,28},{4,0},{12,8},{20,16},{28,24},{1,5},{9... | collective-permute-start | bytes 786440 | tf_op jit(solution)/shard_map/ppermute | solution.py:731
  1.9 7.7 %collective-permute-start.1 = (f32[32,2048]{1,0:T(8,128)S(1)}, f32[32,2048]{1,0:T(8,128)S(1)}, u32[]{:S(2)}, u32[]{:S(2)}) collective-permute-start(f32[32,2048]{1,0:T(8,128)S(1)} %get-tuple-element.86), channel_id=1, source_target_pairs={{4,8},{12,16},{20,24},{8,4},{16,12},{24,20},{5,9},{13,17},{21,25},... | collective-permute-start | bytes 786440 | tf_op jit(solution)/shard_map/ppermute | solution.py:731
  3.9 1.6 copy-start.1
  5.5 0.7 copy-start.3
  6.2 0.7 copy-start.4
  6.9 2.7 %copy-start.2 = (f32[2,128,2048]{2,1,0:T(8,128)S(1)}, f32[2,128,2048]{2,1,0:T(8,128)}, u32[]{:S(2)}) copy-start(f32[2,128,2048]{2,1,0:T(8,128)} %refs_5_.1) | copy-start | bytes 6291460
  9.6 1.6 copy-start.5
  16.9 5.6 %collective-permute-start.2 = (f32[32,2048]{1,0:T(8,128)S(1)}, f32[32,2048]{1,0:T(8,128)S(1)}, u32[]{:S(2)}, u32[]{:S(2)}) collective-permute-start(f32[32,2048]{1,0:T(8,128)S(1)} %get-tuple-element.48.send_a), channel_id=1, source_target_pairs={{0,4},{8,12},{16,20},{24,28},{4,0},{12,8},{20,16},{28,24},{1,5},{9... | collective-permute-start | bytes 786440 | tf_op jit(solution)/shard_map/ppermute | solution.py:731
  20.6 8.4 %collective-permute-start.3 = (f32[32,2048]{1,0:T(8,128)S(1)}, f32[32,2048]{1,0:T(8,128)S(1)}, u32[]{:S(2)}, u32[]{:S(2)}) collective-permute-start(f32[32,2048]{1,0:T(8,128)S(1)} %get-tuple-element.50.send_b), channel_id=1, source_target_pairs={{4,8},{12,16},{20,24},{8,4},{16,12},{24,20},{5,9},{13,17},{21,25},... | collective-permute-start | bytes 786440 | tf_op jit(solution)/shard_map/ppermute | solution.py:731
  29.9 20.7 %collective-permute-start.4 = (f32[144,512]{1,0:T(8,128)S(1)}, f32[144,512]{1,0:T(8,128)S(1)}, u32[]{:S(2)}, u32[]{:S(2)}) collective-permute-start(f32[144,512]{1,0:T(8,128)S(1)} %get-tuple-element.53), channel_id=1, source_target_pairs={{0,1},{1,0},{2,3},{3,2},{4,5},{5,4},{6,7},{7,6},{8,9},{9,8},{10,11... | collective-permute-start | bytes 884744 | tf_op jit(solution)/shard_map/ppermute | solution.py:737
  31.0 25.9 %collective-permute-start.6 = (f32[144,512]{1,0:T(8,128)S(1)}, f32[144,512]{1,0:T(8,128)S(1)}, u32[]{:S(2)}, u32[]{:S(2)}) collective-permute-start(f32[144,512]{1,0:T(8,128)S(1)} %get-tuple-element.54), channel_id=1, source_target_pairs={{0,1},{1,0},{2,3},{3,2},{4,5},{5,4},{6,7},{7,6},{8,9},{9,8},{10,11... | collective-permute-start | bytes 884744 | tf_op jit(solution)/shard_map/ppermute | solution.py:737
  32.0 68.2 %collective-permute-start.10 = (f32[264,512]{1,0:T(8,128)S(1)}, f32[264,512]{1,0:T(8,128)S(1)}, u32[]{:S(2)}, u32[]{:S(2)}) collective-permute-start(f32[264,512]{1,0:T(8,128)S(1)} %get-tuple-element.61), channel_id=1, source_target_pairs={{0,2},{1,3},{2,0},{3,1},{4,6},{5,7},{6,4},{7,5},{8,10},{9,11},{10,... | collective-permute-start | bytes 1622024 | tf_op jit(solution)/shard_map/ppermute | solution.py:737
  34.0 68.2 %collective-permute-start.9 = (f32[264,512]{1,0:T(8,128)S(1)}, f32[264,512]{1,0:T(8,128)S(1)}, u32[]{:S(2)}, u32[]{:S(2)}) collective-permute-start(f32[264,512]{1,0:T(8,128)S(1)} %get-tuple-element.60), channel_id=1, source_target_pairs={{0,1},{1,0},{2,3},{3,2},{4,5},{5,4},{6,7},{7,6},{8,9},{9,8},{10,11... | collective-permute-start | bytes 1622024 | tf_op jit(solution)/shard_map/ppermute | solution.py:737
  35.6 68.7 %collective-permute-start.12 = (f32[256,512]{1,0:T(8,128)S(1)}, f32[256,512]{1,0:T(8,128)S(1)}, u32[]{:S(2)}, u32[]{:S(2)}) collective-permute-start(f32[256,512]{1,0:T(8,128)S(1)} %get-tuple-element.66), channel_id=1, source_target_pairs={{1,2},{2,1},{5,6},{6,5},{9,10},{10,9},{13,14},{14,13},{17,18},{18,... | collective-permute-start | bytes 1572872 | tf_op jit(solution)/shard_map/ppermute | solution.py:766
  50.6 53.7 %collective-permute-start.13 = (f32[256,512]{1,0:T(8,128)S(1)}, f32[256,512]{1,0:T(8,128)S(1)}, u32[]{:S(2)}, u32[]{:S(2)}) collective-permute-start(f32[256,512]{1,0:T(8,128)S(1)} %get-tuple-element.66), channel_id=1, source_target_pairs={{0,3},{3,0},{4,7},{7,4},{8,11},{11,8},{12,15},{15,12},{16,19},{19,... | collective-permute-start | bytes 1572872 | tf_op jit(solution)/shard_map/ppermute | solution.py:766
  56.9 37.9 %collective-permute-start.5 = (f32[144,512]{1,0:T(8,128)S(1)}, f32[144,512]{1,0:T(8,128)S(1)}, u32[]{:S(2)}, u32[]{:S(2)}) collective-permute-start(f32[144,512]{1,0:T(8,128)S(1)} %add.23), channel_id=1, source_target_pairs={{0,2},{1,3},{2,0},{3,1},{4,6},{5,7},{6,4},{7,5},{8,10},{9,11},{10,... | collective-permute-start | bytes 884744 | tf_op jit(solution)/shard_map/ppermute | solution.py:737
  94.8 5.4 %collective-permute-start.11 = (f32[8,256]{1,0:T(8,128)S(1)}, f32[8,256]{1,0:T(8,128)S(1)}, u32[]{:S(2)}, u32[]{:S(2)}) collective-permute-start(f32[8,256]{1,0:T(8,128)S(1)} %slice.11), channel_id=1, source_target_pairs={{0,3},{1,2},{2,1},{3,0},{4,7},{5,6},{6,5},{7,4},{8,11},{9,10},{10,... | collective-permute-start | bytes 24584 | tf_op jit(solution)/shard_map/ppermute | solution.py:737
  100.2 4.1 %collective-permute-start.7 = (f32[32,768]{1,0:T(8,128)S(1)}, f32[32,768]{1,0:T(8,128)S(1)}, u32[]{:S(2)}, u32[]{:S(2)}) collective-permute-start(f32[32,768]{1,0:T(8,128)S(1)} %get-tuple-element.57), channel_id=1, source_target_pairs={{0,4},{8,12},{16,20},{24,28},{4,0},{12,8},{20,16},{28,24},{1,5},{9... | collective-permute-start | bytes 294920 | tf_op jit(solution)/shard_map/ppermute | solution.py:731
  100.3 5.9 %collective-permute-start.8 = (f32[32,768]{1,0:T(8,128)S(1)}, f32[32,768]{1,0:T(8,128)S(1)}, u32[]{:S(2)}, u32[]{:S(2)}) collective-permute-start(f32[32,768]{1,0:T(8,128)S(1)} %get-tuple-element.58), channel_id=1, source_target_pairs={{4,8},{12,16},{20,24},{8,4},{16,12},{24,20},{5,9},{13,17},{21,25},... | collective-permute-start | bytes 294920 | tf_op jit(solution)/shard_map/ppermute | solution.py:731
  115.5 3.4 %collective-permute-start.14 = (f32[64,640]{1,0:T(8,128)S(1)}, f32[64,640]{1,0:T(8,128)S(1)}, u32[]{:S(2)}, u32[]{:S(2)}) collective-permute-start(f32[64,640]{1,0:T(8,128)S(1)} %get-tuple-element.68.send_a), channel_id=1, source_target_pairs={{0,4},{8,12},{16,20},{24,28},{4,0},{12,8},{20,16},{28,24},{1,5},{9... | collective-permute-start | bytes 491528 | tf_op jit(solution)/shard_map/ppermute | solution.py:731
  117.0 6.6 %collective-permute-start.15 = (f32[64,640]{1,0:T(8,128)S(1)}, f32[64,640]{1,0:T(8,128)S(1)}, u32[]{:S(2)}, u32[]{:S(2)}) collective-permute-start(f32[64,640]{1,0:T(8,128)S(1)} %get-tuple-element.70.send_b), channel_id=1, source_target_pairs={{4,8},{12,16},{20,24},{8,4},{16,12},{24,20},{5,9},{13,17},{21,25},... | collective-permute-start | bytes 491528 | tf_op jit(solution)/shard_map/ppermute | solution.py:731
  124.3 5.7 %collective-permute-start.16 = (f32[192,128]{1,0:T(8,128)S(1)}, f32[192,128]{1,0:T(8,128)S(1)}, u32[]{:S(2)}, u32[]{:S(2)}) collective-permute-start(f32[192,128]{1,0:T(8,128)S(1)} %get-tuple-element.72), channel_id=1, source_target_pairs={{0,1},{2,3},{1,0},{3,2},{4,5},{6,7},{5,4},{7,6},{8,9},{10,11},{9,8... | collective-permute-start | bytes 294920 | tf_op jit(solution)/shard_map/ppermute | solution.py:731
  124.4 5.6 %collective-permute-start.17 = (f32[192,128]{1,0:T(8,128)S(1)}, f32[192,128]{1,0:T(8,128)S(1)}, u32[]{:S(2)}, u32[]{:S(2)}) collective-permute-start(f32[192,128]{1,0:T(8,128)S(1)} %get-tuple-element.73), channel_id=1, source_target_pairs={{1,2},{2,1},{5,6},{6,5},{9,10},{10,9},{13,14},{14,13},{17,18},{18,... | collective-permute-start | bytes 294920 | tf_op jit(solution)/shard_map/ppermute | solution.py:731
  140.2 5.7 %collective-permute-start.29 = (f32[32,640]{1,0:T(8,128)S(1)}, f32[32,640]{1,0:T(8,128)S(1)}, u32[]{:S(2)}, u32[]{:S(2)}) collective-permute-start(f32[32,640]{1,0:T(8,128)S(1)} %get-tuple-element.83.send_a), channel_id=1, source_target_pairs={{0,4},{8,12},{16,20},{24,28},{4,0},{12,8},{20,16},{28,24},{1,5},{9... | collective-permute-start | bytes 245768 | tf_op jit(solution)/shard_map/ppermute | solution.py:731
  140.4 5.7 %collective-permute-start.30 = (f32[32,640]{1,0:T(8,128)S(1)}, f32[32,640]{1,0:T(8,128)S(1)}, u32[]{:S(2)}, u32[]{:S(2)}) collective-permute-start(f32[32,640]{1,0:T(8,128)S(1)} %get-tuple-element.85.send_b), channel_id=1, source_target_pairs={{4,8},{12,16},{20,24},{8,4},{16,12},{24,20},{5,9},{13,17},{21,25},... | collective-permute-start | bytes 245768 | tf_op jit(solution)/shard_map/ppermute | solution.py:731
  142.3 9.2 %collective-permute-start.18 = (f32[4,8,128]{2,1,0:T(8,128)S(1)}, f32[4,8,128]{2,1,0:T(8,128)S(1)}, u32[]{:S(2)}, u32[]{:S(2)}) collective-permute-start(f32[4,8,128]{2,1,0:T(8,128)S(1)} %pad_maximum_fusion), channel_id=1, source_target_pairs={{0,1},{1,0},{2,3},{3,2},{4,5},{5,4},{6,7},{7,6},{8,9},{9,8},{10,11... | collective-permute-start | bytes 49160 | tf_op jit(solution)/shard_map/ppermute | solution.py:737
  146.8 36.2 %collective-permute-start.32 = (f32[144,512]{1,0:T(8,128)S(1)}, f32[144,512]{1,0:T(8,128)S(1)}, u32[]{:S(2)}, u32[]{:S(2)}) collective-permute-start(f32[144,512]{1,0:T(8,128)S(1)} %wrap.1.refs_0_), channel_id=1, source_target_pairs={{0,2},{1,3},{2,0},{3,1},{4,6},{5,7},{6,4},{7,5},{8,10},{9,11},{10,... | collective-permute-start | bytes 884744 | tf_op jit(solution)/shard_map/ppermute | solution.py:737
  151.5 14.2 %collective-permute-start.19 = (f32[4,8,128]{2,1,0:T(8,128)S(1)}, f32[4,8,128]{2,1,0:T(8,128)S(1)}, u32[]{:S(2)}, u32[]{:S(2)}) collective-permute-start(f32[4,8,128]{2,1,0:T(8,128)S(1)} %fusion), channel_id=1, source_target_pairs={{0,2},{1,3},{2,0},{3,1},{4,6},{5,7},{6,4},{7,5},{8,10},{9,11},{10,... | collective-permute-start | bytes 49160 | tf_op jit(solution)/shard_map/ppermute | solution.py:737
  151.6 33.5 %collective-permute-start.23 = (f32[128,512]{1,0:T(8,128)S(1)}, f32[128,512]{1,0:T(8,128)S(1)}, u32[]{:S(2)}, u32[]{:S(2)}) collective-permute-start(f32[128,512]{1,0:T(8,128)S(1)} %get-tuple-element.78.refs_0_), channel_id=1, source_target_pairs={{0,1},{1,0},{2,3},{3,2},{4,5},{5,4},{6,7},{7,6},{8,9},{9,8},{10,11... | collective-permute-start | bytes 786440 | tf_op jit(solution)/shard_map/ppermute | solution.py:737
  153.4 33.0 %collective-permute-start.24 = (f32[128,512]{1,0:T(8,128)S(1)}, f32[128,512]{1,0:T(8,128)S(1)}, u32[]{:S(2)}, u32[]{:S(2)}) collective-permute-start(f32[128,512]{1,0:T(8,128)S(1)} %get-tuple-element.78.refs_0_), channel_id=1, source_target_pairs={{0,2},{1,3},{2,0},{3,1},{4,6},{5,7},{6,4},{7,5},{8,10},{9,11},{10,... | collective-permute-start | bytes 786440 | tf_op jit(solution)/shard_map/ppermute | solution.py:737
  154.5 32.0 %collective-permute-start.25 = (f32[128,512]{1,0:T(8,128)S(1)}, f32[128,512]{1,0:T(8,128)S(1)}, u32[]{:S(2)}, u32[]{:S(2)}) collective-permute-start(f32[128,512]{1,0:T(8,128)S(1)} %get-tuple-element.78.refs_0_), channel_id=1, source_target_pairs={{0,3},{1,2},{2,1},{3,0},{4,7},{5,6},{6,5},{7,4},{8,11},{9,10},{10,... | collective-permute-start | bytes 786440 | tf_op jit(solution)/shard_map/ppermute | solution.py:737
  165.7 13.6 %collective-permute-start.20 = (f32[4,8,128]{2,1,0:T(8,128)S(1)}, f32[4,8,128]{2,1,0:T(8,128)S(1)}, u32[]{:S(2)}, u32[]{:S(2)}) collective-permute-start(f32[4,8,128]{2,1,0:T(8,128)S(1)} %fusion.1), channel_id=1, source_target_pairs={{0,4},{4,0},{8,12},{12,8},{16,20},{20,16},{24,28},{28,24},{1,5},{5... | collective-permute-start | bytes 49160 | tf_op jit(solution)/shard_map/ppermute | solution.py:737
  179.3 3.7 %collective-permute-start.21 = (f32[4,8,128]{2,1,0:T(8,128)S(1)}, f32[4,8,128]{2,1,0:T(8,128)S(1)}, u32[]{:S(2)}, u32[]{:S(2)}) collective-permute-start(f32[4,8,128]{2,1,0:T(8,128)S(1)} %add.26), channel_id=1, source_target_pairs={{0,8},{4,12},{8,0},{12,4},{16,24},{20,28},{24,16},{28,20},{1,9},{5... | collective-permute-start | bytes 49160 | tf_op jit(solution)/shard_map/ppermute | solution.py:737
  183.0 33.6 %collective-permute-start.31 = (f32[144,512]{1,0:T(8,128)S(1)}, f32[144,512]{1,0:T(8,128)S(1)}, u32[]{:S(2)}, u32[]{:S(2)}) collective-permute-start(f32[144,512]{1,0:T(8,128)S(1)} %wrap.1.refs_0_), channel_id=1, source_target_pairs={{0,1},{1,0},{2,3},{3,2},{4,5},{5,4},{6,7},{7,6},{8,9},{9,8},{10,11... | collective-permute-start | bytes 884744 | tf_op jit(solution)/shard_map/ppermute | solution.py:737
  183.0 33.6 %collective-permute-start.33 = (f32[144,512]{1,0:T(8,128)S(1)}, f32[144,512]{1,0:T(8,128)S(1)}, u32[]{:S(2)}, u32[]{:S(2)}) collective-permute-start(f32[144,512]{1,0:T(8,128)S(1)} %collective-permute-done.32.refs_2_), channel_id=1, source_target_pairs={{0,1},{1,0},{2,3},{3,2},{4,5},{5,4},{6,7},{7,6},{8,9},{9,8},{10,11... | collective-permute-start | bytes 884744 | tf_op jit(solution)/shard_map/ppermute | solution.py:737
  185.1 3.8 %collective-permute-start.22 = (f32[4,8,128]{2,1,0:T(8,128)S(1)}, f32[4,8,128]{2,1,0:T(8,128)S(1)}, u32[]{:S(2)}, u32[]{:S(2)}) collective-permute-start(f32[4,8,128]{2,1,0:T(8,128)S(1)} %add.27), channel_id=1, source_target_pairs={{0,16},{4,20},{8,24},{12,28},{16,0},{20,4},{24,8},{28,12},{1,17},{... | collective-permute-start | bytes 49160 | tf_op jit(solution)/shard_map/ppermute | solution.py:737
  186.4 28.2 %collective-permute-start.26 = (f32[128,512]{1,0:T(8,128)S(1)}, f32[128,512]{1,0:T(8,128)S(1)}, u32[]{:S(2)}, u32[]{:S(2)}) collective-permute-start(f32[128,512]{1,0:T(8,128)S(1)} %get-tuple-element.79.refs_4_.before), channel_id=1, source_target_pairs={{0,1},{1,0},{2,3},{3,2},{4,5},{5,4},{6,7},{7,6},{8,9},{9,8},{10,11... | collective-permute-start | bytes 786440 | tf_op jit(solution)/shard_map/ppermute | solution.py:737
  186.5 28.1 %collective-permute-start.27 = (f32[128,512]{1,0:T(8,128)S(1)}, f32[128,512]{1,0:T(8,128)S(1)}, u32[]{:S(2)}, u32[]{:S(2)}) collective-permute-start(f32[128,512]{1,0:T(8,128)S(1)} %get-tuple-element.79.refs_4_.before), channel_id=1, source_target_pairs={{0,2},{1,3},{2,0},{3,1},{4,6},{5,7},{6,4},{7,5},{8,10},{9,11},{10,... | collective-permute-start | bytes 786440 | tf_op jit(solution)/shard_map/ppermute | solution.py:737
  188.9 25.7 %collective-permute-start.28 = (f32[128,512]{1,0:T(8,128)S(1)}, f32[128,512]{1,0:T(8,128)S(1)}, u32[]{:S(2)}, u32[]{:S(2)}) collective-permute-start(f32[128,512]{1,0:T(8,128)S(1)} %get-tuple-element.79.refs_4_.before), channel_id=1, source_target_pairs={{0,3},{1,2},{2,1},{3,0},{4,7},{5,6},{6,5},{7,4},{8,11},{9,10},{10,... | collective-permute-start | bytes 786440 | tf_op jit(solution)/shard_map/ppermute | solution.py:737

commit v3 on v2

--- a/solution.py
+++ b/solution.py
@@ -15,6 +15,7 @@
 VMEM = pl.BlockSpec(memory_space=pltpu.VMEM)
 ANY = pl.BlockSpec(memory_space=pl.ANY)
 SMEM = pl.BlockSpec(memory_space=pltpu.SMEM)
+HBM = pl.BlockSpec(memory_space=pltpu.HBM)
 
 
 def room(mib):
@@ -295,7 +296,7 @@
             jax.ShapeDtypeStruct((rows, cols), f32),
             jax.ShapeDtypeStruct((halo, cols), f32),
         ],
-        in_specs=[SMEM] + [VMEM] * 7 + [ANY, ANY],
+        in_specs=[SMEM] + [VMEM] * 7 + [HBM, HBM],
         out_specs=[VMEM] * 3,
         scratch_shapes=work_scratch(frames, rows, halo, cols)
         + [
@@ -310,8 +311,15 @@
 
 
 def prepare_kernel(plan, frames, rows, halo, w, place, cols_in, rows_in, weights, *refs):
-    outs, tile, mats, sem = refs[: len(plan)], refs[len(plan)], refs[len(plan) + 1 : -1], refs[-1]
+    outs, tile, mats = refs[: len(plan)], refs[len(plan)], refs[len(plan) + 1 : -4]
+    cols_buf, rows_buf, taps_sem, sem = refs[-4:]
     taps = cols_in.shape[1]
+    taps_copies = (
+        pltpu.make_async_copy(cols_in, cols_buf, taps_sem.at[0]),
+        pltpu.make_async_copy(rows_in, rows_buf, taps_sem.at[1]),
+    )
+    for copy in taps_copies:
+        copy.start()
     pending = []
     for i, (distance, _) in enumerate(plan):
         start = pl.multiple_of(jnp.bitwise_xor(place[0], distance) * w, LANE)
@@ -324,8 +332,10 @@
             copy.start()
             pending.append(copy)
     tile[...] = jnp.zeros_like(tile)
-    tile[:frames, :taps] = cols_in[...]
-    tile[frames : 2 * frames, :taps] = rows_in[...]
+    for copy in taps_copies:
+        copy.wait()
+    tile[:frames, :taps] = cols_buf[...]
+    tile[frames : 2 * frames, :taps] = rows_buf[...]
     for i, (_, with_taps) in enumerate(plan):
         if with_taps:
             outs[i][frames * rows :, :] = tile[...]
@@ -345,9 +355,14 @@
         ]
         + [jax.ShapeDtypeStruct((height, w), f32)]
         + matrix_shapes(1, frames, rows, halo),
-        in_specs=[SMEM, VMEM, VMEM, ANY],
+        in_specs=[SMEM, HBM, HBM, HBM],
         out_specs=[VMEM] * (len(plan) + 5),
-        scratch_shapes=[pltpu.SemaphoreType.DMA((len(plan), frames))],
+        scratch_shapes=[
+            pltpu.VMEM(column_kernels.shape, f32),
+            pltpu.VMEM(row_kernels.shape, f32),
+            pltpu.SemaphoreType.DMA((2,)),
+            pltpu.SemaphoreType.DMA((len(plan), frames)),
+        ],
         compiler_params=room(24),
         name="prepare",
     )(place, column_kernels, row_kernels, weights)
@@ -522,7 +537,7 @@
             jax.ShapeDtypeStruct((8, LANE), f32),
         ]
         + [jax.ShapeDtypeStruct((ext, w + 2 * LANE), f32)] * (len(image) > 1),
-        in_specs=[SMEM] + [VMEM] * len(image) + [ANY] * (5 + len(moved)),
+        in_specs=[SMEM] + [VMEM] * len(image) + [ANY] * 4 + [HBM] + [ANY] * len(moved),
         out_specs=[VMEM] * (4 + (len(image) > 1)),
         scratch_shapes=work_scratch(frames, rows, halo, w)
         + [
@@ -746,6 +761,9 @@
     rows, cols = estimate.shape
     frames = weights.shape[0]
     halo = column_kernels.shape[1] // 2
+    stay = lambda x: pltpu.with_memory_space_constraint(x, pltpu.HBM)
+    weights, observed = stay(weights), stay(observed)
+    column_kernels, row_kernels = stay(column_kernels), stay(row_kernels)
     w = cols // n
     distances = [1 << k for k in range(n.bit_length() - 1)]
 

time: 220 us -> 219 us (level)
  local copies, waits for them, and re-layouts: 4.55 us -> 0.01 us
    unnamed x12 -> x2, local copies, waits for them, and re-layouts: 4.55 us -> 0.01 us
  transfers between devices with their start and end apart: 34 -> 34, of which waited for: 15 -> 15; matrix products, arithmetic and copies ran while one was open for 0% -> 0% of each run, Pallas kernels for 3% -> 4%
where the time goes in v3:
time: 219 us; the launch traced here: 218 us
  waiting for transfers between devices  118 us (54%)
  starting transfers between devices  60 us (27%)
  Pallas kernels  37.1 us (17%)
    ppermute x20, waiting for transfers between devices, swap(): return lax.ppermute(x, axis, [(i, i ^ distance) for i in range(n)])  96.5 us
    ppermute x20, starting transfers between devices, swap(): return lax.ppermute(x, axis, [(i, i ^ distance) for i in range(n)])  41.2 us
    ppermute x12, waiting for transfers between devices, neighbours(): out.append(lax.ppermute(x, axis, pairs + [(b, a) for a, b in pairs]))  21.6 us
    pallas_call x2, Pallas kernels, apply_terms(): pl.pallas_call(functools.partial(apply_kernel, frames, rows, halo, w, gro...  18.8 us
    ppermute x12, starting transfers between devices, neighbours(): out.append(lax.ppermute(x, axis, pairs + [(b, a) for a, b in pairs]))  15.6 us
    pallas_call x1, Pallas kernels, first_terms(): pl.pallas_call(functools.partial(first_kernel, frames, rows, halo), out_s...  6.47 us
  transfers between devices with their start and end apart: 34, of which 15 were waited for; matrix products, arithmetic and copies ran while one was open for 0% of the time, Pallas kernels for 4%

profile of v3, /device:TPU:2, one launch (start us, length us, event | category | flops | bytes accessed | tf_op | source)
XLA Modules:
  0.0 217.6 jit_solution(417870323777010248)
XLA Ops:
  0.7 1.2 slice_select_fusion
  1.9 1.9 collective-permute-start.1
  3.9 2.2 %prepare.1 = (f32[264,512]{1,0:T(8,128)S(1)}, f32[264,512]{1,0:T(8,128)S(1)}, f32[256,512]{1,0:T(8,128)S(1)}, f32[8,512]{1,0:T(8,128)S(1)}, bf16[2,256,256]{2,1,...) custom-call(s32[2]{0:T(128)S(1)} %pad_add_fusion.place, ...), custom_call_target="tpu_custom_call" | custom-call | tf_op jit(solution)/shard_map/prepare/pallas_call | solution.py:350
  6.1 3.4 %collective-permute-done.1.recv_b = f32[32,2048]{1,0:T(8,128)S(1)} collective-permute-done((f32[32,2048]{1,0:T(8,128)S(1)}, f32[32,2048]{1,0:T(8,128)S(1)}, u32[]{:S(2)}, u32[]{:S(2)}) %collective-permute-start.1) | collective-permute-done | bytes 262176 | tf_op jit(solution)/shard_map/ppermute | solution.py:746
  9.6 6.5 %first_terms.1 = (f32[32,2048]{1,0:T(8,128)S(1)}, f32[128,2048]{1,0:T(8,128)S(1)}, f32[32,2048]{1,0:T(8,128)S(1)}) custom-call(s32[2]{0:T(128)S(1)} %pad_add_fusion.place, f32[128,2048]{1,0:T(8,128)S(1)} %copy-done, f32[32,2048]{1,0:T(8,128)S(1)} %collective-permute-done.recv_a, f32[32,2048]{1,0:T(8,128)S(1)} %collective-permute-done.1.recv_b, ...), custom_call_target="tpu_custom_call" | custom-call | flops 8000000000 | bytes 8388608 | tf_op jit(solution)/shard_map/first_terms/pallas_call | solution.py:292
  16.1 3.6 %collective-permute-start.2 = (f32[32,2048]{1,0:T(8,128)S(1)}, f32[32,2048]{1,0:T(8,128)S(1)}, u32[]{:S(2)}, u32[]{:S(2)}) collective-permute-start(f32[32,2048]{1,0:T(8,128)S(1)} %get-tuple-element.48.send_a), channel_id=1, source_target_pairs={{0,4},{8,12},{16,20},{24,28},{4,0},{12,8},{20,16},{28,24},{1,5},{9... | collective-permute-start | bytes 786440 | tf_op jit(solution)/shard_map/ppermute | solution.py:746
  19.7 1.9 collective-permute-start.3
  21.6 6.5 %collective-permute-done.3.recv_b = f32[32,2048]{1,0:T(8,128)S(1)} collective-permute-done((f32[32,2048]{1,0:T(8,128)S(1)}, f32[32,2048]{1,0:T(8,128)S(1)}, u32[]{:S(2)}, u32[]{:S(2)}) %collective-permute-start.3) | collective-permute-done | bytes 262176 | tf_op jit(solution)/shard_map/ppermute | solution.py:746
  28.2 0.9 column_blocks.1
  29.1 1.0 collective-permute-start.4
  30.1 1.1 collective-permute-start.6
  31.2 2.0 collective-permute-start.10
  33.1 1.6 collective-permute-start.9
  34.7 0.7 collective-permute-start.12
  35.4 14.3 %collective-permute-done.4 = f32[144,512]{1,0:T(8,128)S(1)} collective-permute-done((f32[144,512]{1,0:T(8,128)S(1)}, f32[144,512]{1,0:T(8,128)S(1)}, u32[]{:S(2)}, u32[]{:S(2)}) %collective-permute-start.4) | collective-permute-done | bytes 294944 | tf_op jit(solution)/shard_map/ppermute | solution.py:752
  49.7 2.5 %collective-permute-start.13 = (f32[256,512]{1,0:T(8,128)S(1)}, f32[256,512]{1,0:T(8,128)S(1)}, u32[]{:S(2)}, u32[]{:S(2)}) collective-permute-start(f32[256,512]{1,0:T(8,128)S(1)} %get-tuple-element.66), channel_id=1, source_target_pairs={{0,3},{3,0},{4,7},{7,4},{8,11},{11,8},{12,15},{15,12},{16,19},{19,... | collective-permute-start | bytes 1572872 | tf_op jit(solution)/shard_map/ppermute | solution.py:784
  52.3 3.7 %collective-permute-done.6.refs_2_ = f32[144,512]{1,0:T(8,128)S(1)} collective-permute-done((f32[144,512]{1,0:T(8,128)S(1)}, f32[144,512]{1,0:T(8,128)S(1)}, u32[]{:S(2)}, u32[]{:S(2)}) %collective-permute-start.6) | collective-permute-done | bytes 294944 | tf_op jit(solution)/shard_map/ppermute | solution.py:752
  56.0 37.9 %collective-permute-done.5.refs_1_ = f32[144,512]{1,0:T(8,128)S(1)} collective-permute-done((f32[144,512]{1,0:T(8,128)S(1)}, f32[144,512]{1,0:T(8,128)S(1)}, u32[]{:S(2)}, u32[]{:S(2)}) %collective-permute-start.5) | collective-permute-done | bytes 294944 | tf_op jit(solution)/shard_map/ppermute | solution.py:752
  93.9 2.4 %collective-permute-start.11 = (f32[8,256]{1,0:T(8,128)S(1)}, f32[8,256]{1,0:T(8,128)S(1)}, u32[]{:S(2)}, u32[]{:S(2)}) collective-permute-start(f32[8,256]{1,0:T(8,128)S(1)} %slice.11), channel_id=1, source_target_pairs={{0,3},{1,2},{2,1},{3,0},{4,7},{5,6},{6,5},{7,4},{8,11},{9,10},{10,... | collective-permute-start | bytes 24584 | tf_op jit(solution)/shard_map/ppermute | solution.py:752
  96.3 0.7 start_image.1
  97.0 2.4 %collective-permute-done.11.refs_3_ = f32[8,256]{1,0:T(8,128)S(1)} collective-permute-done((f32[8,256]{1,0:T(8,128)S(1)}, f32[8,256]{1,0:T(8,128)S(1)}, u32[]{:S(2)}, u32[]{:S(2)}) %collective-permute-start.11) | collective-permute-done | bytes 8224 | tf_op jit(solution)/shard_map/ppermute | solution.py:752
  99.4 1.9 collective-permute-start.8
  101.3 2.1 setup_all.1
  103.5 1.9 collective-permute-done.8.refs_2_
  105.3 9.3 %shard_map.68 = (f32[64,640]{1,0:T(8,128)S(1)}, f32[64,640]{1,0:T(8,128)S(1)}, f32[64,640]{1,0:T(8,128)S(1)}, f32[8,128]{1,0:T(8,128)S(1)}, f32[192,768]{1,0:T(8,128)S(1)}) custom-call(s32[2]{0:T(128)S(1)} %pad_add_fusion.place, f32[128,768]{1,0:T(8,128)S(1)} %get-tuple-element.56.refs_0_, f32[32,768]{1,0:T(8,128)S(1)} %collective-permute-done.7.refs_1_, ...), custom_call_target="tpu_custom_call" | custom-call | flops 12000000000 | bytes 4194304 | tf_op jit(solution)/shard_map/pallas_call | solution.py:531
  114.7 1.5 collective-permute-start.14
  116.1 1.9 collective-permute-start.15
  118.1 4.7 %collective-permute-done.15.recv_b = f32[64,640]{1,0:T(8,128)S(1)} collective-permute-done((f32[64,640]{1,0:T(8,128)S(1)}, f32[64,640]{1,0:T(8,128)S(1)}, u32[]{:S(2)}, u32[]{:S(2)}) %collective-permute-start.15) | collective-permute-done | bytes 163872 | tf_op jit(solution)/shard_map/ppermute | solution.py:746
  124.2 4.9 %collective-permute-done.16.recv_a = f32[192,128]{1,0:T(8,128)S(1)} collective-permute-done((f32[192,128]{1,0:T(8,128)S(1)}, f32[192,128]{1,0:T(8,128)S(1)}, u32[]{:S(2)}, u32[]{:S(2)}) %collective-permute-start.16) | collective-permute-done | bytes 98336 | tf_op jit(solution)/shard_map/ppermute | solution.py:746
  129.8 9.5 %shard_map.69 = (f32[32,640]{1,0:T(8,128)S(1)}, f32[128,640]{1,0:T(8,128)S(1)}, f32[32,640]{1,0:T(8,128)S(1)}, f32[8,128]{1,0:T(8,128)S(1)}) custom-call(s32[2]{0:T(128)S(1)} %pad_add_fusion.place, f32[192,768]{1,0:T(8,128)S(1)} %get-tuple-element.76.refs_0_, bf16[8,256,256]{2,1,0:T(8,128)(2,1)S(1)} %get-tuple-element.62.refs_3_.refs_1_, ...), custom_call_target="tpu_custom_call" | custom-call | flops 12000000000 | bytes 4194304 | tf_op jit(solution)/shard_map/pallas_call | solution.py:531
  139.5 1.9 collective-permute-start.30
  141.4 3.6 %collective-permute-start.18 = (f32[4,8,128]{2,1,0:T(8,128)S(1)}, f32[4,8,128]{2,1,0:T(8,128)S(1)}, u32[]{:S(2)}, u32[]{:S(2)}) collective-permute-start(f32[4,8,128]{2,1,0:T(8,128)S(1)} %pad_maximum_fusion), channel_id=1, source_target_pairs={{0,1},{1,0},{2,3},{3,2},{4,5},{5,4},{6,7},{7,6},{8,9},{9,8},{10,11... | collective-permute-start | bytes 49160 | tf_op jit(solution)/shard_map/ppermute | solution.py:752
  145.2 0.7 wrap.1.refs_0_
  145.9 4.7 %collective-permute-start.32 = (f32[144,512]{1,0:T(8,128)S(1)}, f32[144,512]{1,0:T(8,128)S(1)}, u32[]{:S(2)}, u32[]{:S(2)}) collective-permute-start(f32[144,512]{1,0:T(8,128)S(1)} %wrap.1.refs_0_), channel_id=1, source_target_pairs={{0,2},{1,3},{2,0},{3,1},{4,6},{5,7},{6,4},{7,5},{8,10},{9,11},{10,... | collective-permute-start | bytes 884744 | tf_op jit(solution)/shard_map/ppermute | solution.py:752
  150.7 1.8 collective-permute-start.23
  152.6 1.1 collective-permute-start.24
  153.6 1.5 collective-permute-start.25
  155.1 9.6 %collective-permute-done.19 = f32[4,8,128]{2,1,0:T(8,128)S(1)} collective-permute-done((f32[4,8,128]{2,1,0:T(8,128)S(1)}, f32[4,8,128]{2,1,0:T(8,128)S(1)}, u32[]{:S(2)}, u32[]{:S(2)}) %collective-permute-start.19) | collective-permute-done | bytes 16416 | tf_op jit(solution)/shard_map/ppermute | solution.py:752
  164.8 12.8 %collective-permute-start.20 = (f32[4,8,128]{2,1,0:T(8,128)S(1)}, f32[4,8,128]{2,1,0:T(8,128)S(1)}, u32[]{:S(2)}, u32[]{:S(2)}) collective-permute-start(f32[4,8,128]{2,1,0:T(8,128)S(1)} %fusion.1), channel_id=1, source_target_pairs={{0,4},{4,0},{8,12},{12,8},{16,20},{20,16},{24,28},{28,24},{1,5},{5... | collective-permute-start | bytes 49160 | tf_op jit(solution)/shard_map/ppermute | solution.py:752
  177.6 0.8 collective-permute-done.20
  178.4 3.7 %collective-permute-done.21 = f32[4,8,128]{2,1,0:T(8,128)S(1)} collective-permute-done((f32[4,8,128]{2,1,0:T(8,128)S(1)}, f32[4,8,128]{2,1,0:T(8,128)S(1)}, u32[]{:S(2)}, u32[]{:S(2)}) %collective-permute-start.21) | collective-permute-done | bytes 16416 | tf_op jit(solution)/shard_map/ppermute | solution.py:752
  182.1 2.0 collective-permute-start.33
  184.2 1.4 collective-permute-start.22
  185.6 2.0 collective-permute-start.27
  188.0 2.2 %collective-permute-start.28 = (f32[128,512]{1,0:T(8,128)S(1)}, f32[128,512]{1,0:T(8,128)S(1)}, u32[]{:S(2)}, u32[]{:S(2)}) collective-permute-start(f32[128,512]{1,0:T(8,128)S(1)} %get-tuple-element.79.refs_4_.before), channel_id=1, source_target_pairs={{0,3},{1,2},{2,1},{3,0},{4,7},{5,6},{6,5},{7,4},{8,11},{9,10},{10,... | collective-permute-start | bytes 786440 | tf_op jit(solution)/shard_map/ppermute | solution.py:752
  190.2 23.5 %collective-permute-done.26.refs_5_ = f32[128,512]{1,0:T(8,128)S(1)} collective-permute-done((f32[128,512]{1,0:T(8,128)S(1)}, f32[128,512]{1,0:T(8,128)S(1)}, u32[]{:S(2)}, u32[]{:S(2)}) %collective-permute-start.26) | collective-permute-done | bytes 262176 | tf_op jit(solution)/shard_map/ppermute | solution.py:752
  213.7 2.0 solution_image.1
  215.8 1.8 residual_image.1
  (44 shorter events, 3.2 us)
Async XLA Ops:
  0.6 9.0 %copy-start = (f32[128,2048]{1,0:T(8,128)S(1)}, f32[128,2048]{1,0:T(8,128)}, u32[]{:S(2)}) copy-start(f32[128,2048]{1,0:T(8,128)} %est.5) | copy-start | bytes 3145732
  1.8 4.3 %collective-permute-start = (f32[32,2048]{1,0:T(8,128)S(1)}, f32[32,2048]{1,0:T(8,128)S(1)}, u32[]{:S(2)}, u32[]{:S(2)}) collective-permute-start(f32[32,2048]{1,0:T(8,128)S(1)} %get-tuple-element.87), channel_id=1, source_target_pairs={{0,4},{8,12},{16,20},{24,28},{4,0},{12,8},{20,16},{28,24},{1,5},{9... | collective-permute-start | bytes 786440 | tf_op jit(solution)/shard_map/ppermute | solution.py:746
  1.9 7.7 %collective-permute-start.1 = (f32[32,2048]{1,0:T(8,128)S(1)}, f32[32,2048]{1,0:T(8,128)S(1)}, u32[]{:S(2)}, u32[]{:S(2)}) collective-permute-start(f32[32,2048]{1,0:T(8,128)S(1)} %get-tuple-element.86), channel_id=1, source_target_pairs={{4,8},{12,16},{20,24},{8,4},{16,12},{24,20},{5,9},{13,17},{21,25},... | collective-permute-start | bytes 786440 | tf_op jit(solution)/shard_map/ppermute | solution.py:746
  16.1 5.6 %collective-permute-start.2 = (f32[32,2048]{1,0:T(8,128)S(1)}, f32[32,2048]{1,0:T(8,128)S(1)}, u32[]{:S(2)}, u32[]{:S(2)}) collective-permute-start(f32[32,2048]{1,0:T(8,128)S(1)} %get-tuple-element.48.send_a), channel_id=1, source_target_pairs={{0,4},{8,12},{16,20},{24,28},{4,0},{12,8},{20,16},{28,24},{1,5},{9... | collective-permute-start | bytes 786440 | tf_op jit(solution)/shard_map/ppermute | solution.py:746
  19.7 8.4 %collective-permute-start.3 = (f32[32,2048]{1,0:T(8,128)S(1)}, f32[32,2048]{1,0:T(8,128)S(1)}, u32[]{:S(2)}, u32[]{:S(2)}) collective-permute-start(f32[32,2048]{1,0:T(8,128)S(1)} %get-tuple-element.50.send_b), channel_id=1, source_target_pairs={{4,8},{12,16},{20,24},{8,4},{16,12},{24,20},{5,9},{13,17},{21,25},... | collective-permute-start | bytes 786440 | tf_op jit(solution)/shard_map/ppermute | solution.py:746
  29.1 20.6 %collective-permute-start.4 = (f32[144,512]{1,0:T(8,128)S(1)}, f32[144,512]{1,0:T(8,128)S(1)}, u32[]{:S(2)}, u32[]{:S(2)}) collective-permute-start(f32[144,512]{1,0:T(8,128)S(1)} %get-tuple-element.53), channel_id=1, source_target_pairs={{0,1},{1,0},{2,3},{3,2},{4,5},{5,4},{6,7},{7,6},{8,9},{9,8},{10,11... | collective-permute-start | bytes 884744 | tf_op jit(solution)/shard_map/ppermute | solution.py:752
  30.1 25.9 %collective-permute-start.6 = (f32[144,512]{1,0:T(8,128)S(1)}, f32[144,512]{1,0:T(8,128)S(1)}, u32[]{:S(2)}, u32[]{:S(2)}) collective-permute-start(f32[144,512]{1,0:T(8,128)S(1)} %get-tuple-element.54), channel_id=1, source_target_pairs={{0,1},{1,0},{2,3},{3,2},{4,5},{5,4},{6,7},{7,6},{8,9},{9,8},{10,11... | collective-permute-start | bytes 884744 | tf_op jit(solution)/shard_map/ppermute | solution.py:752
  31.2 68.2 %collective-permute-start.10 = (f32[264,512]{1,0:T(8,128)S(1)}, f32[264,512]{1,0:T(8,128)S(1)}, u32[]{:S(2)}, u32[]{:S(2)}) collective-permute-start(f32[264,512]{1,0:T(8,128)S(1)} %get-tuple-element.61), channel_id=1, source_target_pairs={{0,2},{1,3},{2,0},{3,1},{4,6},{5,7},{6,4},{7,5},{8,10},{9,11},{10,... | collective-permute-start | bytes 1622024 | tf_op jit(solution)/shard_map/ppermute | solution.py:752
  33.1 68.2 %collective-permute-start.9 = (f32[264,512]{1,0:T(8,128)S(1)}, f32[264,512]{1,0:T(8,128)S(1)}, u32[]{:S(2)}, u32[]{:S(2)}) collective-permute-start(f32[264,512]{1,0:T(8,128)S(1)} %get-tuple-element.60), channel_id=1, source_target_pairs={{0,1},{1,0},{2,3},{3,2},{4,5},{5,4},{6,7},{7,6},{8,9},{9,8},{10,11... | collective-permute-start | bytes 1622024 | tf_op jit(solution)/shard_map/ppermute | solution.py:752
  34.7 68.7 %collective-permute-start.12 = (f32[256,512]{1,0:T(8,128)S(1)}, f32[256,512]{1,0:T(8,128)S(1)}, u32[]{:S(2)}, u32[]{:S(2)}) collective-permute-start(f32[256,512]{1,0:T(8,128)S(1)} %get-tuple-element.66), channel_id=1, source_target_pairs={{1,2},{2,1},{5,6},{6,5},{9,10},{10,9},{13,14},{14,13},{17,18},{18,... | collective-permute-start | bytes 1572872 | tf_op jit(solution)/shard_map/ppermute | solution.py:784
  49.7 53.7 %collective-permute-start.13 = (f32[256,512]{1,0:T(8,128)S(1)}, f32[256,512]{1,0:T(8,128)S(1)}, u32[]{:S(2)}, u32[]{:S(2)}) collective-permute-start(f32[256,512]{1,0:T(8,128)S(1)} %get-tuple-element.66), channel_id=1, source_target_pairs={{0,3},{3,0},{4,7},{7,4},{8,11},{11,8},{12,15},{15,12},{16,19},{19,... | collective-permute-start | bytes 1572872 | tf_op jit(solution)/shard_map/ppermute | solution.py:784
  56.0 37.9 %collective-permute-start.5 = (f32[144,512]{1,0:T(8,128)S(1)}, f32[144,512]{1,0:T(8,128)S(1)}, u32[]{:S(2)}, u32[]{:S(2)}) collective-permute-start(f32[144,512]{1,0:T(8,128)S(1)} %add.23), channel_id=1, source_target_pairs={{0,2},{1,3},{2,0},{3,1},{4,6},{5,7},{6,4},{7,5},{8,10},{9,11},{10,... | collective-permute-start | bytes 884744 | tf_op jit(solution)/shard_map/ppermute | solution.py:752
  93.9 5.4 %collective-permute-start.11 = (f32[8,256]{1,0:T(8,128)S(1)}, f32[8,256]{1,0:T(8,128)S(1)}, u32[]{:S(2)}, u32[]{:S(2)}) collective-permute-start(f32[8,256]{1,0:T(8,128)S(1)} %slice.11), channel_id=1, source_target_pairs={{0,3},{1,2},{2,1},{3,0},{4,7},{5,6},{6,5},{7,4},{8,11},{9,10},{10,... | collective-permute-start | bytes 24584 | tf_op jit(solution)/shard_map/ppermute | solution.py:752
  99.4 4.1 %collective-permute-start.7 = (f32[32,768]{1,0:T(8,128)S(1)}, f32[32,768]{1,0:T(8,128)S(1)}, u32[]{:S(2)}, u32[]{:S(2)}) collective-permute-start(f32[32,768]{1,0:T(8,128)S(1)} %get-tuple-element.57), channel_id=1, source_target_pairs={{0,4},{8,12},{16,20},{24,28},{4,0},{12,8},{20,16},{28,24},{1,5},{9... | collective-permute-start | bytes 294920 | tf_op jit(solution)/shard_map/ppermute | solution.py:746
  99.4 5.9 %collective-permute-start.8 = (f32[32,768]{1,0:T(8,128)S(1)}, f32[32,768]{1,0:T(8,128)S(1)}, u32[]{:S(2)}, u32[]{:S(2)}) collective-permute-start(f32[32,768]{1,0:T(8,128)S(1)} %get-tuple-element.58), channel_id=1, source_target_pairs={{4,8},{12,16},{20,24},{8,4},{16,12},{24,20},{5,9},{13,17},{21,25},... | collective-permute-start | bytes 294920 | tf_op jit(solution)/shard_map/ppermute | solution.py:746
  114.7 3.4 %collective-permute-start.14 = (f32[64,640]{1,0:T(8,128)S(1)}, f32[64,640]{1,0:T(8,128)S(1)}, u32[]{:S(2)}, u32[]{:S(2)}) collective-permute-start(f32[64,640]{1,0:T(8,128)S(1)} %get-tuple-element.68.send_a), channel_id=1, source_target_pairs={{0,4},{8,12},{16,20},{24,28},{4,0},{12,8},{20,16},{28,24},{1,5},{9... | collective-permute-start | bytes 491528 | tf_op jit(solution)/shard_map/ppermute | solution.py:746
  116.1 6.6 %collective-permute-start.15 = (f32[64,640]{1,0:T(8,128)S(1)}, f32[64,640]{1,0:T(8,128)S(1)}, u32[]{:S(2)}, u32[]{:S(2)}) collective-permute-start(f32[64,640]{1,0:T(8,128)S(1)} %get-tuple-element.70.send_b), channel_id=1, source_target_pairs={{4,8},{12,16},{20,24},{8,4},{16,12},{24,20},{5,9},{13,17},{21,25},... | collective-permute-start | bytes 491528 | tf_op jit(solution)/shard_map/ppermute | solution.py:746
  123.4 5.7 %collective-permute-start.16 = (f32[192,128]{1,0:T(8,128)S(1)}, f32[192,128]{1,0:T(8,128)S(1)}, u32[]{:S(2)}, u32[]{:S(2)}) collective-permute-start(f32[192,128]{1,0:T(8,128)S(1)} %get-tuple-element.72), channel_id=1, source_target_pairs={{0,1},{2,3},{1,0},{3,2},{4,5},{6,7},{5,4},{7,6},{8,9},{10,11},{9,8... | collective-permute-start | bytes 294920 | tf_op jit(solution)/shard_map/ppermute | solution.py:746
  123.5 5.6 %collective-permute-start.17 = (f32[192,128]{1,0:T(8,128)S(1)}, f32[192,128]{1,0:T(8,128)S(1)}, u32[]{:S(2)}, u32[]{:S(2)}) collective-permute-start(f32[192,128]{1,0:T(8,128)S(1)} %get-tuple-element.73), channel_id=1, source_target_pairs={{1,2},{2,1},{5,6},{6,5},{9,10},{10,9},{13,14},{14,13},{17,18},{18,... | collective-permute-start | bytes 294920 | tf_op jit(solution)/shard_map/ppermute | solution.py:746
  139.3 5.7 %collective-permute-start.29 = (f32[32,640]{1,0:T(8,128)S(1)}, f32[32,640]{1,0:T(8,128)S(1)}, u32[]{:S(2)}, u32[]{:S(2)}) collective-permute-start(f32[32,640]{1,0:T(8,128)S(1)} %get-tuple-element.83.send_a), channel_id=1, source_target_pairs={{0,4},{8,12},{16,20},{24,28},{4,0},{12,8},{20,16},{28,24},{1,5},{9... | collective-permute-start | bytes 245768 | tf_op jit(solution)/shard_map/ppermute | solution.py:746
  139.5 5.7 %collective-permute-start.30 = (f32[32,640]{1,0:T(8,128)S(1)}, f32[32,640]{1,0:T(8,128)S(1)}, u32[]{:S(2)}, u32[]{:S(2)}) collective-permute-start(f32[32,640]{1,0:T(8,128)S(1)} %get-tuple-element.85.send_b), channel_id=1, source_target_pairs={{4,8},{12,16},{20,24},{8,4},{16,12},{24,20},{5,9},{13,17},{21,25},... | collective-permute-start | bytes 245768 | tf_op jit(solution)/shard_map/ppermute | solution.py:746
  141.4 9.2 %collective-permute-start.18 = (f32[4,8,128]{2,1,0:T(8,128)S(1)}, f32[4,8,128]{2,1,0:T(8,128)S(1)}, u32[]{:S(2)}, u32[]{:S(2)}) collective-permute-start(f32[4,8,128]{2,1,0:T(8,128)S(1)} %pad_maximum_fusion), channel_id=1, source_target_pairs={{0,1},{1,0},{2,3},{3,2},{4,5},{5,4},{6,7},{7,6},{8,9},{9,8},{10,11... | collective-permute-start | bytes 49160 | tf_op jit(solution)/shard_map/ppermute | solution.py:752
  145.9 36.2 %collective-permute-start.32 = (f32[144,512]{1,0:T(8,128)S(1)}, f32[144,512]{1,0:T(8,128)S(1)}, u32[]{:S(2)}, u32[]{:S(2)}) collective-permute-start(f32[144,512]{1,0:T(8,128)S(1)} %wrap.1.refs_0_), channel_id=1, source_target_pairs={{0,2},{1,3},{2,0},{3,1},{4,6},{5,7},{6,4},{7,5},{8,10},{9,11},{10,... | collective-permute-start | bytes 884744 | tf_op jit(solution)/shard_map/ppermute | solution.py:752
  150.6 14.2 %collective-permute-start.19 = (f32[4,8,128]{2,1,0:T(8,128)S(1)}, f32[4,8,128]{2,1,0:T(8,128)S(1)}, u32[]{:S(2)}, u32[]{:S(2)}) collective-permute-start(f32[4,8,128]{2,1,0:T(8,128)S(1)} %fusion), channel_id=1, source_target_pairs={{0,2},{1,3},{2,0},{3,1},{4,6},{5,7},{6,4},{7,5},{8,10},{9,11},{10,... | collective-permute-start | bytes 49160 | tf_op jit(solution)/shard_map/ppermute | solution.py:752
  150.7 33.5 %collective-permute-start.23 = (f32[128,512]{1,0:T(8,128)S(1)}, f32[128,512]{1,0:T(8,128)S(1)}, u32[]{:S(2)}, u32[]{:S(2)}) collective-permute-start(f32[128,512]{1,0:T(8,128)S(1)} %get-tuple-element.78.refs_0_), channel_id=1, source_target_pairs={{0,1},{1,0},{2,3},{3,2},{4,5},{5,4},{6,7},{7,6},{8,9},{9,8},{10,11... | collective-permute-start | bytes 786440 | tf_op jit(solution)/shard_map/ppermute | solution.py:752
  152.6 33.0 %collective-permute-start.24 = (f32[128,512]{1,0:T(8,128)S(1)}, f32[128,512]{1,0:T(8,128)S(1)}, u32[]{:S(2)}, u32[]{:S(2)}) collective-permute-start(f32[128,512]{1,0:T(8,128)S(1)} %get-tuple-element.78.refs_0_), channel_id=1, source_target_pairs={{0,2},{1,3},{2,0},{3,1},{4,6},{5,7},{6,4},{7,5},{8,10},{9,11},{10,... | collective-permute-start | bytes 786440 | tf_op jit(solution)/shard_map/ppermute | solution.py:752
  153.6 32.0 %collective-permute-start.25 = (f32[128,512]{1,0:T(8,128)S(1)}, f32[128,512]{1,0:T(8,128)S(1)}, u32[]{:S(2)}, u32[]{:S(2)}) collective-permute-start(f32[128,512]{1,0:T(8,128)S(1)} %get-tuple-element.78.refs_0_), channel_id=1, source_target_pairs={{0,3},{1,2},{2,1},{3,0},{4,7},{5,6},{6,5},{7,4},{8,11},{9,10},{10,... | collective-permute-start | bytes 786440 | tf_op jit(solution)/shard_map/ppermute | solution.py:752
  164.8 13.6 %collective-permute-start.20 = (f32[4,8,128]{2,1,0:T(8,128)S(1)}, f32[4,8,128]{2,1,0:T(8,128)S(1)}, u32[]{:S(2)}, u32[]{:S(2)}) collective-permute-start(f32[4,8,128]{2,1,0:T(8,128)S(1)} %fusion.1), channel_id=1, source_target_pairs={{0,4},{4,0},{8,12},{12,8},{16,20},{20,16},{24,28},{28,24},{1,5},{5... | collective-permute-start | bytes 49160 | tf_op jit(solution)/shard_map/ppermute | solution.py:752
  178.4 3.7 %collective-permute-start.21 = (f32[4,8,128]{2,1,0:T(8,128)S(1)}, f32[4,8,128]{2,1,0:T(8,128)S(1)}, u32[]{:S(2)}, u32[]{:S(2)}) collective-permute-start(f32[4,8,128]{2,1,0:T(8,128)S(1)} %add.26), channel_id=1, source_target_pairs={{0,8},{4,12},{8,0},{12,4},{16,24},{20,28},{24,16},{28,20},{1,9},{5... | collective-permute-start | bytes 49160 | tf_op jit(solution)/shard_map/ppermute | solution.py:752
  182.1 33.6 %collective-permute-start.31 = (f32[144,512]{1,0:T(8,128)S(1)}, f32[144,512]{1,0:T(8,128)S(1)}, u32[]{:S(2)}, u32[]{:S(2)}) collective-permute-start(f32[144,512]{1,0:T(8,128)S(1)} %wrap.1.refs_0_), channel_id=1, source_target_pairs={{0,1},{1,0},{2,3},{3,2},{4,5},{5,4},{6,7},{7,6},{8,9},{9,8},{10,11... | collective-permute-start | bytes 884744 | tf_op jit(solution)/shard_map/ppermute | solution.py:752
  182.1 33.6 %collective-permute-start.33 = (f32[144,512]{1,0:T(8,128)S(1)}, f32[144,512]{1,0:T(8,128)S(1)}, u32[]{:S(2)}, u32[]{:S(2)}) collective-permute-start(f32[144,512]{1,0:T(8,128)S(1)} %collective-permute-done.32.refs_2_), channel_id=1, source_target_pairs={{0,1},{1,0},{2,3},{3,2},{4,5},{5,4},{6,7},{7,6},{8,9},{9,8},{10,11... | collective-permute-start | bytes 884744 | tf_op jit(solution)/shard_map/ppermute | solution.py:752
  184.2 3.8 %collective-permute-start.22 = (f32[4,8,128]{2,1,0:T(8,128)S(1)}, f32[4,8,128]{2,1,0:T(8,128)S(1)}, u32[]{:S(2)}, u32[]{:S(2)}) collective-permute-start(f32[4,8,128]{2,1,0:T(8,128)S(1)} %add.27), channel_id=1, source_target_pairs={{0,16},{4,20},{8,24},{12,28},{16,0},{20,4},{24,8},{28,12},{1,17},{... | collective-permute-start | bytes 49160 | tf_op jit(solution)/shard_map/ppermute | solution.py:752
  185.5 28.2 %collective-permute-start.26 = (f32[128,512]{1,0:T(8,128)S(1)}, f32[128,512]{1,0:T(8,128)S(1)}, u32[]{:S(2)}, u32[]{:S(2)}) collective-permute-start(f32[128,512]{1,0:T(8,128)S(1)} %get-tuple-element.79.refs_4_.before), channel_id=1, source_target_pairs={{0,1},{1,0},{2,3},{3,2},{4,5},{5,4},{6,7},{7,6},{8,9},{9,8},{10,11... | collective-permute-start | bytes 786440 | tf_op jit(solution)/shard_map/ppermute | solution.py:752
  185.6 28.1 %collective-permute-start.27 = (f32[128,512]{1,0:T(8,128)S(1)}, f32[128,512]{1,0:T(8,128)S(1)}, u32[]{:S(2)}, u32[]{:S(2)}) collective-permute-start(f32[128,512]{1,0:T(8,128)S(1)} %get-tuple-element.79.refs_4_.before), channel_id=1, source_target_pairs={{0,2},{1,3},{2,0},{3,1},{4,6},{5,7},{6,4},{7,5},{8,10},{9,11},{10,... | collective-permute-start | bytes 786440 | tf_op jit(solution)/shard_map/ppermute | solution.py:752
  188.0 25.7 %collective-permute-start.28 = (f32[128,512]{1,0:T(8,128)S(1)}, f32[128,512]{1,0:T(8,128)S(1)}, u32[]{:S(2)}, u32[]{:S(2)}) collective-permute-start(f32[128,512]{1,0:T(8,128)S(1)} %get-tuple-element.79.refs_4_.before), channel_id=1, source_target_pairs={{0,3},{1,2},{2,1},{3,0},{4,7},{5,6},{6,5},{7,4},{8,11},{9,10},{10,... | collective-permute-start | bytes 786440 | tf_op jit(solution)/shard_map/ppermute | solution.py:752

commit v4 on v3

--- a/solution.py
+++ b/solution.py
@@ -452,44 +452,55 @@
     )(place, est, *parts)
 
 
-def apply_kernel(frames, rows, halo, w, groups, cut, count, pieces, place, *refs):
+def apply_kernel(n, frames, rows, halo, w, slots, cut, count, pieces, carried, place, *refs):
     image, refs = refs[:pieces], refs[pieces:]
     t_hbm, b_hbm, bp_hbm, ta_hbm, own = refs[:5]
-    moved = refs[5 : 5 + count]
-    send_a, mid, send_b, stat = refs[5 + count : 9 + count]
-    refs = refs[9 + count :]
+    moved, refs = refs[5 : 5 + count], refs[5 + count :]
+    if carried:
+        (acc_in, stat_in), refs = refs[:2], refs[2:]
+    if cut is None:
+        (acc_out, stat), refs = refs[:2], refs[2:]
+    else:
+        (send_a, mid, send_b, stat), refs = refs[:4], refs[4:]
     if pieces > 1:
         whole, refs = refs[0], refs[1:]
     y_hi, y_lo, us, qs, vs_hi, vs_lo, acc, tb, bb, bpb, tab, wbuf, sem, wsem = refs
     odd = lax.rem(place[1], 2)
     ext = rows + 2 * halo
-
-    def copies(g):
+    quarter = n // 4
+    inner = ((place[0] >= quarter) & (place[0] < n - quarter)).astype(jnp.int32)
+
+    def copies(i, g):
         span = pl.ds(g * frames, frames)
         return [
-            pltpu.make_async_copy(t_hbm.at[span], tb.at[g], sem.at[0, g]),
-            pltpu.make_async_copy(b_hbm.at[span], bb.at[g], sem.at[1, g]),
-            pltpu.make_async_copy(bp_hbm.at[span], bpb.at[g], sem.at[2, g]),
-            pltpu.make_async_copy(ta_hbm.at[g], tab.at[g], sem.at[3, g]),
+            pltpu.make_async_copy(t_hbm.at[span], tb.at[i], sem.at[0, i]),
+            pltpu.make_async_copy(b_hbm.at[span], bb.at[i], sem.at[1, i]),
+            pltpu.make_async_copy(bp_hbm.at[span], bpb.at[i], sem.at[2, i]),
+            pltpu.make_async_copy(ta_hbm.at[g], tab.at[i], sem.at[3, i]),
         ]
 
     mine = pl.ds(pl.multiple_of(place[0] * w, LANE), w)
-    for g in range(groups):
-        for c in copies(g):
+    for i, (distance, late, sources) in enumerate(slots):
+        if len(sources) == 2:
+            group = distance + (1 - inner if late else inner) * quarter
+        else:
+            group = distance
+        for c in copies(i, group):
             c.start()
         for f in range(frames):
             span = pl.ds(f * rows, rows)
-            if g == 0:
-                pltpu.make_async_copy(own.at[f, :, mine], wbuf.at[g, f], wsem.at[g, f]).start()
-            elif g < groups - 1:
-                pltpu.make_async_copy(moved[g - 1].at[span, :], wbuf.at[g, f], wsem.at[g, f]).start()
+            if not sources:
+                pltpu.make_async_copy(own.at[f, :, mine], wbuf.at[i, f], wsem.at[i, f]).start()
+            elif len(sources) == 1:
+                source = moved[sources[0]].at[span, :]
+                pltpu.make_async_copy(source, wbuf.at[i, f], wsem.at[i, f]).start()
             else:
-                inside = (place[0] >= groups // 4) & (place[0] < groups - groups // 4)
-                for flag, ref in ((inside, moved[-2]), (jnp.logical_not(inside), moved[-1])):
-
-                    @pl.when(flag)
-                    def _(ref=ref, span=span, g=g, f=f):
-                        pltpu.make_async_copy(ref.at[span, :], wbuf.at[g, f], wsem.at[g, f]).start()
+                for k in range(2):
+
+                    @pl.when((group - distance) == k * quarter)
+                    def _(source=moved[sources[k]].at[span, :], i=i, f=f):
+                        pltpu.make_async_copy(source, wbuf.at[i, f], wsem.at[i, f]).start()
+
     clear_edges(y_hi, y_lo, qs, ext, rows, w)
     if pieces > 1:
         wide, recv_a, recv_b = image
@@ -499,61 +510,67 @@
         load_image(y_hi, y_lo, whole[...], halo)
     else:
         load_image(y_hi, y_lo, image[0][...], halo)
-    acc[...] = jnp.zeros_like(acc)
-    stat[...] = jnp.zeros_like(stat)
-
-    @pl.loop(0, groups)
-    def _(g):
-        for c in copies(g):
+    acc[...] = acc_in[...] if carried else jnp.zeros_like(acc)
+    stat[...] = stat_in[...] if carried else jnp.zeros_like(stat)
+
+    @pl.loop(0, len(slots))
+    def _(i):
+        for c in copies(i, 0):
             c.wait()
         for f in range(frames):
-            pltpu.make_async_copy(own.at[f, :, mine], wbuf.at[g, f], wsem.at[g, f]).wait()
+            pltpu.make_async_copy(own.at[f, :, mine], wbuf.at[i, f], wsem.at[i, f]).wait()
         group_terms(
             frames, rows, w, y_hi, y_lo,
-            lambda f: tb.at[g, f], lambda f: bb.at[g, f], lambda f: bpb.at[g, f], tab.at[g],
-            lambda f: wbuf.at[g, f], None,
+            lambda f: tb.at[i, f], lambda f: bb.at[i, f], lambda f: bpb.at[i, f], tab.at[i],
+            lambda f: wbuf.at[i, f], None,
             us, qs, vs_hi, vs_lo, acc, stat,
         )
 
-    z = unshift(acc[...], halo)
-    send_a[...] = choose(odd, z[:cut], z[ext - cut :])
-    send_b[...] = choose(odd, z[ext - cut :], z[:cut])
-    mid[...] = z[cut : ext - cut]
-
-
-def apply_terms(place, image, mats, weights, moved, cut, halo):
+    if cut is None:
+        acc_out[...] = acc[...]
+    else:
+        z = unshift(acc[...], halo)
+        send_a[...] = choose(odd, z[:cut], z[ext - cut :])
+        send_b[...] = choose(odd, z[ext - cut :], z[:cut])
+        mid[...] = z[cut : ext - cut]
+
+
+def apply_terms(n, place, image, mats, weights, moved, slots, cut, halo, carry=()):
     frames, rows, _ = weights.shape
     w = image[0].shape[1] - 2 * LANE
     ext = rows + 2 * halo
     t, b, bp, ta = mats
-    groups = ta.shape[0]
+    count = len(slots)
     wide = w + LANE
-    return pl.pallas_call(
-        functools.partial(apply_kernel, frames, rows, halo, w, groups, cut, len(moved), len(image)),
-        out_shape=[
-            jax.ShapeDtypeStruct((cut, wide), f32),
-            jax.ShapeDtypeStruct((ext - 2 * cut, wide), f32),
-            jax.ShapeDtypeStruct((cut, wide), f32),
-            jax.ShapeDtypeStruct((8, LANE), f32),
-        ]
-        + [jax.ShapeDtypeStruct((ext, w + 2 * LANE), f32)] * (len(image) > 1),
-        in_specs=[SMEM] + [VMEM] * len(image) + [ANY] * 4 + [HBM] + [ANY] * len(moved),
-        out_specs=[VMEM] * (4 + (len(image) > 1)),
+    shapes = [(ext, wide)] if cut is None else [(cut, wide), (ext - 2 * cut, wide), (cut, wide)]
+    shapes += [(8, LANE)] + [(ext, w + 2 * LANE)] * (len(image) > 1)
+    return pl.pallas_call(
+        functools.partial(
+            apply_kernel, n, frames, rows, halo, w, slots, cut, len(moved), len(image), bool(carry)
+        ),
+        out_shape=[jax.ShapeDtypeStruct(s, f32) for s in shapes],
+        in_specs=[SMEM]
+        + [VMEM] * len(image)
+        + [ANY] * 4
+        + [HBM]
+        + [ANY] * len(moved)
+        + [VMEM] * len(carry),
+        out_specs=[VMEM] * len(shapes),
         scratch_shapes=work_scratch(frames, rows, halo, w)
         + [
-            pltpu.VMEM((groups, frames) + t.shape[1:], bf16),
-            pltpu.VMEM((groups, frames) + b.shape[1:], bf16),
-            pltpu.VMEM((groups, frames) + bp.shape[1:], bf16),
-            pltpu.VMEM((groups,) + ta.shape[1:], bf16),
-            pltpu.VMEM((groups, frames, rows, w), f32),
-            pltpu.SemaphoreType.DMA((4, groups)),
-            pltpu.SemaphoreType.DMA((groups, frames)),
+            pltpu.VMEM((count, frames) + t.shape[1:], bf16),
+            pltpu.VMEM((count, frames) + b.shape[1:], bf16),
+            pltpu.VMEM((count, frames) + bp.shape[1:], bf16),
+            pltpu.VMEM((count,) + ta.shape[1:], bf16),
+            pltpu.VMEM((count, frames, rows, w), f32),
+            pltpu.SemaphoreType.DMA((4, count)),
+            pltpu.SemaphoreType.DMA((count, frames)),
         ],
         cost_estimate=pl.CostEstimate(
-            flops=groups * 3 * 10**9, bytes_accessed=groups * 2**20, transcendentals=0
+            flops=count * 3 * 10**9, bytes_accessed=count * 2**20, transcendentals=0
         ),
         compiler_params=room(28),
-    )(place, *image, t, b, bp, ta, weights, *moved)
+    )(place, *image, t, b, bp, ta, weights, *moved, *carry)
 
 
 def rows_kernel(strips, halo, w, place, send_a, mid, send_b, recv_a, recv_b, q, col_a, col_b):
@@ -773,21 +790,36 @@
         jnp.where(odd, low, high), jnp.where(odd, high, low), "strip"
     )
 
-    plan = [(d, True) for d in range(1, n - 1)] + [(n - 1, False)]
+    half, quarter = n // 2, n // 4
+    plan = [(d, d < half) for d in range(1, n)]
     packed, tile, own_mats = prepare(plan, place, column_kernels, row_kernels, weights, w, halo)
-    far_tile = swap(tile[:, : 2 * LANE], "frame", n - 1)
+    far_tiles = []
+    for d in range(half, n):
+        far_tiles.append(swap(tile[:, : 2 * LANE], "frame", d))
     moved = []
-    for i in range(n - 2):
-        moved.append(swap(packed[i], "frame", i + 1))
-    middle = range(n // 4, n - n // 4)
-    for members in (middle, [i for i in range(n) if i not in middle]):
-        moved.append(lax.ppermute(packed[-1], "frame", [(i, n - 1 - i) for i in members]))
-    starts = [0] + [frames * rows] * (n - 2) + [0]
+    slots = [(0, False, ())]
+    for d in range(1, half):
+        moved.append(swap(packed[d - 1], "frame", d))
+        slots.append((d, False, (d - 1,)))
+    middle = range(quarter, n - quarter)
+    where = {}
+    for late in (False, True):
+        for d in range(half, n):
+            pairs = [(i, i ^ d) for i in range(n) if (i in middle) != late]
+            where[d, late] = len(moved)
+            moved.append(lax.ppermute(packed[d - 1], "frame", pairs))
+    late_slots = []
+    for late, out in ((False, slots), (True, late_slots)):
+        for u in range(half, half + quarter):
+            out.append((u, late, (where[u, late], where[u + quarter, late])))
+    starts = [0] + [frames * rows] * (half - 1) + [0] * half
 
     send_a, mid, send_b = first_terms(
         place, estimate, est_a, est_b, own_mats, weights, observed
     )
-    mats = setup_matrices([tile] + moved[: n - 2] + [far_tile], starts, frames, rows, halo)
+    mats = setup_matrices(
+        [tile] + moved[: half - 1] + far_tiles, starts, frames, rows, halo
+    )
     recv_a, recv_b = neighbours(send_a, send_b, "strip")
 
     part = list(column_blocks(n, place, send_a, mid, send_b, recv_a, recv_b, w))
@@ -802,15 +834,22 @@
     k0, wide, send_a, send_b, k00_part = start_image(n, place, estimate, mine, halo)
     recv_a, recv_b = neighbours(send_a, send_b, "strip")
 
-    send_a, mid, send_b, stat1, k0x = apply_terms(
-        place, (wide, recv_a, recv_b), mats, weights, moved, 2 * halo, halo
+    acc, stat1, k0x = apply_terms(
+        n, place, (wide, recv_a, recv_b), mats, weights, moved[: where[half, True]],
+        slots, None, halo,
+    )
+    send_a, mid, send_b, stat1 = apply_terms(
+        n, place, (k0x,), mats, weights, moved, late_slots, 2 * halo, halo,
+        carry=(acc, stat1),
     )
     recv_a, recv_b = neighbours(send_a, send_b, "strip")
     q, col_a, col_b = merge_rows(strips, place, send_a, mid, send_b, recv_a, recv_b, halo)
     recv_a, recv_b = neighbours(col_a, col_b, "frame")
     k1x, k1, k11_part = merge_cols(n, rows, place, q, recv_a, recv_b, k0x, halo)
 
-    send_a, mid, send_b, stat2 = apply_terms(place, (k1x,), mats, weights, moved, halo, halo)
+    send_a, mid, send_b, stat2 = apply_terms(
+        n, place, (k1x,), mats, weights, moved, slots + late_slots, halo, halo
+    )
     recv_a, recv_b = neighbours(send_a, send_b, "strip")
     sums = jnp.stack([k00_part, stat1, k11_part, stat2])
     for axis, size in (("frame", n), ("strip", strips)):

time: 219 us -> 216 us (0.986)
  waiting for transfers between devices: 118 us -> 104 us
  starting transfers between devices: 60 us -> 70.2 us
    ppermute x20, waiting for transfers between devices: 96.5 us -> 73.1 us  [swap(): return lax.ppermute(x, axis, [(i, i ^ distance) for i in range(n)])]
    ppermute x2 -> x4, waiting for transfers between devices: 0.01 us -> 11.3 us  [steps(): moved.append(lax.ppermute(packed[d - 1], 'frame', pairs))]
    ppermute x2 -> x4, starting transfers between devices: 3.2 us -> 9.05 us  [steps(): moved.append(lax.ppermute(packed[d - 1], 'frame', pairs))]
    ppermute x20, starting transfers between devices: 41.2 us -> 45.7 us  [swap(): return lax.ppermute(x, axis, [(i, i ^ distance) for i in range(n)])]
    pallas_call x2 -> x3, Pallas kernels: 18.8 us -> 19.6 us  [apply_terms(): pl.pallas_call(functools.partial(apply_kernel, n, frames, rows, halo, w,...]
  transfers between devices with their start and end apart: 34 -> 36, of which waited for: 15 -> 15; matrix products, arithmetic and copies ran while one was open for 0% -> 0% of each run, Pallas kernels for 4% -> 7%
where the time goes in v4:
time: 216 us; the launch traced here: 215 us
  waiting for transfers between devices  104 us (48%)
  starting transfers between devices  70.2 us (32%)
  Pallas kernels  37.9 us (18%)
    ppermute x20, waiting for transfers between devices, swap(): return lax.ppermute(x, axis, [(i, i ^ distance) for i in range(n)])  73.1 us
    ppermute x20, starting transfers between devices, swap(): return lax.ppermute(x, axis, [(i, i ^ distance) for i in range(n)])  45.7 us
    ppermute x12, waiting for transfers between devices, neighbours(): out.append(lax.ppermute(x, axis, pairs + [(b, a) for a, b in pairs]))  19.8 us
    pallas_call x3, Pallas kernels, apply_terms(): pl.pallas_call(functools.partial(apply_kernel, n, frames, rows, halo, w,...  19.6 us
    ppermute x12, starting transfers between devices, neighbours(): out.append(lax.ppermute(x, axis, pairs + [(b, a) for a, b in pairs]))  15.5 us
    ppermute x4, waiting for transfers between devices, steps(): moved.append(lax.ppermute(packed[d - 1], 'frame', pairs))  11.3 us
    ppermute x4, starting transfers between devices, steps(): moved.append(lax.ppermute(packed[d - 1], 'frame', pairs))  9.05 us
    pallas_call x1, Pallas kernels, first_terms(): pl.pallas_call(functools.partial(first_kernel, frames, rows, halo), out_s...  6.47 us
  transfers between devices with their start and end apart: 36, of which 15 were waited for; matrix products, arithmetic and copies ran while one was open for 0% of the time, Pallas kernels for 7%

profile of v4, /device:TPU:2, one launch (start us, length us, event | category | flops | bytes accessed | tf_op | source)
XLA Modules:
  0.0 214.6 jit_solution(12027078793198554427)
XLA Ops:
  0.7 1.2 slice_select_fusion
  1.9 1.9 collective-permute-start.1
  3.9 2.2 %prepare.1 = (f32[264,512]{1,0:T(8,128)S(1)}, f32[256,512]{1,0:T(8,128)S(1)}, f32[256,512]{1,0:T(8,128)S(1)}, f32[8,512]{1,0:T(8,128)S(1)}, bf16[2,256,256]{2,1,...) custom-call(s32[2]{0:T(128)S(1)} %pad_add_fusion.place, ...), custom_call_target="tpu_custom_call" | custom-call | tf_op jit(solution)/shard_map/prepare/pallas_call | solution.py:350
  6.1 3.4 %collective-permute-done.1.recv_b = f32[32,2048]{1,0:T(8,128)S(1)} collective-permute-done((f32[32,2048]{1,0:T(8,128)S(1)}, f32[32,2048]{1,0:T(8,128)S(1)}, u32[]{:S(2)}, u32[]{:S(2)}) %collective-permute-start.1) | collective-permute-done | bytes 262176 | tf_op jit(solution)/shard_map/ppermute | solution.py:763
  9.6 6.5 %first_terms.1 = (f32[32,2048]{1,0:T(8,128)S(1)}, f32[128,2048]{1,0:T(8,128)S(1)}, f32[32,2048]{1,0:T(8,128)S(1)}) custom-call(s32[2]{0:T(128)S(1)} %pad_add_fusion.place, f32[128,2048]{1,0:T(8,128)S(1)} %copy-done, f32[32,2048]{1,0:T(8,128)S(1)} %collective-permute-done.recv_a, f32[32,2048]{1,0:T(8,128)S(1)} %collective-permute-done.1.recv_b, ...), custom_call_target="tpu_custom_call" | custom-call | flops 8000000000 | bytes 8388608 | tf_op jit(solution)/shard_map/first_terms/pallas_call | solution.py:292
  16.1 3.6 %collective-permute-start.2 = (f32[32,2048]{1,0:T(8,128)S(1)}, f32[32,2048]{1,0:T(8,128)S(1)}, u32[]{:S(2)}, u32[]{:S(2)}) collective-permute-start(f32[32,2048]{1,0:T(8,128)S(1)} %get-tuple-element.50.send_a), channel_id=1, source_target_pairs={{0,4},{8,12},{16,20},{24,28},{4,0},{12,8},{20,16},{28,24},{1,5},{9... | collective-permute-start | bytes 786440 | tf_op jit(solution)/shard_map/ppermute | solution.py:763
  19.7 1.9 collective-permute-start.3
  21.6 6.5 %collective-permute-done.3.recv_b = f32[32,2048]{1,0:T(8,128)S(1)} collective-permute-done((f32[32,2048]{1,0:T(8,128)S(1)}, f32[32,2048]{1,0:T(8,128)S(1)}, u32[]{:S(2)}, u32[]{:S(2)}) %collective-permute-start.3) | collective-permute-done | bytes 262176 | tf_op jit(solution)/shard_map/ppermute | solution.py:763
  28.2 0.9 column_blocks.1
  29.1 1.0 collective-permute-start.4
  30.1 1.1 collective-permute-start.9
  31.2 1.3 collective-permute-start.12
  33.2 5.5 %collective-permute-start.6 = (f32[144,512]{1,0:T(8,128)S(1)}, f32[144,512]{1,0:T(8,128)S(1)}, u32[]{:S(2)}, u32[]{:S(2)}) collective-permute-start(f32[144,512]{1,0:T(8,128)S(1)} %get-tuple-element.56), channel_id=1, source_target_pairs={{0,1},{1,0},{2,3},{3,2},{4,5},{5,4},{6,7},{7,6},{8,9},{9,8},{10,11... | collective-permute-start | bytes 884744 | tf_op jit(solution)/shard_map/ppermute | solution.py:769
  38.7 11.1 %collective-permute-done.4 = f32[144,512]{1,0:T(8,128)S(1)} collective-permute-done((f32[144,512]{1,0:T(8,128)S(1)}, f32[144,512]{1,0:T(8,128)S(1)}, u32[]{:S(2)}, u32[]{:S(2)}) %collective-permute-start.4) | collective-permute-done | bytes 294944 | tf_op jit(solution)/shard_map/ppermute | solution.py:769
  49.9 24.1 %collective-permute-done.6.refs_2_ = f32[144,512]{1,0:T(8,128)S(1)} collective-permute-done((f32[144,512]{1,0:T(8,128)S(1)}, f32[144,512]{1,0:T(8,128)S(1)}, u32[]{:S(2)}, u32[]{:S(2)}) %collective-permute-start.6) | collective-permute-done | bytes 294944 | tf_op jit(solution)/shard_map/ppermute | solution.py:769
  74.2 2.1 collective-permute-start.11
  77.0 1.5 collective-permute-done.10.refs_2_
  78.5 1.1 collective-permute-done.11.refs_3_
  79.7 1.9 collective-permute-start.8
  81.6 2.8 %collective-permute-start.14 = (f32[256,512]{1,0:T(8,128)S(1)}, f32[256,512]{1,0:T(8,128)S(1)}, u32[]{:S(2)}, u32[]{:S(2)}) collective-permute-start(f32[256,512]{1,0:T(8,128)S(1)} %get-tuple-element.67), channel_id=1, source_target_pairs={{0,2},{3,1},{4,6},{7,5},{8,10},{11,9},{12,14},{15,13},{16,18},{19,... | collective-permute-start | bytes 1572872 | tf_op jit(solution)/shard_map/ppermute | solution.py:810
  84.4 2.1 setup_all.1
  86.5 4.2 %collective-permute-start.15 = (f32[256,512]{1,0:T(8,128)S(1)}, f32[256,512]{1,0:T(8,128)S(1)}, u32[]{:S(2)}, u32[]{:S(2)}) collective-permute-start(f32[256,512]{1,0:T(8,128)S(1)} %get-tuple-element.68), channel_id=1, source_target_pairs={{0,3},{3,0},{4,7},{7,4},{8,11},{11,8},{12,15},{15,12},{16,19},{19,... | collective-permute-start | bytes 1572872 | tf_op jit(solution)/shard_map/ppermute | solution.py:810
  90.8 7.1 %shard_map.68 = (f32[192,640]{1,0:T(8,128)S(1)}, f32[8,128]{1,0:T(8,128)S(1)}, f32[192,768]{1,0:T(8,128)S(1)}) custom-call(s32[2]{0:T(128)S(1)} %pad_add_fusion.place, f32[128,768]{1,0:T(8,128)S(1)} %get-tuple-element.58.refs_0_, f32[32,768]{1,0:T(8,128)S(1)} %collective-permute-done.7.refs_1_, f32[32,768]{1,0:T(8,128)S(1)} %collective-permute-done.8.refs_2_, ...), custom_call_target="tpu_custom_call" | custom-call | flops 8999999488 | bytes 3145728 | tf_op jit(solution)/shard_map/pallas_call | solution.py:547
  98.0 11.3 %collective-permute-done.15.refs_10_ = f32[256,512]{1,0:T(8,128)S(1)} collective-permute-done((f32[256,512]{1,0:T(8,128)S(1)}, f32[256,512]{1,0:T(8,128)S(1)}, u32[]{:S(2)}, u32[]{:S(2)}) %collective-permute-start.15) | collective-permute-done | bytes 524320 | tf_op jit(solution)/shard_map/ppermute | solution.py:810
  109.2 3.2 %shard_map.69 = (f32[64,640]{1,0:T(8,128)S(1)}, f32[64,640]{1,0:T(8,128)S(1)}, f32[64,640]{1,0:T(8,128)S(1)}, f32[8,128]{1,0:T(8,128)S(1)}) custom-call(s32[2]{0:T(128)S(1)} %pad_add_fusion.place, f32[192,768]{1,0:T(8,128)S(1)} %get-tuple-element.69.refs_0_.before, bf16[8,256,256]{2,1,0:T(8,128)(2,1)S(1)} %get-tuple-element.63.refs_3_.refs_1_, ...), custom_call_target="tpu_custom_call" | custom-call | flops 3000000000 | bytes 1048576 | tf_op jit(solution)/shard_map/pallas_call | solution.py:547
  112.4 1.4 collective-permute-start.16
  113.8 1.9 collective-permute-start.17
  115.7 4.7 %collective-permute-done.17.recv_b = f32[64,640]{1,0:T(8,128)S(1)} collective-permute-done((f32[64,640]{1,0:T(8,128)S(1)}, f32[64,640]{1,0:T(8,128)S(1)}, u32[]{:S(2)}, u32[]{:S(2)}) %collective-permute-start.17) | collective-permute-done | bytes 163872 | tf_op jit(solution)/shard_map/ppermute | solution.py:763
  121.8 4.9 %collective-permute-done.18.recv_a = f32[192,128]{1,0:T(8,128)S(1)} collective-permute-done((f32[192,128]{1,0:T(8,128)S(1)}, f32[192,128]{1,0:T(8,128)S(1)}, u32[]{:S(2)}, u32[]{:S(2)}) %collective-permute-start.18) | collective-permute-done | bytes 98336 | tf_op jit(solution)/shard_map/ppermute | solution.py:763
  127.4 9.3 %shard_map.70 = (f32[32,640]{1,0:T(8,128)S(1)}, f32[128,640]{1,0:T(8,128)S(1)}, f32[32,640]{1,0:T(8,128)S(1)}, f32[8,128]{1,0:T(8,128)S(1)}) custom-call(s32[2]{0:T(128)S(1)} %pad_add_fusion.place, f32[192,768]{1,0:T(8,128)S(1)} %get-tuple-element.80.refs_0_, bf16[8,256,256]{2,1,0:T(8,128)(2,1)S(1)} %get-tuple-element.63.refs_3_.refs_1_, ...), custom_call_target="tpu_custom_call" | custom-call | flops 12000000000 | bytes 4194304 | tf_op jit(solution)/shard_map/pallas_call | solution.py:547
  136.9 1.9 collective-permute-start.32
  138.9 3.7 %collective-permute-start.20 = (f32[4,8,128]{2,1,0:T(8,128)S(1)}, f32[4,8,128]{2,1,0:T(8,128)S(1)}, u32[]{:S(2)}, u32[]{:S(2)}) collective-permute-start(f32[4,8,128]{2,1,0:T(8,128)S(1)} %pad_maximum_fusion), channel_id=1, source_target_pairs={{0,1},{1,0},{2,3},{3,2},{4,5},{5,4},{6,7},{7,6},{8,9},{9,8},{10,11... | collective-permute-start | bytes 49160 | tf_op jit(solution)/shard_map/ppermute | solution.py:769
  143.4 3.7 %collective-permute-start.34 = (f32[144,512]{1,0:T(8,128)S(1)}, f32[144,512]{1,0:T(8,128)S(1)}, u32[]{:S(2)}, u32[]{:S(2)}) collective-permute-start(f32[144,512]{1,0:T(8,128)S(1)} %wrap.1.refs_0_), channel_id=1, source_target_pairs={{0,2},{1,3},{2,0},{3,1},{4,6},{5,7},{6,4},{7,5},{8,10},{9,11},{10,... | collective-permute-start | bytes 884744 | tf_op jit(solution)/shard_map/ppermute | solution.py:769
  147.1 2.9 %collective-permute-start.25 = (f32[128,512]{1,0:T(8,128)S(1)}, f32[128,512]{1,0:T(8,128)S(1)}, u32[]{:S(2)}, u32[]{:S(2)}) collective-permute-start(f32[128,512]{1,0:T(8,128)S(1)} %get-tuple-element.82.refs_0_), channel_id=1, source_target_pairs={{0,1},{1,0},{2,3},{3,2},{4,5},{5,4},{6,7},{7,6},{8,9},{9,8},{10,11... | collective-permute-start | bytes 786440 | tf_op jit(solution)/shard_map/ppermute | solution.py:769
  150.1 2.3 %collective-permute-start.27 = (f32[128,512]{1,0:T(8,128)S(1)}, f32[128,512]{1,0:T(8,128)S(1)}, u32[]{:S(2)}, u32[]{:S(2)}) collective-permute-start(f32[128,512]{1,0:T(8,128)S(1)} %get-tuple-element.82.refs_0_), channel_id=1, source_target_pairs={{0,3},{1,2},{2,1},{3,0},{4,7},{5,6},{6,5},{7,4},{8,11},{9,10},{10,... | collective-permute-start | bytes 786440 | tf_op jit(solution)/shard_map/ppermute | solution.py:769
  152.4 8.7 %collective-permute-done.21 = f32[4,8,128]{2,1,0:T(8,128)S(1)} collective-permute-done((f32[4,8,128]{2,1,0:T(8,128)S(1)}, f32[4,8,128]{2,1,0:T(8,128)S(1)}, u32[]{:S(2)}, u32[]{:S(2)}) %collective-permute-start.21) | collective-permute-done | bytes 16416 | tf_op jit(solution)/shard_map/ppermute | solution.py:769
  161.1 1.9 collective-permute-start.22
  162.9 0.8 collective-permute-done.22
  163.8 7.5 %collective-permute-start.23 = (f32[4,8,128]{2,1,0:T(8,128)S(1)}, f32[4,8,128]{2,1,0:T(8,128)S(1)}, u32[]{:S(2)}, u32[]{:S(2)}) collective-permute-start(f32[4,8,128]{2,1,0:T(8,128)S(1)} %add.26), channel_id=1, source_target_pairs={{0,8},{4,12},{8,0},{12,4},{16,24},{20,28},{24,16},{28,20},{1,9},{5... | collective-permute-start | bytes 49160 | tf_op jit(solution)/shard_map/ppermute | solution.py:769
  171.3 1.7 collective-permute-done.23
  173.0 2.0 collective-permute-start.35
  175.1 7.1 %collective-permute-start.24 = (f32[4,8,128]{2,1,0:T(8,128)S(1)}, f32[4,8,128]{2,1,0:T(8,128)S(1)}, u32[]{:S(2)}, u32[]{:S(2)}) collective-permute-start(f32[4,8,128]{2,1,0:T(8,128)S(1)} %add.27), channel_id=1, source_target_pairs={{0,16},{4,20},{8,24},{12,28},{16,0},{20,4},{24,8},{28,12},{1,17},{... | collective-permute-start | bytes 49160 | tf_op jit(solution)/shard_map/ppermute | solution.py:769
  182.2 3.0 %collective-permute-start.29 = (f32[128,512]{1,0:T(8,128)S(1)}, f32[128,512]{1,0:T(8,128)S(1)}, u32[]{:S(2)}, u32[]{:S(2)}) collective-permute-start(f32[128,512]{1,0:T(8,128)S(1)} %get-tuple-element.83.refs_4_.before), channel_id=1, source_target_pairs={{0,2},{1,3},{2,0},{3,1},{4,6},{5,7},{6,4},{7,5},{8,10},{9,11},{10,... | collective-permute-start | bytes 786440 | tf_op jit(solution)/shard_map/ppermute | solution.py:769
  185.1 1.6 collective-permute-start.30
  186.7 15.9 %collective-permute-done.28.refs_5_ = f32[128,512]{1,0:T(8,128)S(1)} collective-permute-done((f32[128,512]{1,0:T(8,128)S(1)}, f32[128,512]{1,0:T(8,128)S(1)}, u32[]{:S(2)}, u32[]{:S(2)}) %collective-permute-start.28) | collective-permute-done | bytes 262176 | tf_op jit(solution)/shard_map/ppermute | solution.py:769
  202.7 8.1 %collective-permute-done.30.refs_7_ = f32[128,512]{1,0:T(8,128)S(1)} collective-permute-done((f32[128,512]{1,0:T(8,128)S(1)}, f32[128,512]{1,0:T(8,128)S(1)}, u32[]{:S(2)}, u32[]{:S(2)}) %collective-permute-start.30) | collective-permute-done | bytes 262176 | tf_op jit(solution)/shard_map/ppermute | solution.py:769
  210.7 2.0 solution_image.1
  212.8 1.8 residual_image.1
  (49 shorter events, 5.3 us)
Async XLA Ops:
  0.6 9.0 %copy-start = (f32[128,2048]{1,0:T(8,128)S(1)}, f32[128,2048]{1,0:T(8,128)}, u32[]{:S(2)}) copy-start(f32[128,2048]{1,0:T(8,128)} %est.5) | copy-start | bytes 3145732
  1.8 4.3 %collective-permute-start = (f32[32,2048]{1,0:T(8,128)S(1)}, f32[32,2048]{1,0:T(8,128)S(1)}, u32[]{:S(2)}, u32[]{:S(2)}) collective-permute-start(f32[32,2048]{1,0:T(8,128)S(1)} %get-tuple-element.91), channel_id=1, source_target_pairs={{0,4},{8,12},{16,20},{24,28},{4,0},{12,8},{20,16},{28,24},{1,5},{9... | collective-permute-start | bytes 786440 | tf_op jit(solution)/shard_map/ppermute | solution.py:763
  1.9 7.7 %collective-permute-start.1 = (f32[32,2048]{1,0:T(8,128)S(1)}, f32[32,2048]{1,0:T(8,128)S(1)}, u32[]{:S(2)}, u32[]{:S(2)}) collective-permute-start(f32[32,2048]{1,0:T(8,128)S(1)} %get-tuple-element.90), channel_id=1, source_target_pairs={{4,8},{12,16},{20,24},{8,4},{16,12},{24,20},{5,9},{13,17},{21,25},... | collective-permute-start | bytes 786440 | tf_op jit(solution)/shard_map/ppermute | solution.py:763
  16.1 5.6 %collective-permute-start.2 = (f32[32,2048]{1,0:T(8,128)S(1)}, f32[32,2048]{1,0:T(8,128)S(1)}, u32[]{:S(2)}, u32[]{:S(2)}) collective-permute-start(f32[32,2048]{1,0:T(8,128)S(1)} %get-tuple-element.50.send_a), channel_id=1, source_target_pairs={{0,4},{8,12},{16,20},{24,28},{4,0},{12,8},{20,16},{28,24},{1,5},{9... | collective-permute-start | bytes 786440 | tf_op jit(solution)/shard_map/ppermute | solution.py:763
  19.7 8.4 %collective-permute-start.3 = (f32[32,2048]{1,0:T(8,128)S(1)}, f32[32,2048]{1,0:T(8,128)S(1)}, u32[]{:S(2)}, u32[]{:S(2)}) collective-permute-start(f32[32,2048]{1,0:T(8,128)S(1)} %get-tuple-element.52.send_b), channel_id=1, source_target_pairs={{4,8},{12,16},{20,24},{8,4},{16,12},{24,20},{5,9},{13,17},{21,25},... | collective-permute-start | bytes 786440 | tf_op jit(solution)/shard_map/ppermute | solution.py:763
  29.1 20.7 %collective-permute-start.4 = (f32[144,512]{1,0:T(8,128)S(1)}, f32[144,512]{1,0:T(8,128)S(1)}, u32[]{:S(2)}, u32[]{:S(2)}) collective-permute-start(f32[144,512]{1,0:T(8,128)S(1)} %get-tuple-element.55), channel_id=1, source_target_pairs={{0,1},{1,0},{2,3},{3,2},{4,5},{5,4},{6,7},{7,6},{8,9},{9,8},{10,11... | collective-permute-start | bytes 884744 | tf_op jit(solution)/shard_map/ppermute | solution.py:769
  30.1 51.5 %collective-permute-start.9 = (f32[264,512]{1,0:T(8,128)S(1)}, f32[264,512]{1,0:T(8,128)S(1)}, u32[]{:S(2)}, u32[]{:S(2)}) collective-permute-start(f32[264,512]{1,0:T(8,128)S(1)} %get-tuple-element.62), channel_id=1, source_target_pairs={{0,1},{1,0},{2,3},{3,2},{4,5},{5,4},{6,7},{7,6},{8,9},{9,8},{10,11... | collective-permute-start | bytes 1622024 | tf_op jit(solution)/shard_map/ppermute | solution.py:769
  31.2 55.4 %collective-permute-start.12 = (f32[256,512]{1,0:T(8,128)S(1)}, f32[256,512]{1,0:T(8,128)S(1)}, u32[]{:S(2)}, u32[]{:S(2)}) collective-permute-start(f32[256,512]{1,0:T(8,128)S(1)} %get-tuple-element.67), channel_id=1, source_target_pairs={{1,3},{2,0},{5,7},{6,4},{9,11},{10,8},{13,15},{14,12},{17,19},{18,... | collective-permute-start | bytes 1572872 | tf_op jit(solution)/shard_map/ppermute | solution.py:810
  32.5 58.3 %collective-permute-start.13 = (f32[256,512]{1,0:T(8,128)S(1)}, f32[256,512]{1,0:T(8,128)S(1)}, u32[]{:S(2)}, u32[]{:S(2)}) collective-permute-start(f32[256,512]{1,0:T(8,128)S(1)} %get-tuple-element.68), channel_id=1, source_target_pairs={{1,2},{2,1},{5,6},{6,5},{9,10},{10,9},{13,14},{14,13},{17,18},{18,... | collective-permute-start | bytes 1572872 | tf_op jit(solution)/shard_map/ppermute | solution.py:810
  33.2 40.8 %collective-permute-start.6 = (f32[144,512]{1,0:T(8,128)S(1)}, f32[144,512]{1,0:T(8,128)S(1)}, u32[]{:S(2)}, u32[]{:S(2)}) collective-permute-start(f32[144,512]{1,0:T(8,128)S(1)} %get-tuple-element.56), channel_id=1, source_target_pairs={{0,1},{1,0},{2,3},{3,2},{4,5},{5,4},{6,7},{7,6},{8,9},{9,8},{10,11... | collective-permute-start | bytes 884744 | tf_op jit(solution)/shard_map/ppermute | solution.py:769
  49.8 24.4 %collective-permute-start.5 = (f32[144,512]{1,0:T(8,128)S(1)}, f32[144,512]{1,0:T(8,128)S(1)}, u32[]{:S(2)}, u32[]{:S(2)}) collective-permute-start(f32[144,512]{1,0:T(8,128)S(1)} %add.23), channel_id=1, source_target_pairs={{0,2},{1,3},{2,0},{3,1},{4,6},{5,7},{6,4},{7,5},{8,10},{9,11},{10,... | collective-permute-start | bytes 884744 | tf_op jit(solution)/shard_map/ppermute | solution.py:769
  74.0 4.5 %collective-permute-start.10 = (f32[8,256]{1,0:T(8,128)S(1)}, f32[8,256]{1,0:T(8,128)S(1)}, u32[]{:S(2)}, u32[]{:S(2)}) collective-permute-start(f32[8,256]{1,0:T(8,128)S(1)} %slice.12), channel_id=1, source_target_pairs={{0,2},{1,3},{2,0},{3,1},{4,6},{5,7},{6,4},{7,5},{8,10},{9,11},{10,... | collective-permute-start | bytes 24584 | tf_op jit(solution)/shard_map/ppermute | solution.py:769
  74.2 5.4 %collective-permute-start.11 = (f32[8,256]{1,0:T(8,128)S(1)}, f32[8,256]{1,0:T(8,128)S(1)}, u32[]{:S(2)}, u32[]{:S(2)}) collective-permute-start(f32[8,256]{1,0:T(8,128)S(1)} %slice.12), channel_id=1, source_target_pairs={{0,3},{1,2},{2,1},{3,0},{4,7},{5,6},{6,5},{7,4},{8,11},{9,10},{10,... | collective-permute-start | bytes 24584 | tf_op jit(solution)/shard_map/ppermute | solution.py:769
  78.5 12.3 %collective-permute-start.7 = (f32[32,768]{1,0:T(8,128)S(1)}, f32[32,768]{1,0:T(8,128)S(1)}, u32[]{:S(2)}, u32[]{:S(2)}) collective-permute-start(f32[32,768]{1,0:T(8,128)S(1)} %get-tuple-element.59), channel_id=1, source_target_pairs={{0,4},{8,12},{16,20},{24,28},{4,0},{12,8},{20,16},{28,24},{1,5},{9... | collective-permute-start | bytes 294920 | tf_op jit(solution)/shard_map/ppermute | solution.py:763
  79.7 11.2 %collective-permute-start.8 = (f32[32,768]{1,0:T(8,128)S(1)}, f32[32,768]{1,0:T(8,128)S(1)}, u32[]{:S(2)}, u32[]{:S(2)}) collective-permute-start(f32[32,768]{1,0:T(8,128)S(1)} %get-tuple-element.60), channel_id=1, source_target_pairs={{4,8},{12,16},{20,24},{8,4},{16,12},{24,20},{5,9},{13,17},{21,25},... | collective-permute-start | bytes 294920 | tf_op jit(solution)/shard_map/ppermute | solution.py:763
  81.6 16.4 %collective-permute-start.14 = (f32[256,512]{1,0:T(8,128)S(1)}, f32[256,512]{1,0:T(8,128)S(1)}, u32[]{:S(2)}, u32[]{:S(2)}) collective-permute-start(f32[256,512]{1,0:T(8,128)S(1)} %get-tuple-element.67), channel_id=1, source_target_pairs={{0,2},{3,1},{4,6},{7,5},{8,10},{11,9},{12,14},{15,13},{16,18},{19,... | collective-permute-start | bytes 1572872 | tf_op jit(solution)/shard_map/ppermute | solution.py:810
  86.5 22.7 %collective-permute-start.15 = (f32[256,512]{1,0:T(8,128)S(1)}, f32[256,512]{1,0:T(8,128)S(1)}, u32[]{:S(2)}, u32[]{:S(2)}) collective-permute-start(f32[256,512]{1,0:T(8,128)S(1)} %get-tuple-element.68), channel_id=1, source_target_pairs={{0,3},{3,0},{4,7},{7,4},{8,11},{11,8},{12,15},{15,12},{16,19},{19,... | collective-permute-start | bytes 1572872 | tf_op jit(solution)/shard_map/ppermute | solution.py:810
  112.4 3.3 %collective-permute-start.16 = (f32[64,640]{1,0:T(8,128)S(1)}, f32[64,640]{1,0:T(8,128)S(1)}, u32[]{:S(2)}, u32[]{:S(2)}) collective-permute-start(f32[64,640]{1,0:T(8,128)S(1)} %get-tuple-element.73.send_a), channel_id=1, source_target_pairs={{0,4},{8,12},{16,20},{24,28},{4,0},{12,8},{20,16},{28,24},{1,5},{9... | collective-permute-start | bytes 491528 | tf_op jit(solution)/shard_map/ppermute | solution.py:763
  113.8 6.6 %collective-permute-start.17 = (f32[64,640]{1,0:T(8,128)S(1)}, f32[64,640]{1,0:T(8,128)S(1)}, u32[]{:S(2)}, u32[]{:S(2)}) collective-permute-start(f32[64,640]{1,0:T(8,128)S(1)} %get-tuple-element.75.send_b), channel_id=1, source_target_pairs={{4,8},{12,16},{20,24},{8,4},{16,12},{24,20},{5,9},{13,17},{21,25},... | collective-permute-start | bytes 491528 | tf_op jit(solution)/shard_map/ppermute | solution.py:763
  121.1 5.7 %collective-permute-start.18 = (f32[192,128]{1,0:T(8,128)S(1)}, f32[192,128]{1,0:T(8,128)S(1)}, u32[]{:S(2)}, u32[]{:S(2)}) collective-permute-start(f32[192,128]{1,0:T(8,128)S(1)} %get-tuple-element.77), channel_id=1, source_target_pairs={{0,1},{2,3},{1,0},{3,2},{4,5},{6,7},{5,4},{7,6},{8,9},{10,11},{9,8... | collective-permute-start | bytes 294920 | tf_op jit(solution)/shard_map/ppermute | solution.py:763
  121.1 5.6 %collective-permute-start.19 = (f32[192,128]{1,0:T(8,128)S(1)}, f32[192,128]{1,0:T(8,128)S(1)}, u32[]{:S(2)}, u32[]{:S(2)}) collective-permute-start(f32[192,128]{1,0:T(8,128)S(1)} %get-tuple-element.78), channel_id=1, source_target_pairs={{1,2},{2,1},{5,6},{6,5},{9,10},{10,9},{13,14},{14,13},{17,18},{18,... | collective-permute-start | bytes 294920 | tf_op jit(solution)/shard_map/ppermute | solution.py:763
  136.8 5.7 %collective-permute-start.31 = (f32[32,640]{1,0:T(8,128)S(1)}, f32[32,640]{1,0:T(8,128)S(1)}, u32[]{:S(2)}, u32[]{:S(2)}) collective-permute-start(f32[32,640]{1,0:T(8,128)S(1)} %get-tuple-element.87.send_a), channel_id=1, source_target_pairs={{0,4},{8,12},{16,20},{24,28},{4,0},{12,8},{20,16},{28,24},{1,5},{9... | collective-permute-start | bytes 245768 | tf_op jit(solution)/shard_map/ppermute | solution.py:763
  136.9 5.7 %collective-permute-start.32 = (f32[32,640]{1,0:T(8,128)S(1)}, f32[32,640]{1,0:T(8,128)S(1)}, u32[]{:S(2)}, u32[]{:S(2)}) collective-permute-start(f32[32,640]{1,0:T(8,128)S(1)} %get-tuple-element.89.send_b), channel_id=1, source_target_pairs={{4,8},{12,16},{20,24},{8,4},{16,12},{24,20},{5,9},{13,17},{21,25},... | collective-permute-start | bytes 245768 | tf_op jit(solution)/shard_map/ppermute | solution.py:763
  138.9 8.2 %collective-permute-start.20 = (f32[4,8,128]{2,1,0:T(8,128)S(1)}, f32[4,8,128]{2,1,0:T(8,128)S(1)}, u32[]{:S(2)}, u32[]{:S(2)}) collective-permute-start(f32[4,8,128]{2,1,0:T(8,128)S(1)} %pad_maximum_fusion), channel_id=1, source_target_pairs={{0,1},{1,0},{2,3},{3,2},{4,5},{5,4},{6,7},{7,6},{8,9},{9,8},{10,11... | collective-permute-start | bytes 49160 | tf_op jit(solution)/shard_map/ppermute | solution.py:769
  143.4 29.7 %collective-permute-start.34 = (f32[144,512]{1,0:T(8,128)S(1)}, f32[144,512]{1,0:T(8,128)S(1)}, u32[]{:S(2)}, u32[]{:S(2)}) collective-permute-start(f32[144,512]{1,0:T(8,128)S(1)} %wrap.1.refs_0_), channel_id=1, source_target_pairs={{0,2},{1,3},{2,0},{3,1},{4,6},{5,7},{6,4},{7,5},{8,10},{9,11},{10,... | collective-permute-start | bytes 884744 | tf_op jit(solution)/shard_map/ppermute | solution.py:769
  147.1 14.0 %collective-permute-start.21 = (f32[4,8,128]{2,1,0:T(8,128)S(1)}, f32[4,8,128]{2,1,0:T(8,128)S(1)}, u32[]{:S(2)}, u32[]{:S(2)}) collective-permute-start(f32[4,8,128]{2,1,0:T(8,128)S(1)} %fusion), channel_id=1, source_target_pairs={{0,2},{1,3},{2,0},{3,1},{4,6},{5,7},{6,4},{7,5},{8,10},{9,11},{10,... | collective-permute-start | bytes 49160 | tf_op jit(solution)/shard_map/ppermute | solution.py:769
  147.1 27.9 %collective-permute-start.25 = (f32[128,512]{1,0:T(8,128)S(1)}, f32[128,512]{1,0:T(8,128)S(1)}, u32[]{:S(2)}, u32[]{:S(2)}) collective-permute-start(f32[128,512]{1,0:T(8,128)S(1)} %get-tuple-element.82.refs_0_), channel_id=1, source_target_pairs={{0,1},{1,0},{2,3},{3,2},{4,5},{5,4},{6,7},{7,6},{8,9},{9,8},{10,11... | collective-permute-start | bytes 786440 | tf_op jit(solution)/shard_map/ppermute | solution.py:769
  150.0 32.1 %collective-permute-start.26 = (f32[128,512]{1,0:T(8,128)S(1)}, f32[128,512]{1,0:T(8,128)S(1)}, u32[]{:S(2)}, u32[]{:S(2)}) collective-permute-start(f32[128,512]{1,0:T(8,128)S(1)} %get-tuple-element.82.refs_0_), channel_id=1, source_target_pairs={{0,2},{1,3},{2,0},{3,1},{4,6},{5,7},{6,4},{7,5},{8,10},{9,11},{10,... | collective-permute-start | bytes 786440 | tf_op jit(solution)/shard_map/ppermute | solution.py:769
  150.1 32.1 %collective-permute-start.27 = (f32[128,512]{1,0:T(8,128)S(1)}, f32[128,512]{1,0:T(8,128)S(1)}, u32[]{:S(2)}, u32[]{:S(2)}) collective-permute-start(f32[128,512]{1,0:T(8,128)S(1)} %get-tuple-element.82.refs_0_), channel_id=1, source_target_pairs={{0,3},{1,2},{2,1},{3,0},{4,7},{5,6},{6,5},{7,4},{8,11},{9,10},{10,... | collective-permute-start | bytes 786440 | tf_op jit(solution)/shard_map/ppermute | solution.py:769
  161.1 2.7 %collective-permute-start.22 = (f32[4,8,128]{2,1,0:T(8,128)S(1)}, f32[4,8,128]{2,1,0:T(8,128)S(1)}, u32[]{:S(2)}, u32[]{:S(2)}) collective-permute-start(f32[4,8,128]{2,1,0:T(8,128)S(1)} %fusion.1), channel_id=1, source_target_pairs={{0,4},{4,0},{8,12},{12,8},{16,20},{20,16},{24,28},{28,24},{1,5},{5... | collective-permute-start | bytes 49160 | tf_op jit(solution)/shard_map/ppermute | solution.py:769
  163.8 9.3 %collective-permute-start.23 = (f32[4,8,128]{2,1,0:T(8,128)S(1)}, f32[4,8,128]{2,1,0:T(8,128)S(1)}, u32[]{:S(2)}, u32[]{:S(2)}) collective-permute-start(f32[4,8,128]{2,1,0:T(8,128)S(1)} %add.26), channel_id=1, source_target_pairs={{0,8},{4,12},{8,0},{12,4},{16,24},{20,28},{24,16},{28,20},{1,9},{5... | collective-permute-start | bytes 49160 | tf_op jit(solution)/shard_map/ppermute | solution.py:769
  173.0 39.7 %collective-permute-start.33 = (f32[144,512]{1,0:T(8,128)S(1)}, f32[144,512]{1,0:T(8,128)S(1)}, u32[]{:S(2)}, u32[]{:S(2)}) collective-permute-start(f32[144,512]{1,0:T(8,128)S(1)} %wrap.1.refs_0_), channel_id=1, source_target_pairs={{0,1},{1,0},{2,3},{3,2},{4,5},{5,4},{6,7},{7,6},{8,9},{9,8},{10,11... | collective-permute-start | bytes 884744 | tf_op jit(solution)/shard_map/ppermute | solution.py:769
  173.0 39.7 %collective-permute-start.35 = (f32[144,512]{1,0:T(8,128)S(1)}, f32[144,512]{1,0:T(8,128)S(1)}, u32[]{:S(2)}, u32[]{:S(2)}) collective-permute-start(f32[144,512]{1,0:T(8,128)S(1)} %collective-permute-done.34.refs_2_), channel_id=1, source_target_pairs={{0,1},{1,0},{2,3},{3,2},{4,5},{5,4},{6,7},{7,6},{8,9},{9,8},{10,11... | collective-permute-start | bytes 884744 | tf_op jit(solution)/shard_map/ppermute | solution.py:769
  175.1 10.1 %collective-permute-start.24 = (f32[4,8,128]{2,1,0:T(8,128)S(1)}, f32[4,8,128]{2,1,0:T(8,128)S(1)}, u32[]{:S(2)}, u32[]{:S(2)}) collective-permute-start(f32[4,8,128]{2,1,0:T(8,128)S(1)} %add.27), channel_id=1, source_target_pairs={{0,16},{4,20},{8,24},{12,28},{16,0},{20,4},{24,8},{28,12},{1,17},{... | collective-permute-start | bytes 49160 | tf_op jit(solution)/shard_map/ppermute | solution.py:769
  182.2 20.5 %collective-permute-start.28 = (f32[128,512]{1,0:T(8,128)S(1)}, f32[128,512]{1,0:T(8,128)S(1)}, u32[]{:S(2)}, u32[]{:S(2)}) collective-permute-start(f32[128,512]{1,0:T(8,128)S(1)} %get-tuple-element.83.refs_4_.before), channel_id=1, source_target_pairs={{0,1},{1,0},{2,3},{3,2},{4,5},{5,4},{6,7},{7,6},{8,9},{9,8},{10,11... | collective-permute-start | bytes 786440 | tf_op jit(solution)/shard_map/ppermute | solution.py:769
  182.2 20.5 %collective-permute-start.29 = (f32[128,512]{1,0:T(8,128)S(1)}, f32[128,512]{1,0:T(8,128)S(1)}, u32[]{:S(2)}, u32[]{:S(2)}) collective-permute-start(f32[128,512]{1,0:T(8,128)S(1)} %get-tuple-element.83.refs_4_.before), channel_id=1, source_target_pairs={{0,2},{1,3},{2,0},{3,1},{4,6},{5,7},{6,4},{7,5},{8,10},{9,11},{10,... | collective-permute-start | bytes 786440 | tf_op jit(solution)/shard_map/ppermute | solution.py:769
  185.1 25.6 %collective-permute-start.30 = (f32[128,512]{1,0:T(8,128)S(1)}, f32[128,512]{1,0:T(8,128)S(1)}, u32[]{:S(2)}, u32[]{:S(2)}) collective-permute-start(f32[128,512]{1,0:T(8,128)S(1)} %get-tuple-element.83.refs_4_.before), channel_id=1, source_target_pairs={{0,3},{1,2},{2,1},{3,0},{4,7},{5,6},{6,5},{7,4},{8,11},{9,10},{10,... | collective-permute-start | bytes 786440 | tf_op jit(solution)/shard_map/ppermute | solution.py:769

commit v5 on v4

--- a/solution.py
+++ b/solution.py
@@ -860,12 +860,6 @@
     k2 = wrap(place, send_a, mid, send_b, recv_a, recv_b, k1, halo)
 
     def gathered(x):
-        parts = [x]
-        for d in range(1, n):
-            parts.append(swap(x, "frame", d))
-        return parts
-
-    def gathered_tree(x):
         parts = [x] + [None] * (n - 1)
         for i in range(n):
             for d in reversed(distances):
@@ -873,7 +867,7 @@
                     parts[i + d] = swap(parts[i], "frame", d)
         return parts
 
-    g0, g1, g2 = gathered(k0), gathered(k1), gathered_tree(k2)
+    g0, g1, g2 = gathered(k0), gathered(k1), gathered(k2)
     result, base, coef = solution_image(place, estimate, sums, g0, g1)
     return result, residual_image(place, base, coef, g2, halo)
 

time: 216 us -> 219 us (1.014)
  waiting for transfers between devices: 104 us -> 118 us
  starting transfers between devices: 70.2 us -> 59.7 us
    ppermute x20, waiting for transfers between devices: 73.1 us -> 86.8 us  [swap(): return lax.ppermute(x, axis, [(i, i ^ distance) for i in range(n)])]
    ppermute x20, starting transfers between devices: 45.7 us -> 35.1 us  [swap(): return lax.ppermute(x, axis, [(i, i ^ distance) for i in range(n)])]
  transfers between devices with their start and end apart: 36 -> 36, of which waited for: 15 -> 18; matrix products, arithmetic and copies ran while one was open for 0% -> 0% of each run, Pallas kernels for 7% -> 7%
where the time goes in v5:
time: 219 us; the launch traced here: 218 us
  waiting for transfers between devices  118 us (54%)
  starting transfers between devices  59.7 us (27%)
  Pallas kernels  37.9 us (17%)
    ppermute x20, waiting for transfers between devices, swap(): return lax.ppermute(x, axis, [(i, i ^ distance) for i in range(n)])  86.8 us
    ppermute x20, starting transfers between devices, swap(): return lax.ppermute(x, axis, [(i, i ^ distance) for i in range(n)])  35.1 us
    ppermute x12, waiting for transfers between devices, neighbours(): out.append(lax.ppermute(x, axis, pairs + [(b, a) for a, b in pairs]))  19.8 us
    pallas_call x3, Pallas kernels, apply_terms(): pl.pallas_call(functools.partial(apply_kernel, n, frames, rows, halo, w,...  19.6 us
    ppermute x12, starting transfers between devices, neighbours(): out.append(lax.ppermute(x, axis, pairs + [(b, a) for a, b in pairs]))  15.5 us
    ppermute x4, waiting for transfers between devices, steps(): moved.append(lax.ppermute(packed[d - 1], 'frame', pairs))  11.3 us
    ppermute x4, starting transfers between devices, steps(): moved.append(lax.ppermute(packed[d - 1], 'frame', pairs))  9.05 us
    pallas_call x1, Pallas kernels, first_terms(): pl.pallas_call(functools.partial(first_kernel, frames, rows, halo), out_s...  6.47 us
  transfers between devices with their start and end apart: 36, of which 18 were waited for; matrix products, arithmetic and copies ran while one was open for 0% of the time, Pallas kernels for 7%

profile of v5, /device:TPU:2, one launch (start us, length us, event | category | flops | bytes accessed | tf_op | source)
XLA Modules:
  0.0 217.8 jit_solution(14944855832054594244)
XLA Ops:
  0.7 1.2 slice_select_fusion
  1.9 1.9 collective-permute-start.1
  3.9 2.2 %prepare.1 = (f32[264,512]{1,0:T(8,128)S(1)}, f32[256,512]{1,0:T(8,128)S(1)}, f32[256,512]{1,0:T(8,128)S(1)}, f32[8,512]{1,0:T(8,128)S(1)}, bf16[2,256,256]{2,1,...) custom-call(s32[2]{0:T(128)S(1)} %pad_add_fusion.place, ...), custom_call_target="tpu_custom_call" | custom-call | tf_op jit(solution)/shard_map/prepare/pallas_call | solution.py:350
  6.1 3.4 %collective-permute-done.1.recv_b = f32[32,2048]{1,0:T(8,128)S(1)} collective-permute-done((f32[32,2048]{1,0:T(8,128)S(1)}, f32[32,2048]{1,0:T(8,128)S(1)}, u32[]{:S(2)}, u32[]{:S(2)}) %collective-permute-start.1) | collective-permute-done | bytes 262176 | tf_op jit(solution)/shard_map/ppermute | solution.py:763
  9.6 6.5 %first_terms.1 = (f32[32,2048]{1,0:T(8,128)S(1)}, f32[128,2048]{1,0:T(8,128)S(1)}, f32[32,2048]{1,0:T(8,128)S(1)}) custom-call(s32[2]{0:T(128)S(1)} %pad_add_fusion.place, f32[128,2048]{1,0:T(8,128)S(1)} %copy-done, f32[32,2048]{1,0:T(8,128)S(1)} %collective-permute-done.recv_a, f32[32,2048]{1,0:T(8,128)S(1)} %collective-permute-done.1.recv_b, ...), custom_call_target="tpu_custom_call" | custom-call | flops 8000000000 | bytes 8388608 | tf_op jit(solution)/shard_map/first_terms/pallas_call | solution.py:292
  16.1 3.6 %collective-permute-start.2 = (f32[32,2048]{1,0:T(8,128)S(1)}, f32[32,2048]{1,0:T(8,128)S(1)}, u32[]{:S(2)}, u32[]{:S(2)}) collective-permute-start(f32[32,2048]{1,0:T(8,128)S(1)} %get-tuple-element.50.send_a), channel_id=1, source_target_pairs={{0,4},{8,12},{16,20},{24,28},{4,0},{12,8},{20,16},{28,24},{1,5},{9... | collective-permute-start | bytes 786440 | tf_op jit(solution)/shard_map/ppermute | solution.py:763
  19.7 1.9 collective-permute-start.3
  21.6 6.5 %collective-permute-done.3.recv_b = f32[32,2048]{1,0:T(8,128)S(1)} collective-permute-done((f32[32,2048]{1,0:T(8,128)S(1)}, f32[32,2048]{1,0:T(8,128)S(1)}, u32[]{:S(2)}, u32[]{:S(2)}) %collective-permute-start.3) | collective-permute-done | bytes 262176 | tf_op jit(solution)/shard_map/ppermute | solution.py:763
  29.1 1.0 collective-permute-start.4
  30.1 1.1 collective-permute-start.9
  31.2 1.3 collective-permute-start.12
  33.2 5.5 %collective-permute-start.6 = (f32[144,512]{1,0:T(8,128)S(1)}, f32[144,512]{1,0:T(8,128)S(1)}, u32[]{:S(2)}, u32[]{:S(2)}) collective-permute-start(f32[144,512]{1,0:T(8,128)S(1)} %get-tuple-element.56), channel_id=1, source_target_pairs={{0,1},{1,0},{2,3},{3,2},{4,5},{5,4},{6,7},{7,6},{8,9},{9,8},{10,11... | collective-permute-start | bytes 884744 | tf_op jit(solution)/shard_map/ppermute | solution.py:769
  38.7 11.1 %collective-permute-done.4 = f32[144,512]{1,0:T(8,128)S(1)} collective-permute-done((f32[144,512]{1,0:T(8,128)S(1)}, f32[144,512]{1,0:T(8,128)S(1)}, u32[]{:S(2)}, u32[]{:S(2)}) %collective-permute-start.4) | collective-permute-done | bytes 294944 | tf_op jit(solution)/shard_map/ppermute | solution.py:769
  49.9 24.1 %collective-permute-done.6.refs_2_ = f32[144,512]{1,0:T(8,128)S(1)} collective-permute-done((f32[144,512]{1,0:T(8,128)S(1)}, f32[144,512]{1,0:T(8,128)S(1)}, u32[]{:S(2)}, u32[]{:S(2)}) %collective-permute-start.6) | collective-permute-done | bytes 294944 | tf_op jit(solution)/shard_map/ppermute | solution.py:769
  74.2 2.1 collective-permute-start.11
  77.0 1.5 collective-permute-done.10.refs_2_
  78.5 1.1 collective-permute-done.11.refs_3_
  79.7 1.9 collective-permute-start.8
  81.6 2.8 %collective-permute-start.14 = (f32[256,512]{1,0:T(8,128)S(1)}, f32[256,512]{1,0:T(8,128)S(1)}, u32[]{:S(2)}, u32[]{:S(2)}) collective-permute-start(f32[256,512]{1,0:T(8,128)S(1)} %get-tuple-element.67), channel_id=1, source_target_pairs={{0,2},{3,1},{4,6},{7,5},{8,10},{11,9},{12,14},{15,13},{16,18},{19,... | collective-permute-start | bytes 1572872 | tf_op jit(solution)/shard_map/ppermute | solution.py:810
  84.4 2.1 setup_all.1
  86.5 4.2 %collective-permute-start.15 = (f32[256,512]{1,0:T(8,128)S(1)}, f32[256,512]{1,0:T(8,128)S(1)}, u32[]{:S(2)}, u32[]{:S(2)}) collective-permute-start(f32[256,512]{1,0:T(8,128)S(1)} %get-tuple-element.68), channel_id=1, source_target_pairs={{0,3},{3,0},{4,7},{7,4},{8,11},{11,8},{12,15},{15,12},{16,19},{19,... | collective-permute-start | bytes 1572872 | tf_op jit(solution)/shard_map/ppermute | solution.py:810
  90.8 7.1 %shard_map.68 = (f32[192,640]{1,0:T(8,128)S(1)}, f32[8,128]{1,0:T(8,128)S(1)}, f32[192,768]{1,0:T(8,128)S(1)}) custom-call(s32[2]{0:T(128)S(1)} %pad_add_fusion.place, f32[128,768]{1,0:T(8,128)S(1)} %get-tuple-element.58.refs_0_, f32[32,768]{1,0:T(8,128)S(1)} %collective-permute-done.7.refs_1_, f32[32,768]{1,0:T(8,128)S(1)} %collective-permute-done.8.refs_2_, ...), custom_call_target="tpu_custom_call" | custom-call | flops 8999999488 | bytes 3145728 | tf_op jit(solution)/shard_map/pallas_call | solution.py:547
  98.0 11.3 %collective-permute-done.15.refs_10_ = f32[256,512]{1,0:T(8,128)S(1)} collective-permute-done((f32[256,512]{1,0:T(8,128)S(1)}, f32[256,512]{1,0:T(8,128)S(1)}, u32[]{:S(2)}, u32[]{:S(2)}) %collective-permute-start.15) | collective-permute-done | bytes 524320 | tf_op jit(solution)/shard_map/ppermute | solution.py:810
  109.2 3.2 %shard_map.69 = (f32[64,640]{1,0:T(8,128)S(1)}, f32[64,640]{1,0:T(8,128)S(1)}, f32[64,640]{1,0:T(8,128)S(1)}, f32[8,128]{1,0:T(8,128)S(1)}) custom-call(s32[2]{0:T(128)S(1)} %pad_add_fusion.place, f32[192,768]{1,0:T(8,128)S(1)} %get-tuple-element.69.refs_0_.before, bf16[8,256,256]{2,1,0:T(8,128)(2,1)S(1)} %get-tuple-element.63.refs_3_.refs_1_, ...), custom_call_target="tpu_custom_call" | custom-call | flops 3000000000 | bytes 1048576 | tf_op jit(solution)/shard_map/pallas_call | solution.py:547
  112.4 1.4 collective-permute-start.16
  113.8 1.9 collective-permute-start.17
  115.7 4.7 %collective-permute-done.17.recv_b = f32[64,640]{1,0:T(8,128)S(1)} collective-permute-done((f32[64,640]{1,0:T(8,128)S(1)}, f32[64,640]{1,0:T(8,128)S(1)}, u32[]{:S(2)}, u32[]{:S(2)}) %collective-permute-start.17) | collective-permute-done | bytes 163872 | tf_op jit(solution)/shard_map/ppermute | solution.py:763
  121.8 4.9 %collective-permute-done.18.recv_a = f32[192,128]{1,0:T(8,128)S(1)} collective-permute-done((f32[192,128]{1,0:T(8,128)S(1)}, f32[192,128]{1,0:T(8,128)S(1)}, u32[]{:S(2)}, u32[]{:S(2)}) %collective-permute-start.18) | collective-permute-done | bytes 98336 | tf_op jit(solution)/shard_map/ppermute | solution.py:763
  127.4 9.3 %shard_map.70 = (f32[32,640]{1,0:T(8,128)S(1)}, f32[128,640]{1,0:T(8,128)S(1)}, f32[32,640]{1,0:T(8,128)S(1)}, f32[8,128]{1,0:T(8,128)S(1)}) custom-call(s32[2]{0:T(128)S(1)} %pad_add_fusion.place, f32[192,768]{1,0:T(8,128)S(1)} %get-tuple-element.80.refs_0_, bf16[8,256,256]{2,1,0:T(8,128)(2,1)S(1)} %get-tuple-element.63.refs_3_.refs_1_, ...), custom_call_target="tpu_custom_call" | custom-call | flops 12000000000 | bytes 4194304 | tf_op jit(solution)/shard_map/pallas_call | solution.py:547
  136.9 1.9 collective-permute-start.32
  138.9 3.7 %collective-permute-start.20 = (f32[4,8,128]{2,1,0:T(8,128)S(1)}, f32[4,8,128]{2,1,0:T(8,128)S(1)}, u32[]{:S(2)}, u32[]{:S(2)}) collective-permute-start(f32[4,8,128]{2,1,0:T(8,128)S(1)} %pad_maximum_fusion), channel_id=1, source_target_pairs={{0,1},{1,0},{2,3},{3,2},{4,5},{5,4},{6,7},{7,6},{8,9},{9,8},{10,11... | collective-permute-start | bytes 49160 | tf_op jit(solution)/shard_map/ppermute | solution.py:769
  143.4 3.7 %collective-permute-start.34 = (f32[144,512]{1,0:T(8,128)S(1)}, f32[144,512]{1,0:T(8,128)S(1)}, u32[]{:S(2)}, u32[]{:S(2)}) collective-permute-start(f32[144,512]{1,0:T(8,128)S(1)} %wrap.1.refs_0_), channel_id=1, source_target_pairs={{0,2},{1,3},{2,0},{3,1},{4,6},{5,7},{6,4},{7,5},{8,10},{9,11},{10,... | collective-permute-start | bytes 884744 | tf_op jit(solution)/shard_map/ppermute | solution.py:769
  147.1 2.9 %collective-permute-start.26 = (f32[128,512]{1,0:T(8,128)S(1)}, f32[128,512]{1,0:T(8,128)S(1)}, u32[]{:S(2)}, u32[]{:S(2)}) collective-permute-start(f32[128,512]{1,0:T(8,128)S(1)} %get-tuple-element.82.refs_0_), channel_id=1, source_target_pairs={{0,2},{1,3},{2,0},{3,1},{4,6},{5,7},{6,4},{7,5},{8,10},{9,11},{10,... | collective-permute-start | bytes 786440 | tf_op jit(solution)/shard_map/ppermute | solution.py:769
  150.1 2.8 %collective-permute-start.29 = (f32[128,512]{1,0:T(8,128)S(1)}, f32[128,512]{1,0:T(8,128)S(1)}, u32[]{:S(2)}, u32[]{:S(2)}) collective-permute-start(f32[128,512]{1,0:T(8,128)S(1)} %get-tuple-element.83.refs_4_.before), channel_id=1, source_target_pairs={{0,2},{1,3},{2,0},{3,1},{4,6},{5,7},{6,4},{7,5},{8,10},{9,11},{10,... | collective-permute-start | bytes 786440 | tf_op jit(solution)/shard_map/ppermute | solution.py:769
  152.9 13.7 %collective-permute-done.21 = f32[4,8,128]{2,1,0:T(8,128)S(1)} collective-permute-done((f32[4,8,128]{2,1,0:T(8,128)S(1)}, f32[4,8,128]{2,1,0:T(8,128)S(1)}, u32[]{:S(2)}, u32[]{:S(2)}) %collective-permute-start.21) | collective-permute-done | bytes 16416 | tf_op jit(solution)/shard_map/ppermute | solution.py:769
  166.7 1.9 collective-permute-start.22
  169.4 1.9 collective-permute-start.23
  171.3 1.9 collective-permute-done.23
  173.1 2.0 collective-permute-start.35
  175.2 2.8 %collective-permute-done.26.refs_2_ = f32[128,512]{1,0:T(8,128)S(1)} collective-permute-done((f32[128,512]{1,0:T(8,128)S(1)}, f32[128,512]{1,0:T(8,128)S(1)}, u32[]{:S(2)}, u32[]{:S(2)}) %collective-permute-start.26) | collective-permute-done | bytes 262176 | tf_op jit(solution)/shard_map/ppermute | solution.py:769
  178.0 4.2 %collective-permute-start.24 = (f32[4,8,128]{2,1,0:T(8,128)S(1)}, f32[4,8,128]{2,1,0:T(8,128)S(1)}, u32[]{:S(2)}, u32[]{:S(2)}) collective-permute-start(f32[4,8,128]{2,1,0:T(8,128)S(1)} %add.27), channel_id=1, source_target_pairs={{0,16},{4,20},{8,24},{12,28},{16,0},{20,4},{24,8},{28,12},{1,17},{... | collective-permute-start | bytes 49160 | tf_op jit(solution)/shard_map/ppermute | solution.py:769
  182.2 1.7 collective-permute-done.24
  184.2 1.7 collective-permute-start.30
  185.9 16.8 %collective-permute-done.27.refs_3_ = f32[128,512]{1,0:T(8,128)S(1)} collective-permute-done((f32[128,512]{1,0:T(8,128)S(1)}, f32[128,512]{1,0:T(8,128)S(1)}, u32[]{:S(2)}, u32[]{:S(2)}) %collective-permute-start.27) | collective-permute-done | bytes 262176 | tf_op jit(solution)/shard_map/ppermute | solution.py:769
  202.7 5.6 %collective-permute-done.28.refs_5_ = f32[128,512]{1,0:T(8,128)S(1)} collective-permute-done((f32[128,512]{1,0:T(8,128)S(1)}, f32[128,512]{1,0:T(8,128)S(1)}, u32[]{:S(2)}, u32[]{:S(2)}) %collective-permute-start.28) | collective-permute-done | bytes 262176 | tf_op jit(solution)/shard_map/ppermute | solution.py:769
  208.4 5.5 %collective-permute-done.30.refs_7_ = f32[128,512]{1,0:T(8,128)S(1)} collective-permute-done((f32[128,512]{1,0:T(8,128)S(1)}, f32[128,512]{1,0:T(8,128)S(1)}, u32[]{:S(2)}, u32[]{:S(2)}) %collective-permute-start.30) | collective-permute-done | bytes 262176 | tf_op jit(solution)/shard_map/ppermute | solution.py:769
  213.9 2.0 solution_image.1
  215.9 1.8 residual_image.1
  (49 shorter events, 7.3 us)
Async XLA Ops:
  0.6 9.0 %copy-start = (f32[128,2048]{1,0:T(8,128)S(1)}, f32[128,2048]{1,0:T(8,128)}, u32[]{:S(2)}) copy-start(f32[128,2048]{1,0:T(8,128)} %est.5) | copy-start | bytes 3145732
  1.8 4.3 %collective-permute-start = (f32[32,2048]{1,0:T(8,128)S(1)}, f32[32,2048]{1,0:T(8,128)S(1)}, u32[]{:S(2)}, u32[]{:S(2)}) collective-permute-start(f32[32,2048]{1,0:T(8,128)S(1)} %get-tuple-element.91), channel_id=1, source_target_pairs={{0,4},{8,12},{16,20},{24,28},{4,0},{12,8},{20,16},{28,24},{1,5},{9... | collective-permute-start | bytes 786440 | tf_op jit(solution)/shard_map/ppermute | solution.py:763
  1.9 7.7 %collective-permute-start.1 = (f32[32,2048]{1,0:T(8,128)S(1)}, f32[32,2048]{1,0:T(8,128)S(1)}, u32[]{:S(2)}, u32[]{:S(2)}) collective-permute-start(f32[32,2048]{1,0:T(8,128)S(1)} %get-tuple-element.90), channel_id=1, source_target_pairs={{4,8},{12,16},{20,24},{8,4},{16,12},{24,20},{5,9},{13,17},{21,25},... | collective-permute-start | bytes 786440 | tf_op jit(solution)/shard_map/ppermute | solution.py:763
  16.1 5.6 %collective-permute-start.2 = (f32[32,2048]{1,0:T(8,128)S(1)}, f32[32,2048]{1,0:T(8,128)S(1)}, u32[]{:S(2)}, u32[]{:S(2)}) collective-permute-start(f32[32,2048]{1,0:T(8,128)S(1)} %get-tuple-element.50.send_a), channel_id=1, source_target_pairs={{0,4},{8,12},{16,20},{24,28},{4,0},{12,8},{20,16},{28,24},{1,5},{9... | collective-permute-start | bytes 786440 | tf_op jit(solution)/shard_map/ppermute | solution.py:763
  19.7 8.4 %collective-permute-start.3 = (f32[32,2048]{1,0:T(8,128)S(1)}, f32[32,2048]{1,0:T(8,128)S(1)}, u32[]{:S(2)}, u32[]{:S(2)}) collective-permute-start(f32[32,2048]{1,0:T(8,128)S(1)} %get-tuple-element.52.send_b), channel_id=1, source_target_pairs={{4,8},{12,16},{20,24},{8,4},{16,12},{24,20},{5,9},{13,17},{21,25},... | collective-permute-start | bytes 786440 | tf_op jit(solution)/shard_map/ppermute | solution.py:763
  29.1 20.7 %collective-permute-start.4 = (f32[144,512]{1,0:T(8,128)S(1)}, f32[144,512]{1,0:T(8,128)S(1)}, u32[]{:S(2)}, u32[]{:S(2)}) collective-permute-start(f32[144,512]{1,0:T(8,128)S(1)} %get-tuple-element.55), channel_id=1, source_target_pairs={{0,1},{1,0},{2,3},{3,2},{4,5},{5,4},{6,7},{7,6},{8,9},{9,8},{10,11... | collective-permute-start | bytes 884744 | tf_op jit(solution)/shard_map/ppermute | solution.py:769
  30.1 51.5 %collective-permute-start.9 = (f32[264,512]{1,0:T(8,128)S(1)}, f32[264,512]{1,0:T(8,128)S(1)}, u32[]{:S(2)}, u32[]{:S(2)}) collective-permute-start(f32[264,512]{1,0:T(8,128)S(1)} %get-tuple-element.62), channel_id=1, source_target_pairs={{0,1},{1,0},{2,3},{3,2},{4,5},{5,4},{6,7},{7,6},{8,9},{9,8},{10,11... | collective-permute-start | bytes 1622024 | tf_op jit(solution)/shard_map/ppermute | solution.py:769
  31.2 55.4 %collective-permute-start.12 = (f32[256,512]{1,0:T(8,128)S(1)}, f32[256,512]{1,0:T(8,128)S(1)}, u32[]{:S(2)}, u32[]{:S(2)}) collective-permute-start(f32[256,512]{1,0:T(8,128)S(1)} %get-tuple-element.67), channel_id=1, source_target_pairs={{1,3},{2,0},{5,7},{6,4},{9,11},{10,8},{13,15},{14,12},{17,19},{18,... | collective-permute-start | bytes 1572872 | tf_op jit(solution)/shard_map/ppermute | solution.py:810
  32.5 58.3 %collective-permute-start.13 = (f32[256,512]{1,0:T(8,128)S(1)}, f32[256,512]{1,0:T(8,128)S(1)}, u32[]{:S(2)}, u32[]{:S(2)}) collective-permute-start(f32[256,512]{1,0:T(8,128)S(1)} %get-tuple-element.68), channel_id=1, source_target_pairs={{1,2},{2,1},{5,6},{6,5},{9,10},{10,9},{13,14},{14,13},{17,18},{18,... | collective-permute-start | bytes 1572872 | tf_op jit(solution)/shard_map/ppermute | solution.py:810
  33.2 40.8 %collective-permute-start.6 = (f32[144,512]{1,0:T(8,128)S(1)}, f32[144,512]{1,0:T(8,128)S(1)}, u32[]{:S(2)}, u32[]{:S(2)}) collective-permute-start(f32[144,512]{1,0:T(8,128)S(1)} %get-tuple-element.56), channel_id=1, source_target_pairs={{0,1},{1,0},{2,3},{3,2},{4,5},{5,4},{6,7},{7,6},{8,9},{9,8},{10,11... | collective-permute-start | bytes 884744 | tf_op jit(solution)/shard_map/ppermute | solution.py:769
  49.8 24.4 %collective-permute-start.5 = (f32[144,512]{1,0:T(8,128)S(1)}, f32[144,512]{1,0:T(8,128)S(1)}, u32[]{:S(2)}, u32[]{:S(2)}) collective-permute-start(f32[144,512]{1,0:T(8,128)S(1)} %add.23), channel_id=1, source_target_pairs={{0,2},{1,3},{2,0},{3,1},{4,6},{5,7},{6,4},{7,5},{8,10},{9,11},{10,... | collective-permute-start | bytes 884744 | tf_op jit(solution)/shard_map/ppermute | solution.py:769
  74.0 4.5 %collective-permute-start.10 = (f32[8,256]{1,0:T(8,128)S(1)}, f32[8,256]{1,0:T(8,128)S(1)}, u32[]{:S(2)}, u32[]{:S(2)}) collective-permute-start(f32[8,256]{1,0:T(8,128)S(1)} %slice.12), channel_id=1, source_target_pairs={{0,2},{1,3},{2,0},{3,1},{4,6},{5,7},{6,4},{7,5},{8,10},{9,11},{10,... | collective-permute-start | bytes 24584 | tf_op jit(solution)/shard_map/ppermute | solution.py:769
  74.2 5.4 %collective-permute-start.11 = (f32[8,256]{1,0:T(8,128)S(1)}, f32[8,256]{1,0:T(8,128)S(1)}, u32[]{:S(2)}, u32[]{:S(2)}) collective-permute-start(f32[8,256]{1,0:T(8,128)S(1)} %slice.12), channel_id=1, source_target_pairs={{0,3},{1,2},{2,1},{3,0},{4,7},{5,6},{6,5},{7,4},{8,11},{9,10},{10,... | collective-permute-start | bytes 24584 | tf_op jit(solution)/shard_map/ppermute | solution.py:769
  78.5 12.3 %collective-permute-start.7 = (f32[32,768]{1,0:T(8,128)S(1)}, f32[32,768]{1,0:T(8,128)S(1)}, u32[]{:S(2)}, u32[]{:S(2)}) collective-permute-start(f32[32,768]{1,0:T(8,128)S(1)} %get-tuple-element.59), channel_id=1, source_target_pairs={{0,4},{8,12},{16,20},{24,28},{4,0},{12,8},{20,16},{28,24},{1,5},{9... | collective-permute-start | bytes 294920 | tf_op jit(solution)/shard_map/ppermute | solution.py:763
  79.7 11.2 %collective-permute-start.8 = (f32[32,768]{1,0:T(8,128)S(1)}, f32[32,768]{1,0:T(8,128)S(1)}, u32[]{:S(2)}, u32[]{:S(2)}) collective-permute-start(f32[32,768]{1,0:T(8,128)S(1)} %get-tuple-element.60), channel_id=1, source_target_pairs={{4,8},{12,16},{20,24},{8,4},{16,12},{24,20},{5,9},{13,17},{21,25},... | collective-permute-start | bytes 294920 | tf_op jit(solution)/shard_map/ppermute | solution.py:763
  81.6 16.4 %collective-permute-start.14 = (f32[256,512]{1,0:T(8,128)S(1)}, f32[256,512]{1,0:T(8,128)S(1)}, u32[]{:S(2)}, u32[]{:S(2)}) collective-permute-start(f32[256,512]{1,0:T(8,128)S(1)} %get-tuple-element.67), channel_id=1, source_target_pairs={{0,2},{3,1},{4,6},{7,5},{8,10},{11,9},{12,14},{15,13},{16,18},{19,... | collective-permute-start | bytes 1572872 | tf_op jit(solution)/shard_map/ppermute | solution.py:810
  86.5 22.7 %collective-permute-start.15 = (f32[256,512]{1,0:T(8,128)S(1)}, f32[256,512]{1,0:T(8,128)S(1)}, u32[]{:S(2)}, u32[]{:S(2)}) collective-permute-start(f32[256,512]{1,0:T(8,128)S(1)} %get-tuple-element.68), channel_id=1, source_target_pairs={{0,3},{3,0},{4,7},{7,4},{8,11},{11,8},{12,15},{15,12},{16,19},{19,... | collective-permute-start | bytes 1572872 | tf_op jit(solution)/shard_map/ppermute | solution.py:810
  112.4 3.3 %collective-permute-start.16 = (f32[64,640]{1,0:T(8,128)S(1)}, f32[64,640]{1,0:T(8,128)S(1)}, u32[]{:S(2)}, u32[]{:S(2)}) collective-permute-start(f32[64,640]{1,0:T(8,128)S(1)} %get-tuple-element.73.send_a), channel_id=1, source_target_pairs={{0,4},{8,12},{16,20},{24,28},{4,0},{12,8},{20,16},{28,24},{1,5},{9... | collective-permute-start | bytes 491528 | tf_op jit(solution)/shard_map/ppermute | solution.py:763
  113.8 6.6 %collective-permute-start.17 = (f32[64,640]{1,0:T(8,128)S(1)}, f32[64,640]{1,0:T(8,128)S(1)}, u32[]{:S(2)}, u32[]{:S(2)}) collective-permute-start(f32[64,640]{1,0:T(8,128)S(1)} %get-tuple-element.75.send_b), channel_id=1, source_target_pairs={{4,8},{12,16},{20,24},{8,4},{16,12},{24,20},{5,9},{13,17},{21,25},... | collective-permute-start | bytes 491528 | tf_op jit(solution)/shard_map/ppermute | solution.py:763
  121.1 5.7 %collective-permute-start.18 = (f32[192,128]{1,0:T(8,128)S(1)}, f32[192,128]{1,0:T(8,128)S(1)}, u32[]{:S(2)}, u32[]{:S(2)}) collective-permute-start(f32[192,128]{1,0:T(8,128)S(1)} %get-tuple-element.77), channel_id=1, source_target_pairs={{0,1},{2,3},{1,0},{3,2},{4,5},{6,7},{5,4},{7,6},{8,9},{10,11},{9,8... | collective-permute-start | bytes 294920 | tf_op jit(solution)/shard_map/ppermute | solution.py:763
  121.1 5.6 %collective-permute-start.19 = (f32[192,128]{1,0:T(8,128)S(1)}, f32[192,128]{1,0:T(8,128)S(1)}, u32[]{:S(2)}, u32[]{:S(2)}) collective-permute-start(f32[192,128]{1,0:T(8,128)S(1)} %get-tuple-element.78), channel_id=1, source_target_pairs={{1,2},{2,1},{5,6},{6,5},{9,10},{10,9},{13,14},{14,13},{17,18},{18,... | collective-permute-start | bytes 294920 | tf_op jit(solution)/shard_map/ppermute | solution.py:763
  136.8 5.7 %collective-permute-start.31 = (f32[32,640]{1,0:T(8,128)S(1)}, f32[32,640]{1,0:T(8,128)S(1)}, u32[]{:S(2)}, u32[]{:S(2)}) collective-permute-start(f32[32,640]{1,0:T(8,128)S(1)} %get-tuple-element.87.send_a), channel_id=1, source_target_pairs={{0,4},{8,12},{16,20},{24,28},{4,0},{12,8},{20,16},{28,24},{1,5},{9... | collective-permute-start | bytes 245768 | tf_op jit(solution)/shard_map/ppermute | solution.py:763
  136.9 5.7 %collective-permute-start.32 = (f32[32,640]{1,0:T(8,128)S(1)}, f32[32,640]{1,0:T(8,128)S(1)}, u32[]{:S(2)}, u32[]{:S(2)}) collective-permute-start(f32[32,640]{1,0:T(8,128)S(1)} %get-tuple-element.89.send_b), channel_id=1, source_target_pairs={{4,8},{12,16},{20,24},{8,4},{16,12},{24,20},{5,9},{13,17},{21,25},... | collective-permute-start | bytes 245768 | tf_op jit(solution)/shard_map/ppermute | solution.py:763
  138.9 8.2 %collective-permute-start.20 = (f32[4,8,128]{2,1,0:T(8,128)S(1)}, f32[4,8,128]{2,1,0:T(8,128)S(1)}, u32[]{:S(2)}, u32[]{:S(2)}) collective-permute-start(f32[4,8,128]{2,1,0:T(8,128)S(1)} %pad_maximum_fusion), channel_id=1, source_target_pairs={{0,1},{1,0},{2,3},{3,2},{4,5},{5,4},{6,7},{7,6},{8,9},{9,8},{10,11... | collective-permute-start | bytes 49160 | tf_op jit(solution)/shard_map/ppermute | solution.py:769
  143.4 29.8 %collective-permute-start.34 = (f32[144,512]{1,0:T(8,128)S(1)}, f32[144,512]{1,0:T(8,128)S(1)}, u32[]{:S(2)}, u32[]{:S(2)}) collective-permute-start(f32[144,512]{1,0:T(8,128)S(1)} %wrap.1.refs_0_), channel_id=1, source_target_pairs={{0,2},{1,3},{2,0},{3,1},{4,6},{5,7},{6,4},{7,5},{8,10},{9,11},{10,... | collective-permute-start | bytes 884744 | tf_op jit(solution)/shard_map/ppermute | solution.py:769
  147.1 19.6 %collective-permute-start.21 = (f32[4,8,128]{2,1,0:T(8,128)S(1)}, f32[4,8,128]{2,1,0:T(8,128)S(1)}, u32[]{:S(2)}, u32[]{:S(2)}) collective-permute-start(f32[4,8,128]{2,1,0:T(8,128)S(1)} %fusion), channel_id=1, source_target_pairs={{0,2},{1,3},{2,0},{3,1},{4,6},{5,7},{6,4},{7,5},{8,10},{9,11},{10,... | collective-permute-start | bytes 49160 | tf_op jit(solution)/shard_map/ppermute | solution.py:769
  147.1 30.8 %collective-permute-start.26 = (f32[128,512]{1,0:T(8,128)S(1)}, f32[128,512]{1,0:T(8,128)S(1)}, u32[]{:S(2)}, u32[]{:S(2)}) collective-permute-start(f32[128,512]{1,0:T(8,128)S(1)} %get-tuple-element.82.refs_0_), channel_id=1, source_target_pairs={{0,2},{1,3},{2,0},{3,1},{4,6},{5,7},{6,4},{7,5},{8,10},{9,11},{10,... | collective-permute-start | bytes 786440 | tf_op jit(solution)/shard_map/ppermute | solution.py:769
  150.0 32.1 %collective-permute-start.25 = (f32[128,512]{1,0:T(8,128)S(1)}, f32[128,512]{1,0:T(8,128)S(1)}, u32[]{:S(2)}, u32[]{:S(2)}) collective-permute-start(f32[128,512]{1,0:T(8,128)S(1)} %get-tuple-element.82.refs_0_), channel_id=1, source_target_pairs={{0,1},{1,0},{2,3},{3,2},{4,5},{5,4},{6,7},{7,6},{8,9},{9,8},{10,11... | collective-permute-start | bytes 786440 | tf_op jit(solution)/shard_map/ppermute | solution.py:769
  150.1 34.1 %collective-permute-start.29 = (f32[128,512]{1,0:T(8,128)S(1)}, f32[128,512]{1,0:T(8,128)S(1)}, u32[]{:S(2)}, u32[]{:S(2)}) collective-permute-start(f32[128,512]{1,0:T(8,128)S(1)} %get-tuple-element.83.refs_4_.before), channel_id=1, source_target_pairs={{0,2},{1,3},{2,0},{3,1},{4,6},{5,7},{6,4},{7,5},{8,10},{9,11},{10,... | collective-permute-start | bytes 786440 | tf_op jit(solution)/shard_map/ppermute | solution.py:769
  166.7 2.7 %collective-permute-start.22 = (f32[4,8,128]{2,1,0:T(8,128)S(1)}, f32[4,8,128]{2,1,0:T(8,128)S(1)}, u32[]{:S(2)}, u32[]{:S(2)}) collective-permute-start(f32[4,8,128]{2,1,0:T(8,128)S(1)} %fusion.1), channel_id=1, source_target_pairs={{0,4},{4,0},{8,12},{12,8},{16,20},{20,16},{24,28},{28,24},{1,5},{5... | collective-permute-start | bytes 49160 | tf_op jit(solution)/shard_map/ppermute | solution.py:769
  169.4 3.7 %collective-permute-start.23 = (f32[4,8,128]{2,1,0:T(8,128)S(1)}, f32[4,8,128]{2,1,0:T(8,128)S(1)}, u32[]{:S(2)}, u32[]{:S(2)}) collective-permute-start(f32[4,8,128]{2,1,0:T(8,128)S(1)} %add.26), channel_id=1, source_target_pairs={{0,8},{4,12},{8,0},{12,4},{16,24},{20,28},{24,16},{28,20},{1,9},{5... | collective-permute-start | bytes 49160 | tf_op jit(solution)/shard_map/ppermute | solution.py:769
  173.1 42.8 %collective-permute-start.33 = (f32[144,512]{1,0:T(8,128)S(1)}, f32[144,512]{1,0:T(8,128)S(1)}, u32[]{:S(2)}, u32[]{:S(2)}) collective-permute-start(f32[144,512]{1,0:T(8,128)S(1)} %wrap.1.refs_0_), channel_id=1, source_target_pairs={{0,1},{1,0},{2,3},{3,2},{4,5},{5,4},{6,7},{7,6},{8,9},{9,8},{10,11... | collective-permute-start | bytes 884744 | tf_op jit(solution)/shard_map/ppermute | solution.py:769
  173.1 42.8 %collective-permute-start.35 = (f32[144,512]{1,0:T(8,128)S(1)}, f32[144,512]{1,0:T(8,128)S(1)}, u32[]{:S(2)}, u32[]{:S(2)}) collective-permute-start(f32[144,512]{1,0:T(8,128)S(1)} %collective-permute-done.34.refs_2_), channel_id=1, source_target_pairs={{0,1},{1,0},{2,3},{3,2},{4,5},{5,4},{6,7},{7,6},{8,9},{9,8},{10,11... | collective-permute-start | bytes 884744 | tf_op jit(solution)/shard_map/ppermute | solution.py:769
  178.0 5.9 %collective-permute-start.24 = (f32[4,8,128]{2,1,0:T(8,128)S(1)}, f32[4,8,128]{2,1,0:T(8,128)S(1)}, u32[]{:S(2)}, u32[]{:S(2)}) collective-permute-start(f32[4,8,128]{2,1,0:T(8,128)S(1)} %add.27), channel_id=1, source_target_pairs={{0,16},{4,20},{8,24},{12,28},{16,0},{20,4},{24,8},{28,12},{1,17},{... | collective-permute-start | bytes 49160 | tf_op jit(solution)/shard_map/ppermute | solution.py:769
  182.2 20.6 %collective-permute-start.27 = (f32[128,512]{1,0:T(8,128)S(1)}, f32[128,512]{1,0:T(8,128)S(1)}, u32[]{:S(2)}, u32[]{:S(2)}) collective-permute-start(f32[128,512]{1,0:T(8,128)S(1)} %collective-permute-done.26.refs_2_), channel_id=1, source_target_pairs={{0,1},{1,0},{2,3},{3,2},{4,5},{5,4},{6,7},{7,6},{8,9},{9,8},{10,11... | collective-permute-start | bytes 786440 | tf_op jit(solution)/shard_map/ppermute | solution.py:769
  183.9 24.5 %collective-permute-start.28 = (f32[128,512]{1,0:T(8,128)S(1)}, f32[128,512]{1,0:T(8,128)S(1)}, u32[]{:S(2)}, u32[]{:S(2)}) collective-permute-start(f32[128,512]{1,0:T(8,128)S(1)} %get-tuple-element.83.refs_4_.before), channel_id=1, source_target_pairs={{0,1},{1,0},{2,3},{3,2},{4,5},{5,4},{6,7},{7,6},{8,9},{9,8},{10,11... | collective-permute-start | bytes 786440 | tf_op jit(solution)/shard_map/ppermute | solution.py:769
  184.2 29.7 %collective-permute-start.30 = (f32[128,512]{1,0:T(8,128)S(1)}, f32[128,512]{1,0:T(8,128)S(1)}, u32[]{:S(2)}, u32[]{:S(2)}) collective-permute-start(f32[128,512]{1,0:T(8,128)S(1)} %collective-permute-done.29.refs_6_), channel_id=1, source_target_pairs={{0,1},{1,0},{2,3},{3,2},{4,5},{5,4},{6,7},{7,6},{8,9},{9,8},{10,11... | collective-permute-start | bytes 786440 | tf_op jit(solution)/shard_map/ppermute | solution.py:769

commit v6 on v5

--- a/solution.py
+++ b/solution.py
@@ -488,18 +488,21 @@
         for c in copies(i, group):
             c.start()
         for f in range(frames):
-            span = pl.ds(f * rows, rows)
             if not sources:
                 pltpu.make_async_copy(own.at[f, :, mine], wbuf.at[i, f], wsem.at[i, f]).start()
-            elif len(sources) == 1:
-                source = moved[sources[0]].at[span, :]
-                pltpu.make_async_copy(source, wbuf.at[i, f], wsem.at[i, f]).start()
-            else:
-                for k in range(2):
-
-                    @pl.when((group - distance) == k * quarter)
-                    def _(source=moved[sources[k]].at[span, :], i=i, f=f):
-                        pltpu.make_async_copy(source, wbuf.at[i, f], wsem.at[i, f]).start()
+                continue
+            picked = []
+            for source in sources:
+                ref, row = source[f]
+                picked.append(moved[ref].at[pl.ds(row, rows), :])
+            if len(picked) == 1:
+                pltpu.make_async_copy(picked[0], wbuf.at[i, f], wsem.at[i, f]).start()
+                continue
+            for k in range(2):
+
+                @pl.when((group - distance) == k * quarter)
+                def _(source=picked[k], i=i, f=f):
+                    pltpu.make_async_copy(source, wbuf.at[i, f], wsem.at[i, f]).start()
 
     clear_edges(y_hi, y_lo, qs, ext, rows, w)
     if pieces > 1:
@@ -797,17 +800,29 @@
     for d in range(half, n):
         far_tiles.append(swap(tile[:, : 2 * LANE], "frame", d))
     moved = []
+
+    def move(x, pairs, lead=0):
+        moved.append(lax.ppermute(x, "frame", pairs))
+        return tuple((len(moved) - 1, k * rows) for k in range(frames - lead))
+
     slots = [(0, False, ())]
     for d in range(1, half):
-        moved.append(swap(packed[d - 1], "frame", d))
-        slots.append((d, False, (d - 1,)))
+        slots.append((d, False, (move(packed[d - 1], [(i, i ^ d) for i in range(n)]),)))
     middle = range(quarter, n - quarter)
     where = {}
-    for late in (False, True):
-        for d in range(half, n):
-            pairs = [(i, i ^ d) for i in range(n) if (i in middle) != late]
-            where[d, late] = len(moved)
-            moved.append(lax.ppermute(packed[d - 1], "frame", pairs))
+    for d in range(half, n):
+        pairs = [(i, i ^ d) for i in middle]
+        where[d, False] = move(packed[d - 1], pairs)
+    early_count = len(moved)
+    lead = frames // 2
+    for d in range(half, n):
+        pairs = [(i, i ^ d) for i in range(n) if i not in middle]
+        x = packed[d - 1]
+        if d == half and lead:
+            ahead = move(x[: lead * rows], pairs, frames - lead)
+            where[d, True] = ahead + move(x[lead * rows :], pairs, lead)
+        else:
+            where[d, True] = move(x, pairs)
     late_slots = []
     for late, out in ((False, slots), (True, late_slots)):
         for u in range(half, half + quarter):
@@ -835,7 +850,7 @@
     recv_a, recv_b = neighbours(send_a, send_b, "strip")
 
     acc, stat1, k0x = apply_terms(
-        n, place, (wide, recv_a, recv_b), mats, weights, moved[: where[half, True]],
+        n, place, (wide, recv_a, recv_b), mats, weights, moved[:early_count],
         slots, None, halo,
     )
     send_a, mid, send_b, stat1 = apply_terms(

time: 219 us -> 217 us (level)
  starting transfers between devices: 59.7 us -> 57 us
    ppermute x20 -> x19, starting transfers between devices: 35.1 us -> 28.9 us  [swap(): return lax.ppermute(x, axis, [(i, i ^ distance) for i in range(n)])]
    ppermute x20 -> x19, waiting for transfers between devices: 86.8 us -> 91.3 us  [swap(): return lax.ppermute(x, axis, [(i, i ^ distance) for i in range(n)])]
    ppermute x12, waiting for transfers between devices: 19.8 us -> 17 us  [neighbours(): out.append(lax.ppermute(x, axis, pairs + [(b, a) for a, b in pairs]))]
    ppermute x12, starting transfers between devices: 15.5 us -> 17.7 us  [neighbours(): out.append(lax.ppermute(x, axis, pairs + [(b, a) for a, b in pairs]))]
    ppermute x4 -> x6, starting transfers between devices: 9.05 us -> 10.3 us  [move(): moved.append(lax.ppermute(x, 'frame', pairs))]
    ppermute x4 -> x6, waiting for transfers between devices: 11.3 us -> 10.7 us  [move(): moved.append(lax.ppermute(x, 'frame', pairs))]
  transfers between devices with their start and end apart: 36 -> 37, of which waited for: 18 -> 19; matrix products, arithmetic and copies ran while one was open for 0% -> 0% of each run, Pallas kernels for 7% -> 7%
where the time goes in v6:
time: 217 us; the launch traced here: 216 us
  waiting for transfers between devices  119 us (55%)
  starting transfers between devices  57 us (26%)
  Pallas kernels  37.9 us (17%)
    ppermute x19, waiting for transfers between devices, swap(): return lax.ppermute(x, axis, [(i, i ^ distance) for i in range(n)])  91.3 us
    ppermute x19, starting transfers between devices, swap(): return lax.ppermute(x, axis, [(i, i ^ distance) for i in range(n)])  28.9 us
    pallas_call x3, Pallas kernels, apply_terms(): pl.pallas_call(functools.partial(apply_kernel, n, frames, rows, halo, w,...  19.6 us
    ppermute x12, starting transfers between devices, neighbours(): out.append(lax.ppermute(x, axis, pairs + [(b, a) for a, b in pairs]))  17.7 us
    ppermute x12, waiting for transfers between devices, neighbours(): out.append(lax.ppermute(x, axis, pairs + [(b, a) for a, b in pairs]))  17 us
    ppermute x6, waiting for transfers between devices, move(): moved.append(lax.ppermute(x, 'frame', pairs))  10.7 us
    ppermute x6, starting transfers between devices, move(): moved.append(lax.ppermute(x, 'frame', pairs))  10.3 us
    pallas_call x1, Pallas kernels, first_terms(): pl.pallas_call(functools.partial(first_kernel, frames, rows, halo), out_s...  6.47 us
  transfers between devices with their start and end apart: 37, of which 19 were waited for; matrix products, arithmetic and copies ran while one was open for 0% of the time, Pallas kernels for 7%

profile of v6, /device:TPU:2, one launch (start us, length us, event | category | flops | bytes accessed | tf_op | source)
XLA Modules:
  0.0 216.2 jit_solution(6340952995632843851)
XLA Ops:
  0.7 1.2 slice_select_fusion
  1.9 1.9 collective-permute-start.1
  3.9 2.2 %prepare.1 = (f32[264,512]{1,0:T(8,128)S(1)}, f32[256,512]{1,0:T(8,128)S(1)}, f32[256,512]{1,0:T(8,128)S(1)}, f32[8,512]{1,0:T(8,128)S(1)}, bf16[2,256,256]{2,1,...) custom-call(s32[2]{0:T(128)S(1)} %pad_add_fusion.place, ...), custom_call_target="tpu_custom_call" | custom-call | tf_op jit(solution)/shard_map/prepare/pallas_call | solution.py:350
  6.1 3.4 %collective-permute-done.1.recv_b = f32[32,2048]{1,0:T(8,128)S(1)} collective-permute-done((f32[32,2048]{1,0:T(8,128)S(1)}, f32[32,2048]{1,0:T(8,128)S(1)}, u32[]{:S(2)}, u32[]{:S(2)}) %collective-permute-start.1) | collective-permute-done | bytes 262176 | tf_op jit(solution)/shard_map/ppermute | solution.py:766
  9.6 6.5 %first_terms.1 = (f32[32,2048]{1,0:T(8,128)S(1)}, f32[128,2048]{1,0:T(8,128)S(1)}, f32[32,2048]{1,0:T(8,128)S(1)}) custom-call(s32[2]{0:T(128)S(1)} %pad_add_fusion.place, f32[128,2048]{1,0:T(8,128)S(1)} %copy-done, f32[32,2048]{1,0:T(8,128)S(1)} %collective-permute-done.recv_a, f32[32,2048]{1,0:T(8,128)S(1)} %collective-permute-done.1.recv_b, ...), custom_call_target="tpu_custom_call" | custom-call | flops 8000000000 | bytes 8388608 | tf_op jit(solution)/shard_map/first_terms/pallas_call | solution.py:292
  16.1 3.6 %collective-permute-start.2 = (f32[32,2048]{1,0:T(8,128)S(1)}, f32[32,2048]{1,0:T(8,128)S(1)}, u32[]{:S(2)}, u32[]{:S(2)}) collective-permute-start(f32[32,2048]{1,0:T(8,128)S(1)} %get-tuple-element.50.send_a), channel_id=1, source_target_pairs={{0,4},{8,12},{16,20},{24,28},{4,0},{12,8},{20,16},{28,24},{1,5},{9... | collective-permute-start | bytes 786440 | tf_op jit(solution)/shard_map/ppermute | solution.py:766
  19.7 1.9 collective-permute-start.3
  21.6 6.5 %collective-permute-done.3.recv_b = f32[32,2048]{1,0:T(8,128)S(1)} collective-permute-done((f32[32,2048]{1,0:T(8,128)S(1)}, f32[32,2048]{1,0:T(8,128)S(1)}, u32[]{:S(2)}, u32[]{:S(2)}) %collective-permute-start.3) | collective-permute-done | bytes 262176 | tf_op jit(solution)/shard_map/ppermute | solution.py:766
  31.2 7.4 %collective-permute-done.4 = f32[144,512]{1,0:T(8,128)S(1)} collective-permute-done((f32[144,512]{1,0:T(8,128)S(1)}, f32[144,512]{1,0:T(8,128)S(1)}, u32[]{:S(2)}, u32[]{:S(2)}) %collective-permute-start.4) | collective-permute-done | bytes 294944 | tf_op jit(solution)/shard_map/ppermute | solution.py:772
  38.6 1.3 collective-permute-start.5
  39.9 1.6 collective-permute-start.9
  41.5 1.3 collective-permute-start.12
  43.5 5.1 %collective-permute-done.6.refs_2_ = f32[144,512]{1,0:T(8,128)S(1)} collective-permute-done((f32[144,512]{1,0:T(8,128)S(1)}, f32[144,512]{1,0:T(8,128)S(1)}, u32[]{:S(2)}, u32[]{:S(2)}) %collective-permute-start.6) | collective-permute-done | bytes 294944 | tf_op jit(solution)/shard_map/ppermute | solution.py:772
  49.0 6.7 %collective-permute-done.5.refs_1_ = f32[144,512]{1,0:T(8,128)S(1)} collective-permute-done((f32[144,512]{1,0:T(8,128)S(1)}, f32[144,512]{1,0:T(8,128)S(1)}, u32[]{:S(2)}, u32[]{:S(2)}) %collective-permute-start.5) | collective-permute-done | bytes 294944 | tf_op jit(solution)/shard_map/ppermute | solution.py:772
  57.4 21.2 %collective-permute-done.10.refs_2_ = f32[8,256]{1,0:T(8,128)S(1)} collective-permute-done((f32[8,256]{1,0:T(8,128)S(1)}, f32[8,256]{1,0:T(8,128)S(1)}, u32[]{:S(2)}, u32[]{:S(2)}) %collective-permute-start.10) | collective-permute-done | bytes 8224 | tf_op jit(solution)/shard_map/ppermute | solution.py:772
  78.8 1.9 collective-permute-start.8
  80.7 4.2 %collective-permute-start.16 = (f32[256,512]{1,0:T(8,128)S(1)}, f32[256,512]{1,0:T(8,128)S(1)}, u32[]{:S(2)}, u32[]{:S(2)}) collective-permute-start(f32[256,512]{1,0:T(8,128)S(1)} %get-tuple-element.68), channel_id=1, source_target_pairs={{0,3},{3,0},{4,7},{7,4},{8,11},{11,8},{12,15},{15,12},{16,19},{19,... | collective-permute-start | bytes 1572872 | tf_op jit(solution)/shard_map/ppermute | solution.py:805
  84.9 2.1 setup_all.1
  87.0 1.3 collective-permute-start.14
  88.3 1.3 collective-permute-start.15
  89.7 7.1 %shard_map.68 = (f32[192,640]{1,0:T(8,128)S(1)}, f32[8,128]{1,0:T(8,128)S(1)}, f32[192,768]{1,0:T(8,128)S(1)}) custom-call(s32[2]{0:T(128)S(1)} %pad_add_fusion.place, f32[128,768]{1,0:T(8,128)S(1)} %get-tuple-element.58.refs_0_, f32[32,768]{1,0:T(8,128)S(1)} %collective-permute-done.7.refs_1_, f32[32,768]{1,0:T(8,128)S(1)} %collective-permute-done.8.refs_2_, ...), custom_call_target="tpu_custom_call" | custom-call | flops 8999999488 | bytes 3145728 | tf_op jit(solution)/shard_map/pallas_call | solution.py:550
  96.8 6.0 %collective-permute-done.14.refs_9_ = f32[128,512]{1,0:T(8,128)S(1)} collective-permute-done((f32[128,512]{1,0:T(8,128)S(1)}, f32[128,512]{1,0:T(8,128)S(1)}, u32[]{:S(2)}, u32[]{:S(2)}) %collective-permute-start.14) | collective-permute-done | bytes 262176 | tf_op jit(solution)/shard_map/ppermute | solution.py:805
  102.8 4.7 %collective-permute-done.15.refs_10_ = f32[128,512]{1,0:T(8,128)S(1)} collective-permute-done((f32[128,512]{1,0:T(8,128)S(1)}, f32[128,512]{1,0:T(8,128)S(1)}, u32[]{:S(2)}, u32[]{:S(2)}) %collective-permute-start.15) | collective-permute-done | bytes 262176 | tf_op jit(solution)/shard_map/ppermute | solution.py:805
  107.5 3.2 %shard_map.69 = (f32[64,640]{1,0:T(8,128)S(1)}, f32[64,640]{1,0:T(8,128)S(1)}, f32[64,640]{1,0:T(8,128)S(1)}, f32[8,128]{1,0:T(8,128)S(1)}) custom-call(s32[2]{0:T(128)S(1)} %pad_add_fusion.place, f32[192,768]{1,0:T(8,128)S(1)} %get-tuple-element.69.refs_0_.before, bf16[8,256,256]{2,1,0:T(8,128)(2,1)S(1)} %get-tuple-element.63.refs_3_.refs_1_, ...), custom_call_target="tpu_custom_call" | custom-call | flops 3000000000 | bytes 1048576 | tf_op jit(solution)/shard_map/pallas_call | solution.py:550
  110.7 1.9 collective-permute-start.18
  112.7 4.7 %collective-permute-done.18.recv_b = f32[64,640]{1,0:T(8,128)S(1)} collective-permute-done((f32[64,640]{1,0:T(8,128)S(1)}, f32[64,640]{1,0:T(8,128)S(1)}, u32[]{:S(2)}, u32[]{:S(2)}) %collective-permute-start.18) | collective-permute-done | bytes 163872 | tf_op jit(solution)/shard_map/ppermute | solution.py:766
  118.0 3.0 %collective-permute-start.19 = (f32[192,128]{1,0:T(8,128)S(1)}, f32[192,128]{1,0:T(8,128)S(1)}, u32[]{:S(2)}, u32[]{:S(2)}) collective-permute-start(f32[192,128]{1,0:T(8,128)S(1)} %get-tuple-element.77), channel_id=1, source_target_pairs={{0,1},{2,3},{1,0},{3,2},{4,5},{6,7},{5,4},{7,6},{8,9},{10,11},{9,8... | collective-permute-start | bytes 294920 | tf_op jit(solution)/shard_map/ppermute | solution.py:766
  121.7 2.3 %collective-permute-done.19.recv_a = f32[192,128]{1,0:T(8,128)S(1)} collective-permute-done((f32[192,128]{1,0:T(8,128)S(1)}, f32[192,128]{1,0:T(8,128)S(1)}, u32[]{:S(2)}, u32[]{:S(2)}) %collective-permute-start.19) | collective-permute-done | bytes 98336 | tf_op jit(solution)/shard_map/ppermute | solution.py:766
  124.7 9.3 %shard_map.70 = (f32[32,640]{1,0:T(8,128)S(1)}, f32[128,640]{1,0:T(8,128)S(1)}, f32[32,640]{1,0:T(8,128)S(1)}, f32[8,128]{1,0:T(8,128)S(1)}) custom-call(s32[2]{0:T(128)S(1)} %pad_add_fusion.place, f32[192,768]{1,0:T(8,128)S(1)} %get-tuple-element.80.refs_0_, bf16[8,256,256]{2,1,0:T(8,128)(2,1)S(1)} %get-tuple-element.63.refs_3_.refs_1_, ...), custom_call_target="tpu_custom_call" | custom-call | flops 12000000000 | bytes 4194304 | tf_op jit(solution)/shard_map/pallas_call | solution.py:550
  134.6 1.9 collective-permute-start.33
  136.6 4.0 %collective-permute-start.21 = (f32[4,8,128]{2,1,0:T(8,128)S(1)}, f32[4,8,128]{2,1,0:T(8,128)S(1)}, u32[]{:S(2)}, u32[]{:S(2)}) collective-permute-start(f32[4,8,128]{2,1,0:T(8,128)S(1)} %pad_maximum_fusion), channel_id=1, source_target_pairs={{0,1},{1,0},{2,3},{3,2},{4,5},{5,4},{6,7},{7,6},{8,9},{9,8},{10,11... | collective-permute-start | bytes 49160 | tf_op jit(solution)/shard_map/ppermute | solution.py:772
  141.3 4.2 %collective-permute-start.35 = (f32[144,512]{1,0:T(8,128)S(1)}, f32[144,512]{1,0:T(8,128)S(1)}, u32[]{:S(2)}, u32[]{:S(2)}) collective-permute-start(f32[144,512]{1,0:T(8,128)S(1)} %wrap.1.refs_0_), channel_id=1, source_target_pairs={{0,2},{1,3},{2,0},{3,1},{4,6},{5,7},{6,4},{7,5},{8,10},{9,11},{10,... | collective-permute-start | bytes 884744 | tf_op jit(solution)/shard_map/ppermute | solution.py:772
  145.6 2.9 %collective-permute-start.27 = (f32[128,512]{1,0:T(8,128)S(1)}, f32[128,512]{1,0:T(8,128)S(1)}, u32[]{:S(2)}, u32[]{:S(2)}) collective-permute-start(f32[128,512]{1,0:T(8,128)S(1)} %get-tuple-element.82.refs_0_), channel_id=1, source_target_pairs={{0,2},{1,3},{2,0},{3,1},{4,6},{5,7},{6,4},{7,5},{8,10},{9,11},{10,... | collective-permute-start | bytes 786440 | tf_op jit(solution)/shard_map/ppermute | solution.py:772
  148.5 2.5 %collective-permute-start.30 = (f32[128,512]{1,0:T(8,128)S(1)}, f32[128,512]{1,0:T(8,128)S(1)}, u32[]{:S(2)}, u32[]{:S(2)}) collective-permute-start(f32[128,512]{1,0:T(8,128)S(1)} %get-tuple-element.83.refs_4_.before), channel_id=1, source_target_pairs={{0,2},{1,3},{2,0},{3,1},{4,6},{5,7},{6,4},{7,5},{8,10},{9,11},{10,... | collective-permute-start | bytes 786440 | tf_op jit(solution)/shard_map/ppermute | solution.py:772
  151.0 14.5 %collective-permute-done.22 = f32[4,8,128]{2,1,0:T(8,128)S(1)} collective-permute-done((f32[4,8,128]{2,1,0:T(8,128)S(1)}, f32[4,8,128]{2,1,0:T(8,128)S(1)}, u32[]{:S(2)}, u32[]{:S(2)}) %collective-permute-start.22) | collective-permute-done | bytes 16416 | tf_op jit(solution)/shard_map/ppermute | solution.py:772
  165.5 1.1 collective-permute-start.23
  167.4 2.4 %collective-permute-start.24 = (f32[4,8,128]{2,1,0:T(8,128)S(1)}, f32[4,8,128]{2,1,0:T(8,128)S(1)}, u32[]{:S(2)}, u32[]{:S(2)}) collective-permute-start(f32[4,8,128]{2,1,0:T(8,128)S(1)} %add.26), channel_id=1, source_target_pairs={{0,8},{4,12},{8,0},{12,4},{16,24},{20,28},{24,16},{28,20},{1,9},{5... | collective-permute-start | bytes 49160 | tf_op jit(solution)/shard_map/ppermute | solution.py:772
  169.8 1.7 collective-permute-done.24
  171.5 2.0 collective-permute-start.36
  173.5 3.3 %collective-permute-done.27.refs_2_ = f32[128,512]{1,0:T(8,128)S(1)} collective-permute-done((f32[128,512]{1,0:T(8,128)S(1)}, f32[128,512]{1,0:T(8,128)S(1)}, u32[]{:S(2)}, u32[]{:S(2)}) %collective-permute-start.27) | collective-permute-done | bytes 262176 | tf_op jit(solution)/shard_map/ppermute | solution.py:772
  176.8 3.2 %collective-permute-start.25 = (f32[4,8,128]{2,1,0:T(8,128)S(1)}, f32[4,8,128]{2,1,0:T(8,128)S(1)}, u32[]{:S(2)}, u32[]{:S(2)}) collective-permute-start(f32[4,8,128]{2,1,0:T(8,128)S(1)} %add.27), channel_id=1, source_target_pairs={{0,16},{4,20},{8,24},{12,28},{16,0},{20,4},{24,8},{28,12},{1,17},{... | collective-permute-start | bytes 49160 | tf_op jit(solution)/shard_map/ppermute | solution.py:772
  180.1 1.7 collective-permute-done.25
  182.4 1.4 collective-permute-start.31
  183.8 17.4 %collective-permute-done.28.refs_3_ = f32[128,512]{1,0:T(8,128)S(1)} collective-permute-done((f32[128,512]{1,0:T(8,128)S(1)}, f32[128,512]{1,0:T(8,128)S(1)}, u32[]{:S(2)}, u32[]{:S(2)}) %collective-permute-start.28) | collective-permute-done | bytes 262176 | tf_op jit(solution)/shard_map/ppermute | solution.py:772
  201.2 5.6 %collective-permute-done.29.refs_5_ = f32[128,512]{1,0:T(8,128)S(1)} collective-permute-done((f32[128,512]{1,0:T(8,128)S(1)}, f32[128,512]{1,0:T(8,128)S(1)}, u32[]{:S(2)}, u32[]{:S(2)}) %collective-permute-start.29) | collective-permute-done | bytes 262176 | tf_op jit(solution)/shard_map/ppermute | solution.py:772
  206.8 5.5 %collective-permute-done.31.refs_7_ = f32[128,512]{1,0:T(8,128)S(1)} collective-permute-done((f32[128,512]{1,0:T(8,128)S(1)}, f32[128,512]{1,0:T(8,128)S(1)}, u32[]{:S(2)}, u32[]{:S(2)}) %collective-permute-start.31) | collective-permute-done | bytes 262176 | tf_op jit(solution)/shard_map/ppermute | solution.py:772
  212.3 2.0 solution_image.1
  214.4 1.8 residual_image.1
  (52 shorter events, 11.2 us)
Async XLA Ops:
  0.6 9.0 %copy-start = (f32[128,2048]{1,0:T(8,128)S(1)}, f32[128,2048]{1,0:T(8,128)}, u32[]{:S(2)}) copy-start(f32[128,2048]{1,0:T(8,128)} %est.5) | copy-start | bytes 3145732
  1.8 4.3 %collective-permute-start = (f32[32,2048]{1,0:T(8,128)S(1)}, f32[32,2048]{1,0:T(8,128)S(1)}, u32[]{:S(2)}, u32[]{:S(2)}) collective-permute-start(f32[32,2048]{1,0:T(8,128)S(1)} %get-tuple-element.91), channel_id=1, source_target_pairs={{0,4},{8,12},{16,20},{24,28},{4,0},{12,8},{20,16},{28,24},{1,5},{9... | collective-permute-start | bytes 786440 | tf_op jit(solution)/shard_map/ppermute | solution.py:766
  1.9 7.7 %collective-permute-start.1 = (f32[32,2048]{1,0:T(8,128)S(1)}, f32[32,2048]{1,0:T(8,128)S(1)}, u32[]{:S(2)}, u32[]{:S(2)}) collective-permute-start(f32[32,2048]{1,0:T(8,128)S(1)} %get-tuple-element.90), channel_id=1, source_target_pairs={{4,8},{12,16},{20,24},{8,4},{16,12},{24,20},{5,9},{13,17},{21,25},... | collective-permute-start | bytes 786440 | tf_op jit(solution)/shard_map/ppermute | solution.py:766
  16.1 5.6 %collective-permute-start.2 = (f32[32,2048]{1,0:T(8,128)S(1)}, f32[32,2048]{1,0:T(8,128)S(1)}, u32[]{:S(2)}, u32[]{:S(2)}) collective-permute-start(f32[32,2048]{1,0:T(8,128)S(1)} %get-tuple-element.50.send_a), channel_id=1, source_target_pairs={{0,4},{8,12},{16,20},{24,28},{4,0},{12,8},{20,16},{28,24},{1,5},{9... | collective-permute-start | bytes 786440 | tf_op jit(solution)/shard_map/ppermute | solution.py:766
  19.7 8.4 %collective-permute-start.3 = (f32[32,2048]{1,0:T(8,128)S(1)}, f32[32,2048]{1,0:T(8,128)S(1)}, u32[]{:S(2)}, u32[]{:S(2)}) collective-permute-start(f32[32,2048]{1,0:T(8,128)S(1)} %get-tuple-element.52.send_b), channel_id=1, source_target_pairs={{4,8},{12,16},{20,24},{8,4},{16,12},{24,20},{5,9},{13,17},{21,25},... | collective-permute-start | bytes 786440 | tf_op jit(solution)/shard_map/ppermute | solution.py:766
  29.1 9.4 %collective-permute-start.4 = (f32[144,512]{1,0:T(8,128)S(1)}, f32[144,512]{1,0:T(8,128)S(1)}, u32[]{:S(2)}, u32[]{:S(2)}) collective-permute-start(f32[144,512]{1,0:T(8,128)S(1)} %get-tuple-element.55), channel_id=1, source_target_pairs={{0,1},{1,0},{2,3},{3,2},{4,5},{5,4},{6,7},{7,6},{8,9},{9,8},{10,11... | collective-permute-start | bytes 884744 | tf_op jit(solution)/shard_map/ppermute | solution.py:772
  30.1 18.4 %collective-permute-start.6 = (f32[144,512]{1,0:T(8,128)S(1)}, f32[144,512]{1,0:T(8,128)S(1)}, u32[]{:S(2)}, u32[]{:S(2)}) collective-permute-start(f32[144,512]{1,0:T(8,128)S(1)} %get-tuple-element.56), channel_id=1, source_target_pairs={{0,1},{1,0},{2,3},{3,2},{4,5},{5,4},{6,7},{7,6},{8,9},{9,8},{10,11... | collective-permute-start | bytes 884744 | tf_op jit(solution)/shard_map/ppermute | solution.py:772
  38.6 17.1 %collective-permute-start.5 = (f32[144,512]{1,0:T(8,128)S(1)}, f32[144,512]{1,0:T(8,128)S(1)}, u32[]{:S(2)}, u32[]{:S(2)}) collective-permute-start(f32[144,512]{1,0:T(8,128)S(1)} %add.23), channel_id=1, source_target_pairs={{0,2},{1,3},{2,0},{3,1},{4,6},{5,7},{6,4},{7,5},{8,10},{9,11},{10,... | collective-permute-start | bytes 884744 | tf_op jit(solution)/shard_map/ppermute | solution.py:772
  39.9 40.8 %collective-permute-start.9 = (f32[264,512]{1,0:T(8,128)S(1)}, f32[264,512]{1,0:T(8,128)S(1)}, u32[]{:S(2)}, u32[]{:S(2)}) collective-permute-start(f32[264,512]{1,0:T(8,128)S(1)} %get-tuple-element.62), channel_id=1, source_target_pairs={{0,1},{1,0},{2,3},{3,2},{4,5},{5,4},{6,7},{7,6},{8,9},{9,8},{10,11... | collective-permute-start | bytes 1622024 | tf_op jit(solution)/shard_map/ppermute | solution.py:805
  41.5 45.5 %collective-permute-start.12 = (f32[256,512]{1,0:T(8,128)S(1)}, f32[256,512]{1,0:T(8,128)S(1)}, u32[]{:S(2)}, u32[]{:S(2)}) collective-permute-start(f32[256,512]{1,0:T(8,128)S(1)} %get-tuple-element.67), channel_id=1, source_target_pairs={{1,3},{2,0},{5,7},{6,4},{9,11},{10,8},{13,15},{14,12},{17,19},{18,... | collective-permute-start | bytes 1572872 | tf_op jit(solution)/shard_map/ppermute | solution.py:805
  42.8 45.6 %collective-permute-start.13 = (f32[256,512]{1,0:T(8,128)S(1)}, f32[256,512]{1,0:T(8,128)S(1)}, u32[]{:S(2)}, u32[]{:S(2)}) collective-permute-start(f32[256,512]{1,0:T(8,128)S(1)} %get-tuple-element.68), channel_id=1, source_target_pairs={{1,2},{2,1},{5,6},{6,5},{9,10},{10,9},{13,14},{14,13},{17,18},{18,... | collective-permute-start | bytes 1572872 | tf_op jit(solution)/shard_map/ppermute | solution.py:805
  48.6 30.1 %collective-permute-start.10 = (f32[8,256]{1,0:T(8,128)S(1)}, f32[8,256]{1,0:T(8,128)S(1)}, u32[]{:S(2)}, u32[]{:S(2)}) collective-permute-start(f32[8,256]{1,0:T(8,128)S(1)} %slice.18), channel_id=1, source_target_pairs={{0,2},{1,3},{2,0},{3,1},{4,6},{5,7},{6,4},{7,5},{8,10},{9,11},{10,... | collective-permute-start | bytes 24584 | tf_op jit(solution)/shard_map/ppermute | solution.py:772
  55.7 23.1 %collective-permute-start.11 = (f32[8,256]{1,0:T(8,128)S(1)}, f32[8,256]{1,0:T(8,128)S(1)}, u32[]{:S(2)}, u32[]{:S(2)}) collective-permute-start(f32[8,256]{1,0:T(8,128)S(1)} %slice.18), channel_id=1, source_target_pairs={{0,3},{1,2},{2,1},{3,0},{4,7},{5,6},{6,5},{7,4},{8,11},{9,10},{10,... | collective-permute-start | bytes 24584 | tf_op jit(solution)/shard_map/ppermute | solution.py:772
  78.6 11.0 %collective-permute-start.7 = (f32[32,768]{1,0:T(8,128)S(1)}, f32[32,768]{1,0:T(8,128)S(1)}, u32[]{:S(2)}, u32[]{:S(2)}) collective-permute-start(f32[32,768]{1,0:T(8,128)S(1)} %get-tuple-element.59), channel_id=1, source_target_pairs={{0,4},{8,12},{16,20},{24,28},{4,0},{12,8},{20,16},{28,24},{1,5},{9... | collective-permute-start | bytes 294920 | tf_op jit(solution)/shard_map/ppermute | solution.py:766
  78.8 10.9 %collective-permute-start.8 = (f32[32,768]{1,0:T(8,128)S(1)}, f32[32,768]{1,0:T(8,128)S(1)}, u32[]{:S(2)}, u32[]{:S(2)}) collective-permute-start(f32[32,768]{1,0:T(8,128)S(1)} %get-tuple-element.60), channel_id=1, source_target_pairs={{4,8},{12,16},{20,24},{8,4},{16,12},{24,20},{5,9},{13,17},{21,25},... | collective-permute-start | bytes 294920 | tf_op jit(solution)/shard_map/ppermute | solution.py:766
  80.7 26.8 %collective-permute-start.16 = (f32[256,512]{1,0:T(8,128)S(1)}, f32[256,512]{1,0:T(8,128)S(1)}, u32[]{:S(2)}, u32[]{:S(2)}) collective-permute-start(f32[256,512]{1,0:T(8,128)S(1)} %get-tuple-element.68), channel_id=1, source_target_pairs={{0,3},{3,0},{4,7},{7,4},{8,11},{11,8},{12,15},{15,12},{16,19},{19,... | collective-permute-start | bytes 1572872 | tf_op jit(solution)/shard_map/ppermute | solution.py:805
  87.0 15.8 %collective-permute-start.14 = (f32[128,512]{1,0:T(8,128)S(1)}, f32[128,512]{1,0:T(8,128)S(1)}, u32[]{:S(2)}, u32[]{:S(2)}) collective-permute-start(f32[128,512]{1,0:T(8,128)S(1)} %get-tuple-element.93), channel_id=1, source_target_pairs={{0,2},{3,1},{4,6},{7,5},{8,10},{11,9},{12,14},{15,13},{16,18},{19,... | collective-permute-start | bytes 786440 | tf_op jit(solution)/shard_map/ppermute | solution.py:805
  88.3 19.1 %collective-permute-start.15 = (f32[128,512]{1,0:T(8,128)S(1)}, f32[128,512]{1,0:T(8,128)S(1)}, u32[]{:S(2)}, u32[]{:S(2)}) collective-permute-start(f32[128,512]{1,0:T(8,128)S(1)} %get-tuple-element.92), channel_id=1, source_target_pairs={{0,2},{3,1},{4,6},{7,5},{8,10},{11,9},{12,14},{15,13},{16,18},{19,... | collective-permute-start | bytes 786440 | tf_op jit(solution)/shard_map/ppermute | solution.py:805
  110.6 2.0 collective-permute-start.17
  110.7 6.6 %collective-permute-start.18 = (f32[64,640]{1,0:T(8,128)S(1)}, f32[64,640]{1,0:T(8,128)S(1)}, u32[]{:S(2)}, u32[]{:S(2)}) collective-permute-start(f32[64,640]{1,0:T(8,128)S(1)} %get-tuple-element.75.send_b), channel_id=1, source_target_pairs={{4,8},{12,16},{20,24},{8,4},{16,12},{24,20},{5,9},{13,17},{21,25},... | collective-permute-start | bytes 491528 | tf_op jit(solution)/shard_map/ppermute | solution.py:766
  118.0 6.0 %collective-permute-start.19 = (f32[192,128]{1,0:T(8,128)S(1)}, f32[192,128]{1,0:T(8,128)S(1)}, u32[]{:S(2)}, u32[]{:S(2)}) collective-permute-start(f32[192,128]{1,0:T(8,128)S(1)} %get-tuple-element.77), channel_id=1, source_target_pairs={{0,1},{2,3},{1,0},{3,2},{4,5},{6,7},{5,4},{7,6},{8,9},{10,11},{9,8... | collective-permute-start | bytes 294920 | tf_op jit(solution)/shard_map/ppermute | solution.py:766
  121.1 3.0 %collective-permute-start.20 = (f32[192,128]{1,0:T(8,128)S(1)}, f32[192,128]{1,0:T(8,128)S(1)}, u32[]{:S(2)}, u32[]{:S(2)}) collective-permute-start(f32[192,128]{1,0:T(8,128)S(1)} %get-tuple-element.78), channel_id=1, source_target_pairs={{1,2},{2,1},{5,6},{6,5},{9,10},{10,9},{13,14},{14,13},{17,18},{18,... | collective-permute-start | bytes 294920 | tf_op jit(solution)/shard_map/ppermute | solution.py:766
  134.1 6.5 %collective-permute-start.32 = (f32[32,640]{1,0:T(8,128)S(1)}, f32[32,640]{1,0:T(8,128)S(1)}, u32[]{:S(2)}, u32[]{:S(2)}) collective-permute-start(f32[32,640]{1,0:T(8,128)S(1)} %get-tuple-element.87.send_a), channel_id=1, source_target_pairs={{0,4},{8,12},{16,20},{24,28},{4,0},{12,8},{20,16},{28,24},{1,5},{9... | collective-permute-start | bytes 245768 | tf_op jit(solution)/shard_map/ppermute | solution.py:766
  134.6 5.9 %collective-permute-start.33 = (f32[32,640]{1,0:T(8,128)S(1)}, f32[32,640]{1,0:T(8,128)S(1)}, u32[]{:S(2)}, u32[]{:S(2)}) collective-permute-start(f32[32,640]{1,0:T(8,128)S(1)} %get-tuple-element.89.send_b), channel_id=1, source_target_pairs={{4,8},{12,16},{20,24},{8,4},{16,12},{24,20},{5,9},{13,17},{21,25},... | collective-permute-start | bytes 245768 | tf_op jit(solution)/shard_map/ppermute | solution.py:766
  136.6 8.9 %collective-permute-start.21 = (f32[4,8,128]{2,1,0:T(8,128)S(1)}, f32[4,8,128]{2,1,0:T(8,128)S(1)}, u32[]{:S(2)}, u32[]{:S(2)}) collective-permute-start(f32[4,8,128]{2,1,0:T(8,128)S(1)} %pad_maximum_fusion), channel_id=1, source_target_pairs={{0,1},{1,0},{2,3},{3,2},{4,5},{5,4},{6,7},{7,6},{8,9},{9,8},{10,11... | collective-permute-start | bytes 49160 | tf_op jit(solution)/shard_map/ppermute | solution.py:772
  141.3 30.2 %collective-permute-start.35 = (f32[144,512]{1,0:T(8,128)S(1)}, f32[144,512]{1,0:T(8,128)S(1)}, u32[]{:S(2)}, u32[]{:S(2)}) collective-permute-start(f32[144,512]{1,0:T(8,128)S(1)} %wrap.1.refs_0_), channel_id=1, source_target_pairs={{0,2},{1,3},{2,0},{3,1},{4,6},{5,7},{6,4},{7,5},{8,10},{9,11},{10,... | collective-permute-start | bytes 884744 | tf_op jit(solution)/shard_map/ppermute | solution.py:772
  145.5 20.0 %collective-permute-start.22 = (f32[4,8,128]{2,1,0:T(8,128)S(1)}, f32[4,8,128]{2,1,0:T(8,128)S(1)}, u32[]{:S(2)}, u32[]{:S(2)}) collective-permute-start(f32[4,8,128]{2,1,0:T(8,128)S(1)} %fusion), channel_id=1, source_target_pairs={{0,2},{1,3},{2,0},{3,1},{4,6},{5,7},{6,4},{7,5},{8,10},{9,11},{10,... | collective-permute-start | bytes 49160 | tf_op jit(solution)/shard_map/ppermute | solution.py:772
  145.6 31.2 %collective-permute-start.27 = (f32[128,512]{1,0:T(8,128)S(1)}, f32[128,512]{1,0:T(8,128)S(1)}, u32[]{:S(2)}, u32[]{:S(2)}) collective-permute-start(f32[128,512]{1,0:T(8,128)S(1)} %get-tuple-element.82.refs_0_), channel_id=1, source_target_pairs={{0,2},{1,3},{2,0},{3,1},{4,6},{5,7},{6,4},{7,5},{8,10},{9,11},{10,... | collective-permute-start | bytes 786440 | tf_op jit(solution)/shard_map/ppermute | solution.py:772
  148.5 31.6 %collective-permute-start.26 = (f32[128,512]{1,0:T(8,128)S(1)}, f32[128,512]{1,0:T(8,128)S(1)}, u32[]{:S(2)}, u32[]{:S(2)}) collective-permute-start(f32[128,512]{1,0:T(8,128)S(1)} %get-tuple-element.82.refs_0_), channel_id=1, source_target_pairs={{0,1},{1,0},{2,3},{3,2},{4,5},{5,4},{6,7},{7,6},{8,9},{9,8},{10,11... | collective-permute-start | bytes 786440 | tf_op jit(solution)/shard_map/ppermute | solution.py:772
  148.5 34.0 %collective-permute-start.30 = (f32[128,512]{1,0:T(8,128)S(1)}, f32[128,512]{1,0:T(8,128)S(1)}, u32[]{:S(2)}, u32[]{:S(2)}) collective-permute-start(f32[128,512]{1,0:T(8,128)S(1)} %get-tuple-element.83.refs_4_.before), channel_id=1, source_target_pairs={{0,2},{1,3},{2,0},{3,1},{4,6},{5,7},{6,4},{7,5},{8,10},{9,11},{10,... | collective-permute-start | bytes 786440 | tf_op jit(solution)/shard_map/ppermute | solution.py:772
  165.5 1.9 collective-permute-start.23
  167.4 4.1 %collective-permute-start.24 = (f32[4,8,128]{2,1,0:T(8,128)S(1)}, f32[4,8,128]{2,1,0:T(8,128)S(1)}, u32[]{:S(2)}, u32[]{:S(2)}) collective-permute-start(f32[4,8,128]{2,1,0:T(8,128)S(1)} %add.26), channel_id=1, source_target_pairs={{0,8},{4,12},{8,0},{12,4},{16,24},{20,28},{24,16},{28,20},{1,9},{5... | collective-permute-start | bytes 49160 | tf_op jit(solution)/shard_map/ppermute | solution.py:772
  171.5 42.9 %collective-permute-start.34 = (f32[144,512]{1,0:T(8,128)S(1)}, f32[144,512]{1,0:T(8,128)S(1)}, u32[]{:S(2)}, u32[]{:S(2)}) collective-permute-start(f32[144,512]{1,0:T(8,128)S(1)} %wrap.1.refs_0_), channel_id=1, source_target_pairs={{0,1},{1,0},{2,3},{3,2},{4,5},{5,4},{6,7},{7,6},{8,9},{9,8},{10,11... | collective-permute-start | bytes 884744 | tf_op jit(solution)/shard_map/ppermute | solution.py:772
  171.5 42.9 %collective-permute-start.36 = (f32[144,512]{1,0:T(8,128)S(1)}, f32[144,512]{1,0:T(8,128)S(1)}, u32[]{:S(2)}, u32[]{:S(2)}) collective-permute-start(f32[144,512]{1,0:T(8,128)S(1)} %collective-permute-done.35.refs_2_), channel_id=1, source_target_pairs={{0,1},{1,0},{2,3},{3,2},{4,5},{5,4},{6,7},{7,6},{8,9},{9,8},{10,11... | collective-permute-start | bytes 884744 | tf_op jit(solution)/shard_map/ppermute | solution.py:772
  176.8 4.9 %collective-permute-start.25 = (f32[4,8,128]{2,1,0:T(8,128)S(1)}, f32[4,8,128]{2,1,0:T(8,128)S(1)}, u32[]{:S(2)}, u32[]{:S(2)}) collective-permute-start(f32[4,8,128]{2,1,0:T(8,128)S(1)} %add.27), channel_id=1, source_target_pairs={{0,16},{4,20},{8,24},{12,28},{16,0},{20,4},{24,8},{28,12},{1,17},{... | collective-permute-start | bytes 49160 | tf_op jit(solution)/shard_map/ppermute | solution.py:772
  180.1 21.1 %collective-permute-start.28 = (f32[128,512]{1,0:T(8,128)S(1)}, f32[128,512]{1,0:T(8,128)S(1)}, u32[]{:S(2)}, u32[]{:S(2)}) collective-permute-start(f32[128,512]{1,0:T(8,128)S(1)} %collective-permute-done.27.refs_2_), channel_id=1, source_target_pairs={{0,1},{1,0},{2,3},{3,2},{4,5},{5,4},{6,7},{7,6},{8,9},{9,8},{10,11... | collective-permute-start | bytes 786440 | tf_op jit(solution)/shard_map/ppermute | solution.py:772
  181.8 25.0 %collective-permute-start.29 = (f32[128,512]{1,0:T(8,128)S(1)}, f32[128,512]{1,0:T(8,128)S(1)}, u32[]{:S(2)}, u32[]{:S(2)}) collective-permute-start(f32[128,512]{1,0:T(8,128)S(1)} %get-tuple-element.83.refs_4_.before), channel_id=1, source_target_pairs={{0,1},{1,0},{2,3},{3,2},{4,5},{5,4},{6,7},{7,6},{8,9},{9,8},{10,11... | collective-permute-start | bytes 786440 | tf_op jit(solution)/shard_map/ppermute | solution.py:772
  182.4 29.9 %collective-permute-start.31 = (f32[128,512]{1,0:T(8,128)S(1)}, f32[128,512]{1,0:T(8,128)S(1)}, u32[]{:S(2)}, u32[]{:S(2)}) collective-permute-start(f32[128,512]{1,0:T(8,128)S(1)} %collective-permute-done.30.refs_6_), channel_id=1, source_target_pairs={{0,1},{1,0},{2,3},{3,2},{4,5},{5,4},{6,7},{7,6},{8,9},{9,8},{10,11... | collective-permute-start | bytes 786440 | tf_op jit(solution)/shard_map/ppermute | solution.py:772

commit v7 on v5

--- a/solution.py
+++ b/solution.py
@@ -155,13 +155,21 @@
     y_lo[:ext, :] = lo
 
 
+def three_products(left, hi, lo, rows, c, size):
+    span = slice(c, c + size)
+    if size == LANE:
+        r = dot(left[...], jnp.concatenate([hi[:, span], lo[:, span]], axis=1))
+        return r[:rows, :LANE] + r[rows:, :LANE] + r[:rows, LANE:]
+    r = dot(left[...], hi[:, span])
+    return r[:rows] + r[rows:] + dot(left[:rows, :], lo[:, span])
+
+
 def group_terms(frames, rows, w, y_hi, y_lo, t, b, bp, ta, weight, data, us, qs, vs_hi, vs_lo, acc, stat, ready=None):
     total = None
     for f in range(frames):
         for c, size in tiles(w + LANE):
-            r1 = dot(t(f)[...], y_hi[:, c : c + size])
-            r2 = dot(t(f)[:rows, :], y_lo[:, c : c + size])
-            hi, lo = split(r1[:rows] + r1[rows:] + r2)
+            r = three_products(t(f), y_hi, y_lo, rows, c, size)
+            hi, lo = split(r)
             us[:rows, c : c + size] = hi
             us[rows:, c : c + size] = lo
         if ready is not None:
@@ -187,9 +195,7 @@
             vs_lo[f * rows : (f + 1) * rows, c : c + LANE] = lo
     ext = acc.shape[0]
     for c, size in tiles(w + LANE):
-        r1 = dot(ta[...], vs_hi[:, c : c + size])
-        r2 = dot(ta[:ext, :], vs_lo[:, c : c + size])
-        acc[:, c : c + size] += r1[:ext] + r1[ext:] + r2
+        acc[:, c : c + size] += three_products(ta, vs_hi, vs_lo, ext, c, size)
     if stat is not None:
         stat[...] += total
 

time: 219 us -> 219 us (level)
  no operation moved by 1% of the time
where the time goes in v7:
time: 219 us; the launch traced here: 217 us
  waiting for transfers between devices  118 us (54%)
  starting transfers between devices  59.6 us (27%)
  Pallas kernels  37.2 us (17%)
    ppermute x20, waiting for transfers between devices, swap(): return lax.ppermute(x, axis, [(i, i ^ distance) for i in range(n)])  86.9 us
    ppermute x20, starting transfers between devices, swap(): return lax.ppermute(x, axis, [(i, i ^ distance) for i in range(n)])  35.1 us
    ppermute x12, waiting for transfers between devices, neighbours(): out.append(lax.ppermute(x, axis, pairs + [(b, a) for a, b in pairs]))  19.8 us
    pallas_call x3, Pallas kernels, apply_terms(): pl.pallas_call(functools.partial(apply_kernel, n, frames, rows, halo, w,...  19.4 us
    ppermute x12, starting transfers between devices, neighbours(): out.append(lax.ppermute(x, axis, pairs + [(b, a) for a, b in pairs]))  15.5 us
    ppermute x4, waiting for transfers between devices, steps(): moved.append(lax.ppermute(packed[d - 1], 'frame', pairs))  11.4 us
    ppermute x4, starting transfers between devices, steps(): moved.append(lax.ppermute(packed[d - 1], 'frame', pairs))  9.05 us
    pallas_call x1, Pallas kernels, first_terms(): pl.pallas_call(functools.partial(first_kernel, frames, rows, halo), out_s...  5.93 us
  transfers between devices with their start and end apart: 36, of which 18 were waited for; matrix products, arithmetic and copies ran while one was open for 0% of the time, Pallas kernels for 7%

profile of v7, /device:TPU:2, one launch (start us, length us, event | category | flops | bytes accessed | tf_op | source)
XLA Modules:
  0.0 217.1 jit_solution(13890451471579610197)
XLA Ops:
  0.7 1.2 slice_select_fusion
  1.9 1.9 collective-permute-start.1
  3.9 2.2 %prepare.1 = (f32[264,512]{1,0:T(8,128)S(1)}, f32[256,512]{1,0:T(8,128)S(1)}, f32[256,512]{1,0:T(8,128)S(1)}, f32[8,512]{1,0:T(8,128)S(1)}, bf16[2,256,256]{2,1,...) custom-call(s32[2]{0:T(128)S(1)} %pad_add_fusion.place, ...), custom_call_target="tpu_custom_call" | custom-call | tf_op jit(solution)/shard_map/prepare/pallas_call | solution.py:356
  6.1 3.4 %collective-permute-done.1.recv_b = f32[32,2048]{1,0:T(8,128)S(1)} collective-permute-done((f32[32,2048]{1,0:T(8,128)S(1)}, f32[32,2048]{1,0:T(8,128)S(1)}, u32[]{:S(2)}, u32[]{:S(2)}) %collective-permute-start.1) | collective-permute-done | bytes 262176 | tf_op jit(solution)/shard_map/ppermute | solution.py:769
  9.6 5.9 %first_terms.1 = (f32[32,2048]{1,0:T(8,128)S(1)}, f32[128,2048]{1,0:T(8,128)S(1)}, f32[32,2048]{1,0:T(8,128)S(1)}) custom-call(s32[2]{0:T(128)S(1)} %pad_add_fusion.place, f32[128,2048]{1,0:T(8,128)S(1)} %copy-done, f32[32,2048]{1,0:T(8,128)S(1)} %collective-permute-done.recv_a, f32[32,2048]{1,0:T(8,128)S(1)} %collective-permute-done.1.recv_b, ...), custom_call_target="tpu_custom_call" | custom-call | flops 8000000000 | bytes 8388608 | tf_op jit(solution)/shard_map/first_terms/pallas_call | solution.py:298
  15.5 3.6 %collective-permute-start.2 = (f32[32,2048]{1,0:T(8,128)S(1)}, f32[32,2048]{1,0:T(8,128)S(1)}, u32[]{:S(2)}, u32[]{:S(2)}) collective-permute-start(f32[32,2048]{1,0:T(8,128)S(1)} %get-tuple-element.50.send_a), channel_id=1, source_target_pairs={{0,4},{8,12},{16,20},{24,28},{4,0},{12,8},{20,16},{28,24},{1,5},{9... | collective-permute-start | bytes 786440 | tf_op jit(solution)/shard_map/ppermute | solution.py:769
  19.2 1.9 collective-permute-start.3
  21.1 6.5 %collective-permute-done.3.recv_b = f32[32,2048]{1,0:T(8,128)S(1)} collective-permute-done((f32[32,2048]{1,0:T(8,128)S(1)}, f32[32,2048]{1,0:T(8,128)S(1)}, u32[]{:S(2)}, u32[]{:S(2)}) %collective-permute-start.3) | collective-permute-done | bytes 262176 | tf_op jit(solution)/shard_map/ppermute | solution.py:769
  28.5 1.0 collective-permute-start.4
  29.6 1.1 collective-permute-start.9
  30.6 1.3 collective-permute-start.12
  32.6 5.5 %collective-permute-start.6 = (f32[144,512]{1,0:T(8,128)S(1)}, f32[144,512]{1,0:T(8,128)S(1)}, u32[]{:S(2)}, u32[]{:S(2)}) collective-permute-start(f32[144,512]{1,0:T(8,128)S(1)} %get-tuple-element.56), channel_id=1, source_target_pairs={{0,1},{1,0},{2,3},{3,2},{4,5},{5,4},{6,7},{7,6},{8,9},{9,8},{10,11... | collective-permute-start | bytes 884744 | tf_op jit(solution)/shard_map/ppermute | solution.py:775
  38.1 11.1 %collective-permute-done.4 = f32[144,512]{1,0:T(8,128)S(1)} collective-permute-done((f32[144,512]{1,0:T(8,128)S(1)}, f32[144,512]{1,0:T(8,128)S(1)}, u32[]{:S(2)}, u32[]{:S(2)}) %collective-permute-start.4) | collective-permute-done | bytes 294944 | tf_op jit(solution)/shard_map/ppermute | solution.py:775
  49.4 24.1 %collective-permute-done.6.refs_2_ = f32[144,512]{1,0:T(8,128)S(1)} collective-permute-done((f32[144,512]{1,0:T(8,128)S(1)}, f32[144,512]{1,0:T(8,128)S(1)}, u32[]{:S(2)}, u32[]{:S(2)}) %collective-permute-start.6) | collective-permute-done | bytes 294944 | tf_op jit(solution)/shard_map/ppermute | solution.py:775
  73.7 2.1 collective-permute-start.11
  76.4 1.6 collective-permute-done.10.refs_2_
  78.0 1.1 collective-permute-done.11.refs_3_
  79.1 1.9 collective-permute-start.8
  81.0 2.9 %collective-permute-start.14 = (f32[256,512]{1,0:T(8,128)S(1)}, f32[256,512]{1,0:T(8,128)S(1)}, u32[]{:S(2)}, u32[]{:S(2)}) collective-permute-start(f32[256,512]{1,0:T(8,128)S(1)} %get-tuple-element.67), channel_id=1, source_target_pairs={{0,2},{3,1},{4,6},{7,5},{8,10},{11,9},{12,14},{15,13},{16,18},{19,... | collective-permute-start | bytes 1572872 | tf_op jit(solution)/shard_map/ppermute | solution.py:816
  83.9 2.1 setup_all.1
  86.0 4.2 %collective-permute-start.15 = (f32[256,512]{1,0:T(8,128)S(1)}, f32[256,512]{1,0:T(8,128)S(1)}, u32[]{:S(2)}, u32[]{:S(2)}) collective-permute-start(f32[256,512]{1,0:T(8,128)S(1)} %get-tuple-element.68), channel_id=1, source_target_pairs={{0,3},{3,0},{4,7},{7,4},{8,11},{11,8},{12,15},{15,12},{16,19},{19,... | collective-permute-start | bytes 1572872 | tf_op jit(solution)/shard_map/ppermute | solution.py:816
  90.3 7.0 %shard_map.68 = (f32[192,640]{1,0:T(8,128)S(1)}, f32[8,128]{1,0:T(8,128)S(1)}, f32[192,768]{1,0:T(8,128)S(1)}) custom-call(s32[2]{0:T(128)S(1)} %pad_add_fusion.place, f32[128,768]{1,0:T(8,128)S(1)} %get-tuple-element.58.refs_0_, f32[32,768]{1,0:T(8,128)S(1)} %collective-permute-done.7.refs_1_, f32[32,768]{1,0:T(8,128)S(1)} %collective-permute-done.8.refs_2_, ...), custom_call_target="tpu_custom_call" | custom-call | flops 8999999488 | bytes 3145728 | tf_op jit(solution)/shard_map/pallas_call | solution.py:553
  97.3 11.4 %collective-permute-done.15.refs_10_ = f32[256,512]{1,0:T(8,128)S(1)} collective-permute-done((f32[256,512]{1,0:T(8,128)S(1)}, f32[256,512]{1,0:T(8,128)S(1)}, u32[]{:S(2)}, u32[]{:S(2)}) %collective-permute-start.15) | collective-permute-done | bytes 524320 | tf_op jit(solution)/shard_map/ppermute | solution.py:816
  108.7 3.1 %shard_map.69 = (f32[64,640]{1,0:T(8,128)S(1)}, f32[64,640]{1,0:T(8,128)S(1)}, f32[64,640]{1,0:T(8,128)S(1)}, f32[8,128]{1,0:T(8,128)S(1)}) custom-call(s32[2]{0:T(128)S(1)} %pad_add_fusion.place, f32[192,768]{1,0:T(8,128)S(1)} %get-tuple-element.69.refs_0_.before, bf16[8,256,256]{2,1,0:T(8,128)(2,1)S(1)} %get-tuple-element.63.refs_3_.refs_1_, ...), custom_call_target="tpu_custom_call" | custom-call | flops 3000000000 | bytes 1048576 | tf_op jit(solution)/shard_map/pallas_call | solution.py:553
  111.9 1.4 collective-permute-start.16
  113.2 1.9 collective-permute-start.17
  115.1 4.7 %collective-permute-done.17.recv_b = f32[64,640]{1,0:T(8,128)S(1)} collective-permute-done((f32[64,640]{1,0:T(8,128)S(1)}, f32[64,640]{1,0:T(8,128)S(1)}, u32[]{:S(2)}, u32[]{:S(2)}) %collective-permute-start.17) | collective-permute-done | bytes 163872 | tf_op jit(solution)/shard_map/ppermute | solution.py:769
  121.3 4.9 %collective-permute-done.18.recv_a = f32[192,128]{1,0:T(8,128)S(1)} collective-permute-done((f32[192,128]{1,0:T(8,128)S(1)}, f32[192,128]{1,0:T(8,128)S(1)}, u32[]{:S(2)}, u32[]{:S(2)}) %collective-permute-start.18) | collective-permute-done | bytes 98336 | tf_op jit(solution)/shard_map/ppermute | solution.py:769
  126.9 9.2 %shard_map.70 = (f32[32,640]{1,0:T(8,128)S(1)}, f32[128,640]{1,0:T(8,128)S(1)}, f32[32,640]{1,0:T(8,128)S(1)}, f32[8,128]{1,0:T(8,128)S(1)}) custom-call(s32[2]{0:T(128)S(1)} %pad_add_fusion.place, f32[192,768]{1,0:T(8,128)S(1)} %get-tuple-element.80.refs_0_, bf16[8,256,256]{2,1,0:T(8,128)(2,1)S(1)} %get-tuple-element.63.refs_3_.refs_1_, ...), custom_call_target="tpu_custom_call" | custom-call | flops 12000000000 | bytes 4194304 | tf_op jit(solution)/shard_map/pallas_call | solution.py:553
  136.3 1.9 collective-permute-start.32
  138.2 3.6 %collective-permute-start.20 = (f32[4,8,128]{2,1,0:T(8,128)S(1)}, f32[4,8,128]{2,1,0:T(8,128)S(1)}, u32[]{:S(2)}, u32[]{:S(2)}) collective-permute-start(f32[4,8,128]{2,1,0:T(8,128)S(1)} %pad_maximum_fusion), channel_id=1, source_target_pairs={{0,1},{1,0},{2,3},{3,2},{4,5},{5,4},{6,7},{7,6},{8,9},{9,8},{10,11... | collective-permute-start | bytes 49160 | tf_op jit(solution)/shard_map/ppermute | solution.py:775
  142.7 3.7 %collective-permute-start.34 = (f32[144,512]{1,0:T(8,128)S(1)}, f32[144,512]{1,0:T(8,128)S(1)}, u32[]{:S(2)}, u32[]{:S(2)}) collective-permute-start(f32[144,512]{1,0:T(8,128)S(1)} %wrap.1.refs_0_), channel_id=1, source_target_pairs={{0,2},{1,3},{2,0},{3,1},{4,6},{5,7},{6,4},{7,5},{8,10},{9,11},{10,... | collective-permute-start | bytes 884744 | tf_op jit(solution)/shard_map/ppermute | solution.py:775
  146.5 2.9 %collective-permute-start.26 = (f32[128,512]{1,0:T(8,128)S(1)}, f32[128,512]{1,0:T(8,128)S(1)}, u32[]{:S(2)}, u32[]{:S(2)}) collective-permute-start(f32[128,512]{1,0:T(8,128)S(1)} %get-tuple-element.82.refs_0_), channel_id=1, source_target_pairs={{0,2},{1,3},{2,0},{3,1},{4,6},{5,7},{6,4},{7,5},{8,10},{9,11},{10,... | collective-permute-start | bytes 786440 | tf_op jit(solution)/shard_map/ppermute | solution.py:775
  149.4 2.8 %collective-permute-start.29 = (f32[128,512]{1,0:T(8,128)S(1)}, f32[128,512]{1,0:T(8,128)S(1)}, u32[]{:S(2)}, u32[]{:S(2)}) collective-permute-start(f32[128,512]{1,0:T(8,128)S(1)} %get-tuple-element.83.refs_4_.before), channel_id=1, source_target_pairs={{0,2},{1,3},{2,0},{3,1},{4,6},{5,7},{6,4},{7,5},{8,10},{9,11},{10,... | collective-permute-start | bytes 786440 | tf_op jit(solution)/shard_map/ppermute | solution.py:775
  152.3 13.7 %collective-permute-done.21 = f32[4,8,128]{2,1,0:T(8,128)S(1)} collective-permute-done((f32[4,8,128]{2,1,0:T(8,128)S(1)}, f32[4,8,128]{2,1,0:T(8,128)S(1)}, u32[]{:S(2)}, u32[]{:S(2)}) %collective-permute-start.21) | collective-permute-done | bytes 16416 | tf_op jit(solution)/shard_map/ppermute | solution.py:775
  166.0 1.9 collective-permute-start.22
  168.7 1.9 collective-permute-start.23
  170.6 1.9 collective-permute-done.23
  172.5 2.0 collective-permute-start.35
  174.5 2.8 %collective-permute-done.26.refs_2_ = f32[128,512]{1,0:T(8,128)S(1)} collective-permute-done((f32[128,512]{1,0:T(8,128)S(1)}, f32[128,512]{1,0:T(8,128)S(1)}, u32[]{:S(2)}, u32[]{:S(2)}) %collective-permute-start.26) | collective-permute-done | bytes 262176 | tf_op jit(solution)/shard_map/ppermute | solution.py:775
  177.3 4.2 %collective-permute-start.24 = (f32[4,8,128]{2,1,0:T(8,128)S(1)}, f32[4,8,128]{2,1,0:T(8,128)S(1)}, u32[]{:S(2)}, u32[]{:S(2)}) collective-permute-start(f32[4,8,128]{2,1,0:T(8,128)S(1)} %add.27), channel_id=1, source_target_pairs={{0,16},{4,20},{8,24},{12,28},{16,0},{20,4},{24,8},{28,12},{1,17},{... | collective-permute-start | bytes 49160 | tf_op jit(solution)/shard_map/ppermute | solution.py:775
  181.5 1.7 collective-permute-done.24
  183.5 1.7 collective-permute-start.30
  185.2 16.8 %collective-permute-done.27.refs_3_ = f32[128,512]{1,0:T(8,128)S(1)} collective-permute-done((f32[128,512]{1,0:T(8,128)S(1)}, f32[128,512]{1,0:T(8,128)S(1)}, u32[]{:S(2)}, u32[]{:S(2)}) %collective-permute-start.27) | collective-permute-done | bytes 262176 | tf_op jit(solution)/shard_map/ppermute | solution.py:775
  202.1 5.6 %collective-permute-done.28.refs_5_ = f32[128,512]{1,0:T(8,128)S(1)} collective-permute-done((f32[128,512]{1,0:T(8,128)S(1)}, f32[128,512]{1,0:T(8,128)S(1)}, u32[]{:S(2)}, u32[]{:S(2)}) %collective-permute-start.28) | collective-permute-done | bytes 262176 | tf_op jit(solution)/shard_map/ppermute | solution.py:775
  207.7 5.5 %collective-permute-done.30.refs_7_ = f32[128,512]{1,0:T(8,128)S(1)} collective-permute-done((f32[128,512]{1,0:T(8,128)S(1)}, f32[128,512]{1,0:T(8,128)S(1)}, u32[]{:S(2)}, u32[]{:S(2)}) %collective-permute-start.30) | collective-permute-done | bytes 262176 | tf_op jit(solution)/shard_map/ppermute | solution.py:775
  213.2 2.0 solution_image.1
  215.3 1.8 residual_image.1
  (49 shorter events, 7.3 us)
Async XLA Ops:
  0.6 9.0 %copy-start = (f32[128,2048]{1,0:T(8,128)S(1)}, f32[128,2048]{1,0:T(8,128)}, u32[]{:S(2)}) copy-start(f32[128,2048]{1,0:T(8,128)} %est.5) | copy-start | bytes 3145732
  1.8 4.3 %collective-permute-start = (f32[32,2048]{1,0:T(8,128)S(1)}, f32[32,2048]{1,0:T(8,128)S(1)}, u32[]{:S(2)}, u32[]{:S(2)}) collective-permute-start(f32[32,2048]{1,0:T(8,128)S(1)} %get-tuple-element.91), channel_id=1, source_target_pairs={{0,4},{8,12},{16,20},{24,28},{4,0},{12,8},{20,16},{28,24},{1,5},{9... | collective-permute-start | bytes 786440 | tf_op jit(solution)/shard_map/ppermute | solution.py:769
  1.9 7.7 %collective-permute-start.1 = (f32[32,2048]{1,0:T(8,128)S(1)}, f32[32,2048]{1,0:T(8,128)S(1)}, u32[]{:S(2)}, u32[]{:S(2)}) collective-permute-start(f32[32,2048]{1,0:T(8,128)S(1)} %get-tuple-element.90), channel_id=1, source_target_pairs={{4,8},{12,16},{20,24},{8,4},{16,12},{24,20},{5,9},{13,17},{21,25},... | collective-permute-start | bytes 786440 | tf_op jit(solution)/shard_map/ppermute | solution.py:769
  15.5 5.6 %collective-permute-start.2 = (f32[32,2048]{1,0:T(8,128)S(1)}, f32[32,2048]{1,0:T(8,128)S(1)}, u32[]{:S(2)}, u32[]{:S(2)}) collective-permute-start(f32[32,2048]{1,0:T(8,128)S(1)} %get-tuple-element.50.send_a), channel_id=1, source_target_pairs={{0,4},{8,12},{16,20},{24,28},{4,0},{12,8},{20,16},{28,24},{1,5},{9... | collective-permute-start | bytes 786440 | tf_op jit(solution)/shard_map/ppermute | solution.py:769
  19.2 8.4 %collective-permute-start.3 = (f32[32,2048]{1,0:T(8,128)S(1)}, f32[32,2048]{1,0:T(8,128)S(1)}, u32[]{:S(2)}, u32[]{:S(2)}) collective-permute-start(f32[32,2048]{1,0:T(8,128)S(1)} %get-tuple-element.52.send_b), channel_id=1, source_target_pairs={{4,8},{12,16},{20,24},{8,4},{16,12},{24,20},{5,9},{13,17},{21,25},... | collective-permute-start | bytes 786440 | tf_op jit(solution)/shard_map/ppermute | solution.py:769
  28.5 20.7 %collective-permute-start.4 = (f32[144,512]{1,0:T(8,128)S(1)}, f32[144,512]{1,0:T(8,128)S(1)}, u32[]{:S(2)}, u32[]{:S(2)}) collective-permute-start(f32[144,512]{1,0:T(8,128)S(1)} %get-tuple-element.55), channel_id=1, source_target_pairs={{0,1},{1,0},{2,3},{3,2},{4,5},{5,4},{6,7},{7,6},{8,9},{9,8},{10,11... | collective-permute-start | bytes 884744 | tf_op jit(solution)/shard_map/ppermute | solution.py:775
  29.6 51.5 %collective-permute-start.9 = (f32[264,512]{1,0:T(8,128)S(1)}, f32[264,512]{1,0:T(8,128)S(1)}, u32[]{:S(2)}, u32[]{:S(2)}) collective-permute-start(f32[264,512]{1,0:T(8,128)S(1)} %get-tuple-element.62), channel_id=1, source_target_pairs={{0,1},{1,0},{2,3},{3,2},{4,5},{5,4},{6,7},{7,6},{8,9},{9,8},{10,11... | collective-permute-start | bytes 1622024 | tf_op jit(solution)/shard_map/ppermute | solution.py:775
  30.6 55.4 %collective-permute-start.12 = (f32[256,512]{1,0:T(8,128)S(1)}, f32[256,512]{1,0:T(8,128)S(1)}, u32[]{:S(2)}, u32[]{:S(2)}) collective-permute-start(f32[256,512]{1,0:T(8,128)S(1)} %get-tuple-element.67), channel_id=1, source_target_pairs={{1,3},{2,0},{5,7},{6,4},{9,11},{10,8},{13,15},{14,12},{17,19},{18,... | collective-permute-start | bytes 1572872 | tf_op jit(solution)/shard_map/ppermute | solution.py:816
  31.9 58.3 %collective-permute-start.13 = (f32[256,512]{1,0:T(8,128)S(1)}, f32[256,512]{1,0:T(8,128)S(1)}, u32[]{:S(2)}, u32[]{:S(2)}) collective-permute-start(f32[256,512]{1,0:T(8,128)S(1)} %get-tuple-element.68), channel_id=1, source_target_pairs={{1,2},{2,1},{5,6},{6,5},{9,10},{10,9},{13,14},{14,13},{17,18},{18,... | collective-permute-start | bytes 1572872 | tf_op jit(solution)/shard_map/ppermute | solution.py:816
  32.6 40.8 %collective-permute-start.6 = (f32[144,512]{1,0:T(8,128)S(1)}, f32[144,512]{1,0:T(8,128)S(1)}, u32[]{:S(2)}, u32[]{:S(2)}) collective-permute-start(f32[144,512]{1,0:T(8,128)S(1)} %get-tuple-element.56), channel_id=1, source_target_pairs={{0,1},{1,0},{2,3},{3,2},{4,5},{5,4},{6,7},{7,6},{8,9},{9,8},{10,11... | collective-permute-start | bytes 884744 | tf_op jit(solution)/shard_map/ppermute | solution.py:775
  49.3 24.4 %collective-permute-start.5 = (f32[144,512]{1,0:T(8,128)S(1)}, f32[144,512]{1,0:T(8,128)S(1)}, u32[]{:S(2)}, u32[]{:S(2)}) collective-permute-start(f32[144,512]{1,0:T(8,128)S(1)} %add.23), channel_id=1, source_target_pairs={{0,2},{1,3},{2,0},{3,1},{4,6},{5,7},{6,4},{7,5},{8,10},{9,11},{10,... | collective-permute-start | bytes 884744 | tf_op jit(solution)/shard_map/ppermute | solution.py:775
  73.5 4.5 %collective-permute-start.10 = (f32[8,256]{1,0:T(8,128)S(1)}, f32[8,256]{1,0:T(8,128)S(1)}, u32[]{:S(2)}, u32[]{:S(2)}) collective-permute-start(f32[8,256]{1,0:T(8,128)S(1)} %slice.12), channel_id=1, source_target_pairs={{0,2},{1,3},{2,0},{3,1},{4,6},{5,7},{6,4},{7,5},{8,10},{9,11},{10,... | collective-permute-start | bytes 24584 | tf_op jit(solution)/shard_map/ppermute | solution.py:775
  73.7 5.4 %collective-permute-start.11 = (f32[8,256]{1,0:T(8,128)S(1)}, f32[8,256]{1,0:T(8,128)S(1)}, u32[]{:S(2)}, u32[]{:S(2)}) collective-permute-start(f32[8,256]{1,0:T(8,128)S(1)} %slice.12), channel_id=1, source_target_pairs={{0,3},{1,2},{2,1},{3,0},{4,7},{5,6},{6,5},{7,4},{8,11},{9,10},{10,... | collective-permute-start | bytes 24584 | tf_op jit(solution)/shard_map/ppermute | solution.py:775
  78.0 12.3 %collective-permute-start.7 = (f32[32,768]{1,0:T(8,128)S(1)}, f32[32,768]{1,0:T(8,128)S(1)}, u32[]{:S(2)}, u32[]{:S(2)}) collective-permute-start(f32[32,768]{1,0:T(8,128)S(1)} %get-tuple-element.59), channel_id=1, source_target_pairs={{0,4},{8,12},{16,20},{24,28},{4,0},{12,8},{20,16},{28,24},{1,5},{9... | collective-permute-start | bytes 294920 | tf_op jit(solution)/shard_map/ppermute | solution.py:769
  79.1 11.2 %collective-permute-start.8 = (f32[32,768]{1,0:T(8,128)S(1)}, f32[32,768]{1,0:T(8,128)S(1)}, u32[]{:S(2)}, u32[]{:S(2)}) collective-permute-start(f32[32,768]{1,0:T(8,128)S(1)} %get-tuple-element.60), channel_id=1, source_target_pairs={{4,8},{12,16},{20,24},{8,4},{16,12},{24,20},{5,9},{13,17},{21,25},... | collective-permute-start | bytes 294920 | tf_op jit(solution)/shard_map/ppermute | solution.py:769
  81.0 16.3 %collective-permute-start.14 = (f32[256,512]{1,0:T(8,128)S(1)}, f32[256,512]{1,0:T(8,128)S(1)}, u32[]{:S(2)}, u32[]{:S(2)}) collective-permute-start(f32[256,512]{1,0:T(8,128)S(1)} %get-tuple-element.67), channel_id=1, source_target_pairs={{0,2},{3,1},{4,6},{7,5},{8,10},{11,9},{12,14},{15,13},{16,18},{19,... | collective-permute-start | bytes 1572872 | tf_op jit(solution)/shard_map/ppermute | solution.py:816
  86.0 22.7 %collective-permute-start.15 = (f32[256,512]{1,0:T(8,128)S(1)}, f32[256,512]{1,0:T(8,128)S(1)}, u32[]{:S(2)}, u32[]{:S(2)}) collective-permute-start(f32[256,512]{1,0:T(8,128)S(1)} %get-tuple-element.68), channel_id=1, source_target_pairs={{0,3},{3,0},{4,7},{7,4},{8,11},{11,8},{12,15},{15,12},{16,19},{19,... | collective-permute-start | bytes 1572872 | tf_op jit(solution)/shard_map/ppermute | solution.py:816
  111.9 3.3 %collective-permute-start.16 = (f32[64,640]{1,0:T(8,128)S(1)}, f32[64,640]{1,0:T(8,128)S(1)}, u32[]{:S(2)}, u32[]{:S(2)}) collective-permute-start(f32[64,640]{1,0:T(8,128)S(1)} %get-tuple-element.73.send_a), channel_id=1, source_target_pairs={{0,4},{8,12},{16,20},{24,28},{4,0},{12,8},{20,16},{28,24},{1,5},{9... | collective-permute-start | bytes 491528 | tf_op jit(solution)/shard_map/ppermute | solution.py:769
  113.2 6.6 %collective-permute-start.17 = (f32[64,640]{1,0:T(8,128)S(1)}, f32[64,640]{1,0:T(8,128)S(1)}, u32[]{:S(2)}, u32[]{:S(2)}) collective-permute-start(f32[64,640]{1,0:T(8,128)S(1)} %get-tuple-element.75.send_b), channel_id=1, source_target_pairs={{4,8},{12,16},{20,24},{8,4},{16,12},{24,20},{5,9},{13,17},{21,25},... | collective-permute-start | bytes 491528 | tf_op jit(solution)/shard_map/ppermute | solution.py:769
  120.5 5.7 %collective-permute-start.18 = (f32[192,128]{1,0:T(8,128)S(1)}, f32[192,128]{1,0:T(8,128)S(1)}, u32[]{:S(2)}, u32[]{:S(2)}) collective-permute-start(f32[192,128]{1,0:T(8,128)S(1)} %get-tuple-element.77), channel_id=1, source_target_pairs={{0,1},{2,3},{1,0},{3,2},{4,5},{6,7},{5,4},{7,6},{8,9},{10,11},{9,8... | collective-permute-start | bytes 294920 | tf_op jit(solution)/shard_map/ppermute | solution.py:769
  120.6 5.6 %collective-permute-start.19 = (f32[192,128]{1,0:T(8,128)S(1)}, f32[192,128]{1,0:T(8,128)S(1)}, u32[]{:S(2)}, u32[]{:S(2)}) collective-permute-start(f32[192,128]{1,0:T(8,128)S(1)} %get-tuple-element.78), channel_id=1, source_target_pairs={{1,2},{2,1},{5,6},{6,5},{9,10},{10,9},{13,14},{14,13},{17,18},{18,... | collective-permute-start | bytes 294920 | tf_op jit(solution)/shard_map/ppermute | solution.py:769
  136.1 5.7 %collective-permute-start.31 = (f32[32,640]{1,0:T(8,128)S(1)}, f32[32,640]{1,0:T(8,128)S(1)}, u32[]{:S(2)}, u32[]{:S(2)}) collective-permute-start(f32[32,640]{1,0:T(8,128)S(1)} %get-tuple-element.87.send_a), channel_id=1, source_target_pairs={{0,4},{8,12},{16,20},{24,28},{4,0},{12,8},{20,16},{28,24},{1,5},{9... | collective-permute-start | bytes 245768 | tf_op jit(solution)/shard_map/ppermute | solution.py:769
  136.3 5.7 %collective-permute-start.32 = (f32[32,640]{1,0:T(8,128)S(1)}, f32[32,640]{1,0:T(8,128)S(1)}, u32[]{:S(2)}, u32[]{:S(2)}) collective-permute-start(f32[32,640]{1,0:T(8,128)S(1)} %get-tuple-element.89.send_b), channel_id=1, source_target_pairs={{4,8},{12,16},{20,24},{8,4},{16,12},{24,20},{5,9},{13,17},{21,25},... | collective-permute-start | bytes 245768 | tf_op jit(solution)/shard_map/ppermute | solution.py:769
  138.2 8.2 %collective-permute-start.20 = (f32[4,8,128]{2,1,0:T(8,128)S(1)}, f32[4,8,128]{2,1,0:T(8,128)S(1)}, u32[]{:S(2)}, u32[]{:S(2)}) collective-permute-start(f32[4,8,128]{2,1,0:T(8,128)S(1)} %pad_maximum_fusion), channel_id=1, source_target_pairs={{0,1},{1,0},{2,3},{3,2},{4,5},{5,4},{6,7},{7,6},{8,9},{9,8},{10,11... | collective-permute-start | bytes 49160 | tf_op jit(solution)/shard_map/ppermute | solution.py:775
  142.7 29.8 %collective-permute-start.34 = (f32[144,512]{1,0:T(8,128)S(1)}, f32[144,512]{1,0:T(8,128)S(1)}, u32[]{:S(2)}, u32[]{:S(2)}) collective-permute-start(f32[144,512]{1,0:T(8,128)S(1)} %wrap.1.refs_0_), channel_id=1, source_target_pairs={{0,2},{1,3},{2,0},{3,1},{4,6},{5,7},{6,4},{7,5},{8,10},{9,11},{10,... | collective-permute-start | bytes 884744 | tf_op jit(solution)/shard_map/ppermute | solution.py:775
  146.4 19.6 %collective-permute-start.21 = (f32[4,8,128]{2,1,0:T(8,128)S(1)}, f32[4,8,128]{2,1,0:T(8,128)S(1)}, u32[]{:S(2)}, u32[]{:S(2)}) collective-permute-start(f32[4,8,128]{2,1,0:T(8,128)S(1)} %fusion), channel_id=1, source_target_pairs={{0,2},{1,3},{2,0},{3,1},{4,6},{5,7},{6,4},{7,5},{8,10},{9,11},{10,... | collective-permute-start | bytes 49160 | tf_op jit(solution)/shard_map/ppermute | solution.py:775
  146.5 30.8 %collective-permute-start.26 = (f32[128,512]{1,0:T(8,128)S(1)}, f32[128,512]{1,0:T(8,128)S(1)}, u32[]{:S(2)}, u32[]{:S(2)}) collective-permute-start(f32[128,512]{1,0:T(8,128)S(1)} %get-tuple-element.82.refs_0_), channel_id=1, source_target_pairs={{0,2},{1,3},{2,0},{3,1},{4,6},{5,7},{6,4},{7,5},{8,10},{9,11},{10,... | collective-permute-start | bytes 786440 | tf_op jit(solution)/shard_map/ppermute | solution.py:775
  149.4 32.1 %collective-permute-start.25 = (f32[128,512]{1,0:T(8,128)S(1)}, f32[128,512]{1,0:T(8,128)S(1)}, u32[]{:S(2)}, u32[]{:S(2)}) collective-permute-start(f32[128,512]{1,0:T(8,128)S(1)} %get-tuple-element.82.refs_0_), channel_id=1, source_target_pairs={{0,1},{1,0},{2,3},{3,2},{4,5},{5,4},{6,7},{7,6},{8,9},{9,8},{10,11... | collective-permute-start | bytes 786440 | tf_op jit(solution)/shard_map/ppermute | solution.py:775
  149.4 34.1 %collective-permute-start.29 = (f32[128,512]{1,0:T(8,128)S(1)}, f32[128,512]{1,0:T(8,128)S(1)}, u32[]{:S(2)}, u32[]{:S(2)}) collective-permute-start(f32[128,512]{1,0:T(8,128)S(1)} %get-tuple-element.83.refs_4_.before), channel_id=1, source_target_pairs={{0,2},{1,3},{2,0},{3,1},{4,6},{5,7},{6,4},{7,5},{8,10},{9,11},{10,... | collective-permute-start | bytes 786440 | tf_op jit(solution)/shard_map/ppermute | solution.py:775
  166.0 2.7 %collective-permute-start.22 = (f32[4,8,128]{2,1,0:T(8,128)S(1)}, f32[4,8,128]{2,1,0:T(8,128)S(1)}, u32[]{:S(2)}, u32[]{:S(2)}) collective-permute-start(f32[4,8,128]{2,1,0:T(8,128)S(1)} %fusion.1), channel_id=1, source_target_pairs={{0,4},{4,0},{8,12},{12,8},{16,20},{20,16},{24,28},{28,24},{1,5},{5... | collective-permute-start | bytes 49160 | tf_op jit(solution)/shard_map/ppermute | solution.py:775
  168.7 3.7 %collective-permute-start.23 = (f32[4,8,128]{2,1,0:T(8,128)S(1)}, f32[4,8,128]{2,1,0:T(8,128)S(1)}, u32[]{:S(2)}, u32[]{:S(2)}) collective-permute-start(f32[4,8,128]{2,1,0:T(8,128)S(1)} %add.26), channel_id=1, source_target_pairs={{0,8},{4,12},{8,0},{12,4},{16,24},{20,28},{24,16},{28,20},{1,9},{5... | collective-permute-start | bytes 49160 | tf_op jit(solution)/shard_map/ppermute | solution.py:775
  172.5 42.8 %collective-permute-start.33 = (f32[144,512]{1,0:T(8,128)S(1)}, f32[144,512]{1,0:T(8,128)S(1)}, u32[]{:S(2)}, u32[]{:S(2)}) collective-permute-start(f32[144,512]{1,0:T(8,128)S(1)} %wrap.1.refs_0_), channel_id=1, source_target_pairs={{0,1},{1,0},{2,3},{3,2},{4,5},{5,4},{6,7},{7,6},{8,9},{9,8},{10,11... | collective-permute-start | bytes 884744 | tf_op jit(solution)/shard_map/ppermute | solution.py:775
  172.5 42.8 %collective-permute-start.35 = (f32[144,512]{1,0:T(8,128)S(1)}, f32[144,512]{1,0:T(8,128)S(1)}, u32[]{:S(2)}, u32[]{:S(2)}) collective-permute-start(f32[144,512]{1,0:T(8,128)S(1)} %collective-permute-done.34.refs_2_), channel_id=1, source_target_pairs={{0,1},{1,0},{2,3},{3,2},{4,5},{5,4},{6,7},{7,6},{8,9},{9,8},{10,11... | collective-permute-start | bytes 884744 | tf_op jit(solution)/shard_map/ppermute | solution.py:775
  177.3 5.9 %collective-permute-start.24 = (f32[4,8,128]{2,1,0:T(8,128)S(1)}, f32[4,8,128]{2,1,0:T(8,128)S(1)}, u32[]{:S(2)}, u32[]{:S(2)}) collective-permute-start(f32[4,8,128]{2,1,0:T(8,128)S(1)} %add.27), channel_id=1, source_target_pairs={{0,16},{4,20},{8,24},{12,28},{16,0},{20,4},{24,8},{28,12},{1,17},{... | collective-permute-start | bytes 49160 | tf_op jit(solution)/shard_map/ppermute | solution.py:775
  181.5 20.6 %collective-permute-start.27 = (f32[128,512]{1,0:T(8,128)S(1)}, f32[128,512]{1,0:T(8,128)S(1)}, u32[]{:S(2)}, u32[]{:S(2)}) collective-permute-start(f32[128,512]{1,0:T(8,128)S(1)} %collective-permute-done.26.refs_2_), channel_id=1, source_target_pairs={{0,1},{1,0},{2,3},{3,2},{4,5},{5,4},{6,7},{7,6},{8,9},{9,8},{10,11... | collective-permute-start | bytes 786440 | tf_op jit(solution)/shard_map/ppermute | solution.py:775
  183.2 24.5 %collective-permute-start.28 = (f32[128,512]{1,0:T(8,128)S(1)}, f32[128,512]{1,0:T(8,128)S(1)}, u32[]{:S(2)}, u32[]{:S(2)}) collective-permute-start(f32[128,512]{1,0:T(8,128)S(1)} %get-tuple-element.83.refs_4_.before), channel_id=1, source_target_pairs={{0,1},{1,0},{2,3},{3,2},{4,5},{5,4},{6,7},{7,6},{8,9},{9,8},{10,11... | collective-permute-start | bytes 786440 | tf_op jit(solution)/shard_map/ppermute | solution.py:775
  183.5 29.7 %collective-permute-start.30 = (f32[128,512]{1,0:T(8,128)S(1)}, f32[128,512]{1,0:T(8,128)S(1)}, u32[]{:S(2)}, u32[]{:S(2)}) collective-permute-start(f32[128,512]{1,0:T(8,128)S(1)} %collective-permute-done.29.refs_6_), channel_id=1, source_target_pairs={{0,1},{1,0},{2,3},{3,2},{4,5},{5,4},{6,7},{7,6},{8,9},{9,8},{10,11... | collective-permute-start | bytes 786440 | tf_op jit(solution)/shard_map/ppermute | solution.py:775
